TPU v7x, 128 devices: a whole 4x4x4 slice. The times are simulated.
128 devices in a mesh: ctx: 32 (over y, z, x_lo), head: 4 (over x_hi, core).
Axes of the slice: x: 4 (x_hi: 2, x_lo: 2; x = x_hi * 2 + x_lo), y: 4, z: 4, core: 2. Of those that a mesh axis runs over, the one named last changes fastest.
Arguments:
- hidden: bfloat16 [8192, 2560], P('ctx'), may hold values from -6 to 6
- norm_gain: float32 [2560], replicated, may hold values from 0.1 to 1.9
- x_weight: bfloat16 [2560, 5120], P(None, 'head'), may hold values from -0.125 to 0.125
- z_weight: bfloat16 [2560, 5120], P(None, 'head'), may hold values from -0.125 to 0.125
- bc_weight: bfloat16 [2560, 256], replicated, may hold values from -0.125 to 0.125
- dt_weight: bfloat16 [2560, 80], P(None, 'head'), may hold values from -0.125 to 0.125
- x_kernel: float32 [4, 5120], P(None, 'head'), may hold values from -3 to 3
- bc_kernel: float32 [4, 256], replicated, may hold values from -3 to 3
- dt_bias: float32 [80], P('head'), may hold values from -1 to 1
- log_rate: float32 [80], P('head'), may hold values from -13 to -3
- out_gain: float32 [5120], P('head'), may hold values from 0.1 to 1.9
- out_weight: bfloat16 [5120, 2560], P('head'), may hold values from -0.078125 to 0.078125
Outputs:
- layer_out: bfloat16 [8192, 2560], P('ctx', 'head')
All inputs are finite; a program needn't handle non-finite values.
Results may differ from a plain program's by a relative error of at most 0.014.
Values may be sent and summed in bfloat16 or wider, within the bound.
No kernel may reach another device: no remote copies, remote signals or barrier semaphores. Data moves between devices by JAX's collectives and lax.ppermute only.
A program may use at most 128 MiB of HBM per device.

v0:
```python
import jax
import jax.numpy as jnp
from jax import lax
from jax.sharding import PartitionSpec as P

HEAD_DIM = 64
STATE = 128


epsilon = 1e-05
highest = lax.Precision.HIGHEST


def from_behind(value, axis, steps):
    count = lax.axis_size(axis)
    first, last = (max(0, -steps), min(count, count - steps))
    return lax.ppermute(value, axis, [(source, source + steps) for source in range(first, last)])


def prefix(value, axis, join, neutral, backward):
    count = lax.axis_size(axis)
    place = lax.axis_index(axis)
    ahead = count - 1 - place if backward else place
    gathered = jax.tree.map(
        lambda a, kind: lax.all_gather(a.astype(kind), axis), value, (jnp.bfloat16, jnp.bfloat16)
    )
    state = jax.tree.map(lambda a, e: jnp.zeros_like(a) + jnp.asarray(e, a.dtype), value, neutral)

    def one(lap, state):
        source = count - 1 - lap if backward else lap
        return join(
            state,
            jax.tree.map(
                lambda a, own: lax.dynamic_index_in_dim(a, source, 0, False).astype(own.dtype),
                gathered,
                value,
            ),
        )

    return lax.fori_loop(0, ahead, one, state)


def rms_scale(values, scaling):
    mean_sq = jnp.mean(values * values, axis=-1, keepdims=True)
    return values * lax.rsqrt(mean_sq + epsilon) * scaling


def rim_prior(rim_rows):
    return from_behind(rim_rows, "ctx", 1)


def rim_next(rim_rows):
    return from_behind(rim_rows, "ctx", -1)


def link_states(earlier, later_part):
    return (earlier[0] * later_part[0], later_part[0][..., None, None] * earlier[1] + later_part[1])


def carry_prior(decays, states):
    identity = (jnp.ones_like(decays), jnp.zeros_like(states))
    return prefix((decays, states), "ctx", link_states, identity, False)[1]


def carry_next(decays, states):
    identity = (jnp.ones_like(decays), jnp.zeros_like(states))
    return prefix((decays, states), "ctx", link_states, identity, True)[1]


def conv_silu(extended, kernel, row_count):
    running = jnp.zeros(extended.shape[:1] + (row_count,) + extended.shape[2:], jnp.float32)
    for offset in range(kernel.shape[0]):
        running = running + kernel[offset] * extended[:, offset : offset + row_count].astype(
            jnp.float32
        )
    return jax.nn.silu(running).astype(jnp.bfloat16)


def mixer(stacked, params, fetch_rim, fetch_carry):
    (
        norm_gain,
        x_weight,
        z_weight,
        bc_weight,
        dt_weight,
        x_kernel,
        bc_kernel,
        dt_bias,
        log_rate,
        out_gain,
    ) = params
    count_dirs, row_count, model_width = stacked.shape
    normed = rms_scale(stacked.astype(jnp.float32), norm_gain).astype(jnp.bfloat16)
    normed = normed.reshape(count_dirs * row_count, model_width)
    x_in = jnp.dot(normed, x_weight, preferred_element_type=jnp.float32).astype(jnp.bfloat16)
    z_in = jnp.dot(normed, z_weight, preferred_element_type=jnp.float32).astype(jnp.bfloat16)
    bc_in = jnp.dot(normed, bc_weight, preferred_element_type=jnp.float32).astype(jnp.bfloat16)
    dt_raw = jnp.dot(normed, dt_weight, preferred_element_type=jnp.float32).reshape(
        count_dirs, row_count, -1
    )
    inner_width = x_in.shape[1]
    joined = jnp.concatenate([x_in, bc_in], axis=1).reshape(count_dirs, row_count, -1)
    tap_count = x_kernel.shape[0]
    rim_rows = fetch_rim(joined[:, row_count - tap_count + 1 :])
    extended = jnp.concatenate([rim_rows, joined], axis=1)
    kernel = jnp.concatenate([x_kernel, bc_kernel], axis=1)
    conv_out = conv_silu(extended, kernel, row_count)
    x_conv = conv_out[..., :inner_width]
    b_mat = conv_out[..., inner_width : inner_width + STATE]
    c_mat = conv_out[..., inner_width + STATE :]
    head_count = inner_width // HEAD_DIM
    step_size = jax.nn.softplus(dt_raw + dt_bias)
    log_decay = -step_size * jnp.exp(log_rate)
    cumulative = jnp.cumsum(log_decay, axis=1)
    cumul_heads = jnp.swapaxes(cumulative, 1, 2)
    step_heads = jnp.swapaxes(step_size, 1, 2)
    gram_rows = jnp.einsum("btn,bsn->bts", c_mat, b_mat, preferred_element_type=jnp.float32)
    causal = jnp.arange(row_count)[:, None] >= jnp.arange(row_count)[None, :]
    segment = cumul_heads[:, :, :, None] - cumul_heads[:, :, None, :]
    weights = (
        jnp.exp(jnp.where(causal, segment, -jnp.inf))
        * gram_rows[:, None]
        * step_heads[:, :, None, :]
    )
    x_float = x_conv.astype(jnp.float32).reshape(count_dirs, row_count, head_count, HEAD_DIM)
    b_float = b_mat.astype(jnp.float32)
    c_float = c_mat.astype(jnp.float32)
    within = jnp.einsum("bhts,bshp->bthp", weights, x_float, precision=highest)
    final_log = cumul_heads[:, :, -1]
    weight_end = jnp.exp(final_log[:, :, None] - cumul_heads) * step_heads
    local_state = jnp.einsum("bhs,bshp,bsn->bhpn", weight_end, x_float, b_float, precision=highest)
    carried = fetch_carry(jnp.exp(final_log), local_state)
    from_carry = (
        jnp.einsum("btn,bhpn->bthp", c_float, carried, precision=highest)
        * jnp.exp(cumulative)[..., None]
    )
    y_full = within + from_carry
    gating = jax.nn.silu(z_in.astype(jnp.float32)).reshape(
        count_dirs, row_count, head_count, HEAD_DIM
    )
    gated_out = rms_scale(y_full * gating, out_gain.reshape(head_count, HEAD_DIM))
    return gated_out.astype(jnp.bfloat16).reshape(count_dirs, row_count, inner_width)


def per_device(
    hidden,
    norm_gain,
    x_weight,
    z_weight,
    bc_weight,
    dt_weight,
    x_kernel,
    bc_kernel,
    dt_bias,
    log_rate,
    out_gain,
    out_weight,
):
    params = (
        norm_gain,
        x_weight,
        z_weight,
        bc_weight,
        dt_weight,
        x_kernel,
        bc_kernel,
        dt_bias,
        log_rate,
        out_gain,
    )
    forward_out = mixer(hidden[None], params, rim_prior, carry_prior)[0]
    backward_out = mixer(hidden[::-1, ::-1][None], params, rim_next, carry_next)[0][::-1]
    row_count = forward_out.shape[0]
    projected = jnp.dot(
        jnp.concatenate([forward_out, backward_out], axis=0),
        out_weight,
        preferred_element_type=jnp.float32,
    )
    partial_sum = projected[:row_count] + projected[row_count:, ::-1]
    summed = lax.psum_scatter(
        partial_sum.astype(jnp.bfloat16), "head", scatter_dimension=1, tiled=True
    ).astype(jnp.float32)
    first_col = lax.axis_index("head") * summed.shape[1]
    residual = lax.dynamic_slice_in_dim(hidden, first_col, summed.shape[1], 1).astype(jnp.float32)
    return (residual + summed).astype(jnp.bfloat16)


def solution(mesh):
    return jax.shard_map(
        per_device,
        mesh=mesh,
        in_specs=(
            P("ctx", None),
            P(),
            P(None, "head"),
            P(None, "head"),
            P(),
            P(None, "head"),
            P(None, "head"),
            P(),
            P("head"),
            P("head"),
            P("head"),
            P("head", None),
        ),
        out_specs=P("ctx", "head"),
        check_vma=False,
    )
```

profile of v0, /device:TPU:1, one launch (start us, length us, event | category | flops | bytes accessed | tf_op | source)
XLA Modules:
  0.0 679.0 jit_solution(8506788863843893133)
XLA Ops:
  6.5 17.4 %rev.9 = bf16[256,2560]{1,0:T(8,128)(2,1)S(1)} reverse(bf16[256,2560]{1,0:T(8,128)(2,1)} %param.16), dimensions={0,1} | reverse | bytes 2621440 | tf_op jit(solution)/shard_map/rev | solution.py:172
  24.4 5.4 convolution_convert_fusion.1
  36.8 4.7 collective-permute-start
  48.2 6.4 multiply_convert_fusion.1
  56.7 2.2 copy.95
  58.9 2.6 fusion.66
  69.8 2.3 copy.78
  72.0 2.6 fusion.63
  78.8 74.0 %all-gather.2 = bf16[32,20,1]{1,2,0:T(2,128)(2,1)S(1)} all-gather(bf16[1,20,1]{1,2,0:T(2,128)(2,1)} %get-tuple-element.206), channel_id=4, replica_groups=mesh['ctx'=32,'head'=4] {'ctx'}, dimensions={0}, use_global_device_ids=true | all-gather | bytes 1320 | tf_op jit(solution)/shard_map/all_gather | solution.py:25
  158.2 6.0 divide_multiply_fusion
  164.2 2.9 copy.110
  167.0 67.1 %all-gather = bf16[32,20,1]{1,2,0:T(2,128)(2,1)S(1)} all-gather(bf16[1,20,1]{1,2,0:T(2,128)(2,1)S(1)} %copy-done.34), channel_id=2, replica_groups=mesh['ctx'=32,'head'=4] {'ctx'}, dimensions={0}, use_global_device_ids=true | all-gather | bytes 1320 | tf_op jit(solution)/shard_map/all_gather | solution.py:25
  235.9 4.9 divide_multiply_fusion.1
  244.3 57.2 %all-gather.9.cloned.1.call-done = bf16[640,64,128]{2,1,0:T(8,128)(2,1)} async-done(((bf16[20,64,128]{2,1,0:T(8,128)(2,1)}), bf16[640,64,128]{2,1,0:T(8,128)(2,1)}) %all-gather.9.cloned.1.call-update) | async-done | bytes 10485776 | tf_op jit(solution)/shard_map/all_gather | solution.py:25
  301.6 56.5 %while.27 = (s32[]{:T(128)}, f32[1,20,64,128]{3,2,1,0:T(8,128)S(1)}, s32[]{:T(128)}, bf16[32,1,20]{2,1,0:T(2,128)(2,1)}, bf16[32,1,20,64,128]{4,3,2,1,0:T(8,128)...) while((s32[]{:T(128)}, f32[1,20,64,128]{3,2,1,0:T(8,128)S(1)}, s32[]{:T(128)}, ...), condition=%wide.region_10.11_spmd, body=%wide.region_9.10_spmd.sunk | while | flops 491546 | bytes 1638747 | solution.py:40
  358.1 175.8 %all-gather.7.cloned.1.call-done = bf16[640,64,128]{2,1,0:T(8,128)(2,1)} async-done(((bf16[20,64,128]{2,1,0:T(8,128)(2,1)}), bf16[640,64,128]{2,1,0:T(8,128)(2,1)}) %all-gather.7.cloned.1.call-update) | async-done | bytes 10485776 | tf_op jit(solution)/shard_map/all_gather | solution.py:25
  537.2 4.0 multiply_reduce_fusion
  541.2 4.0 multiply_reduce_fusion.1
  547.7 8.2 %fusion.53 = f32[512,2560]{1,0:T(8,128)} fusion(bf16[1280,2560]{1,0:T(8,128)(2,1)} %param.27, bf16[256,1280]{0,1:T(8,128)(2,1)S(1)} %rev.10, bf16[256,1280]{0,1:T(8,128)(2,1)S(1)} %bitcast.193), kind=kOutput, calls=%fused_computation.58 | convolution fusion | flops 3358064640 | bytes 13107200 | tf_op jit(solution)/shard_map/dot_general | solution.py:174
  555.9 3.4 slice.133
  559.3 18.6 %rev.11 = f32[256,2560]{1,0:T(8,128)S(1)} reverse(f32[256,2560]{1,0:T(8,128)} %slice.133), dimensions={1} | reverse | bytes 5242880 | tf_op jit(solution)/shard_map/rev | solution.py:179
  577.9 3.1 fusion.18
  581.1 2.5 copy.121
  583.6 85.8 %reduce-scatter.4.cloned.1.call-done = bf16[640,256]{1,0:T(8,128)(2,1)} async-done(((bf16[2560,256]{1,0:T(8,128)(2,1)}), bf16[640,256]{1,0:T(8,128)(2,1)}) %reduce-scatter.4.cloned.1.call-update) | async-done | bytes 327696
  (234 shorter events, 102.7 us)
Async XLA Ops:
  6.5 23.3 %copy-start = (bf16[2560,256]{1,0:T(8,128)(2,1)S(1)}, bf16[2560,256]{1,0:T(8,128)(2,1)}, u32[]{:S(2)}) copy-start(bf16[2560,256]{1,0:T(8,128)(2,1)} %param.20) | copy-start | bytes 3932164
  6.5 17.8 %copy-start.36 = (f32[2560]{0:T(1024)S(1)}, f32[2560]{0:T(1024)}, u32[]{:S(2)}) copy-start(f32[2560]{0:T(1024)} %param.17) | copy-start | bytes 30724
  6.5 295.0 %all-gather.9.cloned.1.call-start = ((), (), s32[]{:S(2)}) async-start(), calls=%async_computation.2 | async-start | bytes 10813440 | tf_op jit(solution)/shard_map/all_gather | solution.py:25
  24.0 5.8 copy-start.3
  24.0 9.9 %slice-start = ((s8[6553600]{0:T(1024)(128)(4,1)}), s8[4194304]{0:T(1024)(128)(4,1)S(1)}, s32[]{:S(2)}) async-start(s8[6553600]{0:T(1024)(128)(4,1)} %bitcast.219), calls=%async_computation.4 | async-start | bytes 8388608
  24.3 17.2 %copy-start.33 = (f32[256]{0:T(256)}, f32[256]{0:T(256)S(1)}, u32[]{:S(2)}) copy-start(f32[256]{0:T(256)S(1)} %add_rsqrt_fusion.2) | copy-start | bytes 3076
  24.4 9.5 %slice-start.1 = ((s8[6553600]{0:T(1024)(128)(4,1)}), s8[2359296]{0:T(1024)(128)(4,1)S(1)}, s32[]{:S(2)}) async-start(s8[6553600]{0:T(1024)(128)(4,1)} %bitcast.219), calls=%async_computation.5 | async-start | bytes 4718592
  32.2 15.4 %collective-permute-start.1 = (bf16[1,3,1536]{2,1,0:T(4,128)(2,1)}, bf16[1,3,1536]{2,1,0:T(4,128)(2,1)}, u32[]{:S(2)}, u32[]{:S(2)}) collective-permute-start(bf16[1,3,1536]{2,1,0:T(4,128)(2,1)} %slice.122), channel_id=1, source_target_pairs={{4,0},{8,4},{12,8},{16,12},{20,16},{24,20},{28,24},{32,28},{36,32}... | collective-permute-start | bytes 27656 | tf_op jit(solution)/shard_map/ppermute | solution.py:17
  33.9 8.3 %copy-start.32 = (f32[256]{0:T(256)}, f32[256]{0:T(256)S(1)}, u32[]{:S(2)}) copy-start(f32[256]{0:T(256)S(1)} %add_rsqrt_fusion.3) | copy-start | bytes 3076
  36.7 5.5 copy-start.13
  36.7 4.8 copy-start.35
  36.7 4.9 copy-start.38
  36.8 5.4 copy-start.6
  36.8 10.8 %collective-permute-start = (bf16[1,3,1536]{2,1,0:T(4,128)(2,1)S(1)}, bf16[1,3,1536]{2,1,0:T(4,128)(2,1)S(1)}, u32[]{:S(2)}, u32[]{:S(2)}) collective-permute-start(bf16[1,3,1536]{2,1,0:T(4,128)(2,1)S(1)} %slice.109), channel_id=1, source_target_pairs={{0,4},{4,8},{8,12},{12,16},{16,20},{20,24},{24,28},{28,32},{32,36}... | collective-permute-start | bytes 27656 | tf_op jit(solution)/shard_map/ppermute | solution.py:17
  56.7 4.9 copy-start.20
  61.6 472.4 %all-gather.7.cloned.1.call-start = ((), (), s32[]{:S(2)}) async-start(), calls=%async_computation.1 | async-start | bytes 10813440 | tf_op jit(solution)/shard_map/all_gather | solution.py:25
  69.8 4.9 copy-start.29
  69.8 85.1 %copy-start.14 = (f32[256,20]{1,0:T(8,128)S(1)}, f32[256,20]{1,0:T(8,128)}, u32[]{:S(2)}) copy-start(f32[256,20]{1,0:T(8,128)} %get-tuple-element.201) | copy-start | bytes 61444
  74.7 594.8 %reduce-scatter.4.cloned.1.call-start = ((), (), s32[]{:S(2)}) async-start(), calls=%async_computation.3 | async-start | bytes 1638400
  164.2 70.8 %copy-start.15 = (f32[256,20]{1,0:T(8,128)S(1)}, f32[256,20]{1,0:T(8,128)}, u32[]{:S(2)}) copy-start(f32[256,20]{1,0:T(8,128)} %get-tuple-element.199) | copy-start | bytes 61444
  164.2 70.9 %copy-start.23 = (f32[20,2]{1,0:T(8,128)S(1)}, f32[20,2]{1,0:T(8,128)}, u32[]{:S(2)}) copy-start(f32[20,2]{1,0:T(8,128)} %copy.83) | copy-start | bytes 484
  164.2 71.0 %copy-start.22 = (f32[1,20,2,128]{3,2,1,0:T(2,128)S(1)}, f32[1,20,2,128]{3,2,1,0:T(2,128)}, u32[]{:S(2)}) copy-start(f32[1,20,2,128]{3,2,1,0:T(2,128)} %copy.132) | copy-start | bytes 61444
  164.2 71.1 %copy-start.16 = (f32[256,20]{1,0:T(8,128)S(1)}, f32[256,20]{1,0:T(8,128)}, u32[]{:S(2)}) copy-start(f32[256,20]{1,0:T(8,128)} %get-tuple-element.213) | copy-start | bytes 61444
  581.1 91.4 %copy-start.1 = (bf16[2560,256]{1,0:T(8,128)(2,1)S(1)}, bf16[2560,256]{1,0:T(8,128)(2,1)}, u32[]{:S(2)}) copy-start(bf16[2560,256]{1,0:T(8,128)(2,1)} %param.20) | copy-start | bytes 3932164
  (22 other events, 54.6 us)
Sparse Core Ops, SparseCore 0:
  61.7 239.8 all-gather.8
  303.2 230.6 all-gather.6
  583.7 85.6 reduce-scatter.3
where the time goes:
time: 684 us; the launch traced here: 679 us
  waiting for transfers between devices  319 us (47%)
  blocking collectives  141 us (21%)
  local copies, waits for them, and re-layouts  77.5 us (11%)
  other arithmetic  74.1 us (11%)
  matrix products  46.3 us (7%)
  between operations  13.8 us (2%)
    all_gather x2, waiting for transfers between devices, prefix(): lax.all_gather(a.astype(kind), axis)  233 us
    all_gather x2, blocking collectives, prefix(): lax.all_gather(a.astype(kind), axis)  141 us
    unnamed x4, waiting for transfers between devices  85.9 us
    add x31, other arithmetic, link_states(): later_part[0][..., None, None] * earlier[1] + later_part[1]  35.6 us
    convert_element_type x31, other arithmetic, one(): lax.dynamic_index_in_dim(a, source, 0, False).astype(own.dtype)  19.9 us
    rev x1, local copies, waits for them, and re-layouts, per_device(): partial_sum = projected[:row_count] + projected[row_count:, ::-1]  18.6 us
    rev x1, local copies, waits for them, and re-layouts, per_device(): hidden[::-1, ::-1][None]  17.4 us
  transfers between devices with their start and end apart: 5, of which 3 were waited for; matrix products, arithmetic and copies ran while one was open for 16% of the time, Pallas kernels for 0%

commit v1 on v0

v1 whole, which is shorter than its diff:
```python
import functools

import jax
import jax.numpy as jnp
from jax import lax
from jax.experimental import pallas as pl
from jax.experimental.pallas import tpu as pltpu
from jax.sharding import PartitionSpec as P

HEAD_DIM = 64
STATE = 128
HALO = 16
TILE = 256
LANES = 128
epsilon = 1e-05
highest = lax.Precision.HIGHEST
f32 = jnp.float32
bf16 = jnp.bfloat16


def mm(a, b, precision=None):
    return jnp.dot(a, b, preferred_element_type=f32, precision=precision)


def iota(shape, dim):
    return lax.broadcasted_iota(jnp.int32, shape, dim)


def silu(v):
    return v * jax.nn.sigmoid(v)


def flip_matrix(n):
    return (iota((n, n), 0) + iota((n, n), 1) == n - 1).astype(bf16)


def hi_lo(v):
    hi = v.astype(bf16)
    return jnp.concatenate([hi, (v - hi.astype(f32)).astype(bf16)], axis=1)


def spread(first, width):
    rows = iota((2 * LANES, width), 0) % LANES
    return (rows == first + iota((2 * LANES, width), 1) // HEAD_DIM).astype(bf16)


def conv_pair(ext, taps, rows):
    half = rows + HALO
    ahead, behind = ext[:half], ext[half:]
    fwd = jnp.zeros((rows, ext.shape[1]), f32)
    bwd = jnp.zeros((rows, ext.shape[1]), f32)
    for k in range(4):
        fwd = fwd + taps[k : k + 1] * ahead[HALO - 3 + k : HALO - 3 + k + rows]
        bwd = bwd + taps[k : k + 1] * behind[3 - k : 3 - k + rows]
    return silu(fwd).astype(bf16), silu(bwd).astype(bf16)


def entry_kernel(
    h_ref, prev_ref, next_ref, gain_ref, xw_ref, bcw_ref, dtw_ref, xk_ref, bck_ref, dtb_ref, lr_ref,
    x_ref, xconv_ref, bc_ref, delta_ref, cum_ref, cumt_ref, pay_ref,
    ext_ref, st_ref, bt_ref, wend_ref, dec_ref,
):
    rows, width = h_ref.shape
    n = pl.program_id(0)
    steps = pl.num_programs(0)

    @pl.when(n == 0)
    def _():
        ext_ref[0:HALO] = prev_ref[...]
        ext_ref[HALO : HALO + rows] = h_ref[...]
        flip = flip_matrix(TILE)
        blocks = width // TILE
        for b in range(blocks):
            source = slice((blocks - 1 - b) * TILE, (blocks - b) * TILE)
            cols = slice(b * TILE, (b + 1) * TILE)
            ext_ref[HALO + rows : HALO + 2 * rows, cols] = mm(h_ref[:, source], flip).astype(bf16)
            ext_ref[HALO + 2 * rows :, cols] = mm(next_ref[:, source], flip).astype(bf16)

        def normalise(i, _):
            at = pl.ds(pl.multiple_of(i * 32, 32), 32)
            v = ext_ref[at].astype(f32)
            mean_sq = jnp.mean(v * v, axis=-1, keepdims=True)
            ext_ref[at] = (v * lax.rsqrt(mean_sq + epsilon) * gain_ref[...]).astype(bf16)
            return 0

        lax.fori_loop(0, (2 * rows + 2 * HALO) // 32, normalise, 0)
        main = ext_ref[HALO : HALO + 2 * rows]
        x_ref[...] = main
        bc_in = mm(ext_ref[...], bcw_ref[...]).astype(bf16).astype(f32)
        bc_pair = conv_pair(bc_in, bck_ref[...], rows)
        dt = mm(main, dtw_ref[...]) + dtb_ref[...]
        delta = jnp.maximum(dt, 0.0) + jnp.log1p(jnp.exp(-jnp.abs(dt)))
        delta_ref[...] = delta
        log_decay = -delta * jnp.exp(lr_ref[...])
        lower = (iota((rows, rows), 0) >= iota((rows, rows), 1)).astype(f32)
        upper = (iota((rows, rows), 0) <= iota((rows, rows), 1)).astype(f32)
        for d in range(2):
            at = slice(d * rows, (d + 1) * rows)
            bc_ref[at] = bc_pair[d]
            bt_ref[d] = jnp.transpose(bc_pair[d][:, :STATE].astype(f32)).astype(bf16)
            cum = mm(upper if d else lower, log_decay[at], highest)
            cum_ref[at] = cum
            cumt_ref[d] = jnp.transpose(cum)[: cumt_ref.shape[1]]
            last = cum[0:1] if d else cum[rows - 1 : rows]
            wend_ref[at] = hi_lo(jnp.exp(last - cum) * delta[at])
            dec_ref[d : d + 1] = jnp.exp(last)

    x_in = mm(ext_ref[...], xw_ref[...]).astype(bf16).astype(f32)
    pair = conv_pair(x_in, xk_ref[...], rows)
    spread_n = spread(n * (TILE // HEAD_DIM), TILE)
    for d in range(2):
        at = slice(d * rows, (d + 1) * rows)
        xconv_ref[at] = pair[d]
        weighted = (pair[d].astype(f32) * mm(wend_ref[at], spread_n)).astype(bf16)
        column = pl.multiple_of(d * steps * TILE + n * TILE, TILE)
        st_ref[:, pl.ds(column, TILE)] = mm(bt_ref[d], weighted).astype(bf16)

    @pl.when(n == steps - 1)
    def _():
        slots, lanes = pay_ref.shape[0], pay_ref.shape[2] - LANES
        for slot in range(slots):
            i, q = slot // 4, slot % 4
            pay_ref[slot, :, :lanes] = st_ref[16 * i : 16 * i + 16, q * lanes : (q + 1) * lanes]
            dec = jnp.broadcast_to(dec_ref[q // 2 : q // 2 + 1], (16, LANES))
            hi = dec.astype(bf16)
            lo = (dec - hi.astype(f32)).astype(bf16)
            row = iota((16, LANES), 0)
            both = jnp.where(row == 0, hi.astype(f32), jnp.where(row == 1, lo.astype(f32), 0.0))
            pay_ref[slot, :, lanes:] = both.astype(bf16)


def entry(hidden, prev_rows, next_rows, gain, xw, bcw, dtw, xk, bck, dtb, lr, slots):
    rows, width = hidden.shape
    inner = xw.shape[1]
    steps = inner // TILE
    lanes = 2 * inner // 4
    whole = lambda *shape: pl.BlockSpec(shape, lambda n: (0,) * len(shape))
    return pl.pallas_call(
        entry_kernel,
        grid=(steps,),
        in_specs=[
            whole(rows, width), whole(HALO, width), whole(HALO, width), whole(1, width),
            pl.BlockSpec((width, TILE), lambda n: (0, n)),
            whole(width, 2 * STATE), whole(width, LANES),
            pl.BlockSpec((4, TILE), lambda n: (0, n)),
            whole(4, 2 * STATE), whole(1, LANES), whole(1, LANES),
        ],
        out_specs=[
            whole(2 * rows, width),
            pl.BlockSpec((2 * rows, TILE), lambda n: (0, n)),
            whole(2 * rows, 2 * STATE), whole(2 * rows, LANES), whole(2 * rows, LANES),
            whole(2, 24, rows), whole(slots, 16, lanes + LANES),
        ],
        out_shape=[
            jax.ShapeDtypeStruct((2 * rows, width), bf16),
            jax.ShapeDtypeStruct((2 * rows, inner), bf16),
            jax.ShapeDtypeStruct((2 * rows, 2 * STATE), bf16),
            jax.ShapeDtypeStruct((2 * rows, LANES), f32),
            jax.ShapeDtypeStruct((2 * rows, LANES), f32),
            jax.ShapeDtypeStruct((2, 24, rows), f32),
            jax.ShapeDtypeStruct((slots, 16, lanes + LANES), bf16),
        ],
        scratch_shapes=[
            pltpu.VMEM((2 * rows + 2 * HALO, width), bf16),
            pltpu.VMEM((STATE, 2 * inner), bf16),
            pltpu.VMEM((2, STATE, rows), bf16),
            pltpu.VMEM((2 * rows, 2 * LANES), bf16),
            pltpu.VMEM((8, LANES), f32),
        ],
        compiler_params=pltpu.CompilerParams(
            dimension_semantics=("arbitrary",), vmem_limit_bytes=48 << 20
        ),
        cost_estimate=pl.CostEstimate(
            flops=2 * 544 * width * (inner + 384), bytes_accessed=16 << 20, transcendentals=0
        ),
        name="entry",
    )(hidden, prev_rows, next_rows, gain, xw, bcw, dtw, xk, bck, dtb, lr)


def within_kernel(x_ref, bc_ref, cum_ref, cumt_ref, delta_ref, y_ref, gram_ref):
    d, n = pl.program_id(0), pl.program_id(1)
    rows = x_ref.shape[0]
    heads = TILE // HEAD_DIM

    @pl.when(n == 0)
    def _():
        gram = lax.dot_general(
            bc_ref[:, STATE:], bc_ref[:, :STATE], (((1,), (1,)), ((), ())), preferred_element_type=f32
        )
        t, s = iota((rows, rows), 0), iota((rows, rows), 1)
        seen = jnp.where(d == 0, t - s, s - t) >= 0
        gram_ref[...] = jnp.where(seen, gram, 0.0)

    weighted = x_ref[...].astype(f32) * mm(hi_lo(delta_ref[...]), spread(n * heads, TILE))
    cum = pltpu.roll(cum_ref[...], (LANES - n * heads) % LANES, 1)
    owner = iota((rows, TILE), 1) // HEAD_DIM
    total = jnp.zeros((rows, TILE), f32)
    for k in range(heads):
        behind = cumt_ref[0, pl.ds(n * heads + k, 1), :]
        decay = jnp.exp(jnp.minimum(cum[:, k : k + 1] - behind, 0.0)) * gram_ref[...]
        total = total + mm(decay.astype(bf16), jnp.where(owner == k, weighted, 0.0).astype(bf16))
    y_ref[...] = total


def within(xconv, bc, cum, cumt, delta):
    rows = xconv.shape[0] // 2
    inner = xconv.shape[1]
    return pl.pallas_call(
        within_kernel,
        grid=(2, inner // TILE),
        in_specs=[
            pl.BlockSpec((rows, TILE), lambda d, n: (d, n)),
            pl.BlockSpec((rows, 2 * STATE), lambda d, n: (d, 0)),
            pl.BlockSpec((rows, LANES), lambda d, n: (d, 0)),
            pl.BlockSpec((1, 24, rows), lambda d, n: (d, 0, 0)),
            pl.BlockSpec((rows, LANES), lambda d, n: (d, 0)),
        ],
        out_specs=pl.BlockSpec((rows, TILE), lambda d, n: (d, n)),
        out_shape=jax.ShapeDtypeStruct((2 * rows, inner), f32),
        scratch_shapes=[pltpu.VMEM((rows, rows), f32)],
        compiler_params=pltpu.CompilerParams(dimension_semantics=("arbitrary", "arbitrary")),
        cost_estimate=pl.CostEstimate(flops=3 << 30, bytes_accessed=5 << 20, transcendentals=3 << 20),
        name="within",
    )(xconv, bc, cum, cumt, delta)


def scan_kernel(q_ref, pay_ref, out_ref, dec_ref):
    slots, _, lanes = out_ref.shape
    q = q_ref[0]
    half, turned = q % 2, q // 2
    tail = pay_ref[:, :, lanes:]
    place = (iota((LANES, lanes), 0) == half * (lanes // HEAD_DIM) + iota((LANES, lanes), 1) // HEAD_DIM)
    place = place.astype(bf16)
    dec_ref[...] = mm(tail[:, 0, :], place) + mm(tail[:, 1, :], place)

    def one(i, carry):
        at = jnp.where(turned == 1, slots - 1 - i, i)
        out_ref[at] = carry.astype(bf16)
        return carry * dec_ref[pl.ds(at, 1), :] + pay_ref[at, :, :lanes].astype(f32)

    lax.fori_loop(0, slots, one, jnp.zeros((16, lanes), f32))


def scan(q, pay):
    slots, _, lanes = pay.shape
    lanes -= LANES
    return pl.pallas_call(
        scan_kernel,
        in_specs=[pl.BlockSpec(memory_space=pltpu.SMEM), pl.BlockSpec(memory_space=pltpu.VMEM)],
        out_specs=pl.BlockSpec(memory_space=pltpu.VMEM),
        out_shape=jax.ShapeDtypeStruct((slots, 16, lanes), bf16),
        scratch_shapes=[pltpu.VMEM((slots, lanes), f32)],
        name="scan",
    )(q, pay)


def gate_kernel(y_ref, z_ref, bc_ref, cum_ref, st_ref, gain_ref, out_ref):
    q = pl.program_id(0)
    rows, lanes = y_ref.shape
    state = st_ref[...].reshape(STATE, lanes)
    carried = mm(bc_ref[:, STATE:], state)
    spread_q = spread((q % 2) * (lanes // HEAD_DIM), lanes)
    y = y_ref[...] + carried * mm(hi_lo(jnp.exp(cum_ref[...])), spread_q)
    g = y * silu(z_ref[...].astype(f32))
    same = (iota((2 * LANES, LANES), 0) % LANES) // HEAD_DIM == iota((2 * LANES, LANES), 1) // HEAD_DIM
    same = same.astype(bf16)
    for b in range(lanes // LANES):
        at = slice(b * LANES, (b + 1) * LANES)
        part = g[:, at]
        mean_sq = mm(hi_lo(part * part), same) * (1.0 / HEAD_DIM)
        out_ref[:, at] = (part * lax.rsqrt(mean_sq + epsilon) * gain_ref[:, at]).astype(bf16)


def gate(y, z, bc, cum, state, gain):
    rows = y.shape[0] // 2
    inner = y.shape[1]
    lanes = inner // 2
    return pl.pallas_call(
        gate_kernel,
        grid=(4,),
        in_specs=[
            pl.BlockSpec((rows, lanes), lambda q: (q // 2, q % 2)),
            pl.BlockSpec((rows, lanes), lambda q: (q // 2, q % 2)),
            pl.BlockSpec((rows, 2 * STATE), lambda q: (q // 2, 0)),
            pl.BlockSpec((rows, LANES), lambda q: (q // 2, 0)),
            pl.BlockSpec((8, 1, 16, lanes), lambda q: (0, q, 0, 0)),
            pl.BlockSpec((1, lanes), lambda q: (0, q % 2)),
        ],
        out_specs=pl.BlockSpec((rows, lanes), lambda q: (0, q)),
        out_shape=jax.ShapeDtypeStruct((rows, 2 * inner), bf16),
        compiler_params=pltpu.CompilerParams(dimension_semantics=("arbitrary",)),
        name="gate",
    )(y, z, bc, cum, state.reshape(8, 4, 16, lanes), gain)


def project_kernel(has_add, q_ref, gf_ref, gb_ref, wf_ref, wb_ref, *rest):
    adds, (out_ref, accf_ref, accb_ref) = rest[:has_add], rest[has_add:]
    k = pl.program_id(0)

    @pl.when(k == 0)
    def _():
        accf_ref[...] = mm(gf_ref[...], wf_ref[...])
        accb_ref[...] = mm(gb_ref[...], wb_ref[...])

    @pl.when(k > 0)
    def _():
        accf_ref[...] += mm(gf_ref[...], wf_ref[...])
        accb_ref[...] += mm(gb_ref[...], wb_ref[...])

    @pl.when(k == pl.num_programs(0) - 1)
    def _():
        one = flip_matrix(LANES)
        flip = jnp.concatenate([one, one], axis=0)
        blocks = out_ref.shape[1] // LANES
        for b in range(blocks):
            at = slice(b * LANES, (b + 1) * LANES)
            source = slice((blocks - 1 - b) * LANES, (blocks - b) * LANES)
            total = accf_ref[:, at] + mm(hi_lo(accb_ref[:, source]), flip)
            for add in adds:
                total = total + add[:, at].astype(f32)
            out_ref[:, at] = total.astype(out_ref.dtype)


def project(q, gated, weight, dtype, *adds):
    rows = gated.shape[0]
    inner, width = weight.shape
    lanes = width // 4
    steps = inner // TILE
    return pl.pallas_call(
        functools.partial(project_kernel, len(adds)),
        grid_spec=pltpu.PrefetchScalarGridSpec(
            num_scalar_prefetch=1,
            grid=(steps,),
            in_specs=[
                pl.BlockSpec((rows, TILE), lambda k, q: (0, k)),
                pl.BlockSpec((rows, TILE), lambda k, q: (0, steps + k)),
                pl.BlockSpec((TILE, lanes), lambda k, q: (k, q[0])),
                pl.BlockSpec((TILE, lanes), lambda k, q: (k, 3 - q[0])),
            ]
            + [pl.BlockSpec((rows, lanes), lambda k, q: (0, 0)) for _ in adds],
            out_specs=pl.BlockSpec((rows, lanes), lambda k, q: (0, 0)),
            scratch_shapes=[pltpu.VMEM((rows, lanes), f32), pltpu.VMEM((rows, lanes), f32)],
        ),
        out_shape=jax.ShapeDtypeStruct((rows, lanes), dtype),
        compiler_params=pltpu.CompilerParams(dimension_semantics=("arbitrary",)),
        cost_estimate=pl.CostEstimate(
            flops=4 * rows * inner * lanes, bytes_accessed=5 << 20, transcendentals=0
        ),
        name="project",
    )(q, gated, gated, weight, weight, *adds)


def per_device(
    hidden, norm_gain, x_weight, z_weight, bc_weight, dt_weight, x_kernel, bc_kernel,
    dt_bias, log_rate, out_gain, out_weight,
):
    blocks = lax.axis_size("ctx")
    place = lax.axis_index("ctx")
    head = lax.axis_index("head")
    prev_rows = lax.ppermute(hidden[-HALO:], "ctx", [(i, i + 1) for i in range(blocks - 1)])
    next_rows = lax.ppermute(hidden[:HALO], "ctx", [(i + 1, i) for i in range(blocks - 1)])
    pad = LANES - dt_weight.shape[1]
    normed, xconv, bc, delta, cum, cumt, pay = entry(
        hidden, prev_rows, next_rows, norm_gain[None], x_weight, bc_weight,
        jnp.pad(dt_weight, ((0, 0), (0, pad))), x_kernel, bc_kernel,
        jnp.pad(dt_bias, (0, pad))[None], jnp.pad(log_rate, (0, pad))[None], blocks,
    )
    pay = lax.all_to_all(pay, "ctx", 0, 0, tiled=True)
    z_in = jnp.dot(normed, z_weight, preferred_element_type=f32).astype(bf16)
    y = within(xconv, bc, cum, cumt, delta)
    state = scan((place % 4)[None], pay)
    state = lax.all_to_all(state, "ctx", 0, 0, tiled=True)
    gated = gate(y, z_in, bc, cum, state, out_gain[None])
    core, far = head % 2, head // 2
    quarter = lambda f, c: (2 * f + c)[None]
    core_swap = [(0, 1), (1, 0), (2, 3), (3, 2)]
    far_swap = [(0, 2), (2, 0), (1, 3), (3, 1)]
    first = project(quarter(1 - far, 1 - core), gated, out_weight, bf16)
    first = lax.ppermute(first, "head", core_swap)
    second = project(quarter(1 - far, core), gated, out_weight, bf16, first)
    second = lax.ppermute(second, "head", far_swap)
    third = project(quarter(far, 1 - core), gated, out_weight, bf16)
    third = lax.ppermute(third, "head", core_swap)
    lanes = hidden.shape[1] // 4
    residual = lax.dynamic_slice_in_dim(hidden, head * lanes, lanes, 1)
    own = project(quarter(far, core), gated, out_weight, f32, third, residual)
    return (own + second.astype(f32)).astype(bf16)


def solution(mesh):
    return jax.shard_map(
        per_device,
        mesh=mesh,
        in_specs=(
            P("ctx", None), P(), P(None, "head"), P(None, "head"), P(), P(None, "head"),
            P(None, "head"), P(), P("head"), P("head"), P("head"), P("head", None),
        ),
        out_specs=P("ctx", "head"),
        check_vma=False,
    )
```

time: 684 us -> 121 us (0.18)
  waiting for transfers between devices: 319 us -> 8.16 us
  blocking collectives: 141 us -> 0 us
  other arithmetic: 74.1 us -> 1.87 us
  local copies, waits for them, and re-layouts: 77.5 us -> 15.8 us
  Pallas kernels: 0 us -> 59.7 us
  matrix products: 46.3 us -> 7.46 us
  starting transfers between devices: 6.06 us -> 26.5 us
  between operations: 13.8 us -> 0.1 us
    all_gather x2 -> x0, waiting for transfers between devices: 233 us -> none  [prefix(): lax.all_gather(a.astype(kind), axis)]
    all_gather x2 -> x0, blocking collectives: 141 us -> none  [prefix(): lax.all_gather(a.astype(kind), axis)]
    unnamed x4 -> x0, waiting for transfers between devices: 85.9 us -> none
    pallas_call x0 -> x8, Pallas kernels: none -> 59.7 us  [the longest x4 24 us: project(): pl.pallas_call(functools.partial(project_kernel, len(adds)), grid_spec=pl...]
    dot_general x17 -> x1, matrix products: 46.3 us -> 7.46 us  [per_device(): z_in = jnp.dot(normed, z_weight, preferred_element_type=f32).astype(bf16)]
    rev x3 -> x0, local copies, waits for them, and re-layouts: 38.1 us -> none  [the longest x1 18.6 us: per_device(): partial_sum = projected[:row_count] + projected[row_count:, ::-1]]
    add x31 -> x0, other arithmetic: 35.6 us -> none  [link_states(): later_part[0][..., None, None] * earlier[1] + later_part[1]]
    convert_element_type x35 -> x1, other arithmetic: 31.7 us -> 1.87 us  [per_device(): return (own + second.astype(f32)).astype(bf16)]
  transfers between devices with their start and end apart: 5 -> 7, of which waited for: 3 -> 3; matrix products, arithmetic and copies ran while one was open for 16% -> 11% of each run, Pallas kernels for 0% -> 23%
where the time goes in v1:
time: 121 us; the launch traced here: 120 us
  Pallas kernels  59.7 us (49%)
  starting transfers between devices  26.5 us (22%)
  local copies, waits for them, and re-layouts  15.8 us (13%)
  waiting for transfers between devices  8.16 us (7%)
  matrix products  7.46 us (6%)
  other arithmetic  1.87 us (2%)
    pallas_call x4, Pallas kernels, project(): pl.pallas_call(functools.partial(project_kernel, len(adds)), grid_spec=pl...  24 us
    pallas_call x1, Pallas kernels, entry(): pl.pallas_call(entry_kernel, grid=(steps,), in_specs=[whole(rows, width),...  17.6 us
    unnamed x29, local copies, waits for them, and re-layouts  11 us
    all_to_all x1, starting transfers between devices, per_device(): pay = lax.all_to_all(pay, 'ctx', 0, 0, tiled=True)  10.6 us
    pallas_call x1, Pallas kernels, within(): pl.pallas_call(within_kernel, grid=(2, inner // TILE), in_specs=[pl.Block...  9.85 us
    dot_general x1, matrix products, per_device(): z_in = jnp.dot(normed, z_weight, preferred_element_type=f32).astype(bf16)  7.46 us
    pallas_call x1, Pallas kernels, gate(): pl.pallas_call(gate_kernel, grid=(4,), in_specs=[pl.BlockSpec((rows, lane...  5.66 us
    all_to_all x1, starting transfers between devices, per_device(): state = lax.all_to_all(state, 'ctx', 0, 0, tiled=True)  5.01 us
  transfers between devices with their start and end apart: 7, of which 3 were waited for; matrix products, arithmetic and copies ran while one was open for 11% of the time, Pallas kernels for 23%

profile of v1, /device:TPU:1, one launch (start us, length us, event | category | flops | bytes accessed | tf_op | source)
XLA Modules:
  0.0 119.5 jit_solution(6460511860323931483)
XLA Ops:
  0.0 0.9 fusion
  0.9 3.9 %collective-permute-start = (bf16[16,2560]{1,0:T(8,128)(2,1)S(1)}, bf16[16,2560]{1,0:T(8,128)(2,1)S(1)}, u32[]{:S(2)}, u32[]{:S(2)}) collective-permute-start(bf16[16,2560]{1,0:T(8,128)(2,1)S(1)} %get-tuple-element.20), channel_id=1, source_target_pairs={{0,4},{4,8},{8,12},{12,16},{16,20},{20,24},{24,28},{28,32},{32,36}... | collective-permute-start | bytes 245768 | tf_op jit(solution)/shard_map/ppermute | solution.py:360
  4.9 1.3 %collective-permute-start.1 = (bf16[16,2560]{1,0:T(8,128)(2,1)S(1)}, bf16[16,2560]{1,0:T(8,128)(2,1)S(1)}, u32[]{:S(2)}, u32[]{:S(2)}) collective-permute-start(bf16[16,2560]{1,0:T(8,128)(2,1)S(1)} %get-tuple-element.19), channel_id=1, source_target_pairs={{4,0},{8,4},{12,8},{16,12},{20,16},{24,20},{28,24},{32,28},{36,32}... | collective-permute-start | bytes 245768 | tf_op jit(solution)/shard_map/ppermute | solution.py:361
  6.2 1.3 %copy.13 = bf16[2560,20]{1,0:T(8,128)(2,1)S(1)} copy(bf16[2560,20]{0,1:T(8,128)(2,1)} %param.17) | data formatting | bytes 204800 | tf_op args[5]
  9.0 1.3 %collective-permute-done.1.next_ref = bf16[16,2560]{1,0:T(8,128)(2,1)S(1)} collective-permute-done((bf16[16,2560]{1,0:T(8,128)(2,1)S(1)}, bf16[16,2560]{1,0:T(8,128)(2,1)S(1)}, u32[]{:S(2)}, u32[]{:S(2)}) %collective-permute-start.1) | collective-permute-done | bytes 81952 | tf_op jit(solution)/shard_map/ppermute | solution.py:361
  10.3 1.3 %copy-done.2 = bf16[256,2560]{1,0:T(8,128)(2,1)S(1)} copy-done((bf16[256,2560]{1,0:T(8,128)(2,1)S(1)}, bf16[256,2560]{1,0:T(8,128)(2,1)}, u32[]{:S(2)}) %copy-start.2) | copy-done | bytes 1310744
  13.0 17.6 %entry.1 = (bf16[512,2560]{1,0:T(8,128)(2,1)}, bf16[512,1280]{1,0:T(8,128)(2,1)S(1)}, bf16[512,256]{1,0:T(8,128)(2,1)S(1)}, f32[512,128]{1,0:T(8,128)S(1)}, f32[...) custom-call(bf16[256,2560]{1,0:T(8,128)(2,1)S(1)} %copy-done.2, ...), custom_call_target="tpu_custom_call" | custom-call | flops 4634705920 | bytes 16777216 | tf_op jit(solution)/shard_map/entry/pallas_call | solution.py:138
  32.1 1.1 copy-done.5
  34.5 10.6 %all-to-all-start = ((bf16[32,16,768]{2,1,0:T(8,128)(2,1)}), bf16[32,16,768]{2,1,0:T(8,128)(2,1)S(1)}, u32[]{:S(2)}, u32[]{:S(2)}) async-start(bf16[32,16,768]{2,1,0:T(8,128)(2,1)} %get-tuple-element.18), calls=%async_computation | async-start | bytes 1572864 | tf_op jit(solution)/shard_map/all_to_all | solution.py:368
  45.6 9.9 %within.1.y_ref = f32[512,1280]{1,0:T(8,128)} custom-call(bf16[512,1280]{1,0:T(8,128)(2,1)} %copy-done.5, bf16[512,256]{1,0:T(8,128)(2,1)} %copy-done, f32[512,128]{1,0:T(8,128)} %copy-done.1, f32[2,24,256]{2,1,0:T(8,128)} %copy-done.7, f32[512,128]{1,0:T(8,128)} %copy-done.6), custom_call_target="tpu_custom_call" | custom-call | flops 3221225472 | bytes 5242880 | tf_op jit(solution)/shard_map/within/pallas_call | solution.py:208
  55.5 2.9 %all-to-all-done.pay_ref = bf16[32,16,768]{2,1,0:T(8,128)(2,1)S(1)} async-done(((bf16[32,16,768]{2,1,0:T(8,128)(2,1)}), bf16[32,16,768]{2,1,0:T(8,128)(2,1)S(1)}, u32[]{:S(2)}, u32[]{:S(2)}) %all-to-all-start) | async-done | bytes 786464 | tf_op jit(solution)/shard_map/all_to_all | solution.py:368
  59.3 2.5 %scan.1 = bf16[32,16,640]{2,1,0:T(8,128)(2,1)} custom-call(s32[1]{0:T(128)} %bitcast.3.q_ref, bf16[32,16,768]{2,1,0:T(8,128)(2,1)} %copy-done.8), custom_call_target="tpu_custom_call" | custom-call | tf_op jit(solution)/shard_map/scan/pallas_call | solution.py:247
  61.8 5.0 %all-to-all-start.1 = ((bf16[32,16,640]{2,1,0:T(8,128)(2,1)}), bf16[32,16,640]{2,1,0:T(8,128)(2,1)S(1)}, u32[]{:S(2)}, u32[]{:S(2)}) async-start(bf16[32,16,640]{2,1,0:T(8,128)(2,1)} %scan.1), calls=%async_computation.1 | async-start | bytes 1310720 | tf_op jit(solution)/shard_map/all_to_all | solution.py:372
  66.8 7.5 %convolution_convert_fusion.z_ref = bf16[512,1280]{1,0:T(8,128)(2,1)} fusion(bf16[512,2560]{1,0:T(8,128)(2,1)S(1)} %copy-done.13, bf16[2560,1280]{1,0:T(8,128)(2,1)} %param.15), kind=kOutput, calls=%fused_computation | convolution fusion | flops 3356098560 | bytes 10485760 | tf_op jit(solution)/shard_map/dot_general | solution.py:369
  74.3 3.9 %all-to-all-done.1 = bf16[32,16,640]{2,1,0:T(8,128)(2,1)S(1)} async-done(((bf16[32,16,640]{2,1,0:T(8,128)(2,1)}), bf16[32,16,640]{2,1,0:T(8,128)(2,1)S(1)}, u32[]{:S(2)}, u32[]{:S(2)}) %all-to-all-start.1) | async-done | bytes 655392 | tf_op jit(solution)/shard_map/all_to_all | solution.py:372
  79.1 5.7 %gate.1.gf_ref.gb_ref = bf16[256,2560]{1,0:T(8,128)(2,1)} custom-call(f32[512,1280]{1,0:T(8,128)} %within.1.y_ref, bf16[512,1280]{1,0:T(8,128)(2,1)} %convolution_convert_fusion.z_ref, bf16[512,256]{1,0:T(8,128)(2,1)} %copy-done, f32[512,128]{1,0:T(8,128)} %copy-done.1, bf16[8,4,16,640]{3,2,1,0:T(8,128)(2,1)} %bitcast.12, f32[1,1280]{1,0:T(1,128)} %broadcast_in_dim.32.gain_ref), custom_call_target="tpu_custom_call" | custom-call | tf_op jit(solution)/shard_map/gate/pallas_call | solution.py:278
  84.7 5.9 %project.6 = bf16[256,640]{1,0:T(8,128)(2,1)} custom-call(s32[1]{0:T(128)} %bitcast.7.q_ref, bf16[256,2560]{1,0:T(8,128)(2,1)} %gate.1.gf_ref.gb_ref, bf16[256,2560]{1,0:T(8,128)(2,1)} %gate.1.gf_ref.gb_ref, bf16[1280,2560]{1,0:T(8,128)(2,1)} %wb_ref.7, bf16[1280,2560]{1,0:T(8,128)(2,1)} %wb_ref.7), custom_call_target="tpu_custom_call" | custom-call | flops 838860800 | bytes 5242880 | tf_op jit(solution)/shard_map/project/pallas_call | solution.py:329
  90.6 3.2 %collective-permute-start.3 = (bf16[256,640]{1,0:T(8,128)(2,1)}, bf16[256,640]{1,0:T(8,128)(2,1)S(1)}, u32[]{:S(2)}, u32[]{:S(2)}) collective-permute-start(bf16[256,640]{1,0:T(8,128)(2,1)} %project.6), channel_id=1, source_target_pairs={{0,1},{1,0},{2,3},{3,2},{4,5},{5,4},{6,7},{7,6},{8,9},{9,8},{10,11... | collective-permute-start | bytes 983048 | tf_op jit(solution)/shard_map/ppermute | solution.py:379
  93.8 5.9 %project.4 = bf16[256,640]{1,0:T(8,128)(2,1)} custom-call(s32[1]{0:T(128)} %bitcast.5.q_ref, bf16[256,2560]{1,0:T(8,128)(2,1)} %gate.1.gf_ref.gb_ref, bf16[256,2560]{1,0:T(8,128)(2,1)} %gate.1.gf_ref.gb_ref, bf16[1280,2560]{1,0:T(8,128)(2,1)} %wb_ref.7, bf16[1280,2560]{1,0:T(8,128)(2,1)} %wb_ref.7), custom_call_target="tpu_custom_call" | custom-call | flops 838860800 | bytes 5242880 | tf_op jit(solution)/shard_map/project/pallas_call | solution.py:329
  100.5 6.0 %project.7 = bf16[256,640]{1,0:T(8,128)(2,1)} custom-call(s32[1]{0:T(128)} %bitcast.6.q_ref, bf16[256,2560]{1,0:T(8,128)(2,1)} %gate.1.gf_ref.gb_ref, bf16[256,2560]{1,0:T(8,128)(2,1)} %gate.1.gf_ref.gb_ref, bf16[1280,2560]{1,0:T(8,128)(2,1)} %wb_ref.7, bf16[1280,2560]{1,0:T(8,128)(2,1)} %wb_ref.7, bf16[256,640]{1,0:T(8,128)(2,1)} %copy-done.11), custom_call_target="tpu_custom_call" | custom-call | flops 838860800 | bytes 5242880 | tf_op jit(solution)/shard_map/project/pallas_call | solution.py:329
  106.5 2.5 %collective-permute-start.4 = (bf16[256,640]{1,0:T(8,128)(2,1)}, bf16[256,640]{1,0:T(8,128)(2,1)S(1)}, u32[]{:S(2)}, u32[]{:S(2)}) collective-permute-start(bf16[256,640]{1,0:T(8,128)(2,1)} %project.7), channel_id=1, source_target_pairs={{0,2},{2,0},{1,3},{3,1},{4,6},{6,4},{5,7},{7,5},{8,10},{10,8},{9,1... | collective-permute-start | bytes 983048 | tf_op jit(solution)/shard_map/ppermute | solution.py:381
  108.9 1.7 %constant_dynamic-slice_fusion.rest_1_ = bf16[256,640]{1,0:T(8,128)(2,1)} fusion(bf16[256,2560]{1,0:T(8,128)(2,1)} %h_ref.1, s32[]{:T(128)S(6)} %select_n.21), kind=kLoop, calls=%fused_computation.4 | loop fusion | bytes 655364 | tf_op jit(solution)/shard_map/dynamic_slice | solution.py:385
  111.4 6.2 %project.5 = f32[256,640]{1,0:T(8,128)} custom-call(s32[1]{0:T(128)} %bitcast.q_ref, bf16[256,2560]{1,0:T(8,128)(2,1)} %gate.1.gf_ref.gb_ref, bf16[256,2560]{1,0:T(8,128)(2,1)} %gate.1.gf_ref.gb_ref, bf16[1280,2560]{1,0:T(8,128)(2,1)} %wb_ref.7, bf16[1280,2560]{1,0:T(8,128)(2,1)} %wb_ref.7, bf16[256,640]{1,0:T(8,128)(2,1)} %copy-done.10, ...), custom_call_target="tpu_custom_call" | custom-call | flops 838860800 | bytes 5242880 | tf_op jit(solution)/shard_map/project/pallas_call | solution.py:329
  117.6 1.9 %add_convert_fusion = bf16[256,640]{1,0:T(8,128)(2,1)} fusion(f32[256,640]{1,0:T(8,128)} %project.5, bf16[256,640]{1,0:T(8,128)(2,1)S(1)} %collective-permute-done.4), kind=kLoop, calls=%fused_computation.1 | loop fusion | flops 491520 | bytes 1310720 | tf_op jit(solution)/shard_map/convert_element_type | solution.py:387
  (35 shorter events, 9.5 us)
Async XLA Ops:
  0.9 8.0 %collective-permute-start = (bf16[16,2560]{1,0:T(8,128)(2,1)S(1)}, bf16[16,2560]{1,0:T(8,128)(2,1)S(1)}, u32[]{:S(2)}, u32[]{:S(2)}) collective-permute-start(bf16[16,2560]{1,0:T(8,128)(2,1)S(1)} %get-tuple-element.20), channel_id=1, source_target_pairs={{0,4},{4,8},{8,12},{12,16},{16,20},{20,24},{24,28},{28,32},{32,36}... | collective-permute-start | bytes 245768 | tf_op jit(solution)/shard_map/ppermute | solution.py:360
  4.9 5.4 %collective-permute-start.1 = (bf16[16,2560]{1,0:T(8,128)(2,1)S(1)}, bf16[16,2560]{1,0:T(8,128)(2,1)S(1)}, u32[]{:S(2)}, u32[]{:S(2)}) collective-permute-start(bf16[16,2560]{1,0:T(8,128)(2,1)S(1)} %get-tuple-element.19), channel_id=1, source_target_pairs={{4,0},{8,4},{12,8},{16,12},{20,16},{24,20},{28,24},{32,28},{36,32}... | collective-permute-start | bytes 245768 | tf_op jit(solution)/shard_map/ppermute | solution.py:361
  10.3 1.3 %copy-start.2 = (bf16[256,2560]{1,0:T(8,128)(2,1)S(1)}, bf16[256,2560]{1,0:T(8,128)(2,1)}, u32[]{:S(2)}) copy-start(bf16[256,2560]{1,0:T(8,128)(2,1)} %h_ref.1) | copy-start | bytes 3932164
  11.6 0.7 copy-start.3
  12.4 0.7 copy-start.4
  13.0 32.0 %copy-start.12 = (f32[1280]{0:T(1024)S(1)}, f32[1280]{0:T(1024)}, u32[]{:S(2)}) copy-start(f32[1280]{0:T(1024)} %param.22) | copy-start | bytes 15364
  30.7 0.7 copy-start
  31.4 0.7 copy-start.1
  32.0 1.1 copy-start.5
  33.1 0.7 copy-start.6
  33.8 0.6 copy-start.7
  34.5 23.9 %all-to-all-start = ((bf16[32,16,768]{2,1,0:T(8,128)(2,1)}), bf16[32,16,768]{2,1,0:T(8,128)(2,1)S(1)}, u32[]{:S(2)}, u32[]{:S(2)}) async-start(bf16[32,16,768]{2,1,0:T(8,128)(2,1)} %get-tuple-element.18), calls=%async_computation | async-start | bytes 1572864 | tf_op jit(solution)/shard_map/all_to_all | solution.py:368
  55.5 11.3 %copy-start.13 = (bf16[512,2560]{1,0:T(8,128)(2,1)S(1)}, bf16[512,2560]{1,0:T(8,128)(2,1)}, u32[]{:S(2)}) copy-start(bf16[512,2560]{1,0:T(8,128)(2,1)} %get-tuple-element.17) | copy-start | bytes 7864324
  58.4 0.9 copy-start.8
  61.8 16.4 %all-to-all-start.1 = ((bf16[32,16,640]{2,1,0:T(8,128)(2,1)}), bf16[32,16,640]{2,1,0:T(8,128)(2,1)S(1)}, u32[]{:S(2)}, u32[]{:S(2)}) async-start(bf16[32,16,640]{2,1,0:T(8,128)(2,1)} %scan.1), calls=%async_computation.1 | async-start | bytes 1310720 | tf_op jit(solution)/shard_map/all_to_all | solution.py:372
  78.2 0.8 copy-start.9
  90.6 9.1 %collective-permute-start.3 = (bf16[256,640]{1,0:T(8,128)(2,1)}, bf16[256,640]{1,0:T(8,128)(2,1)S(1)}, u32[]{:S(2)}, u32[]{:S(2)}) collective-permute-start(bf16[256,640]{1,0:T(8,128)(2,1)} %project.6), channel_id=1, source_target_pairs={{0,1},{1,0},{2,3},{3,2},{4,5},{5,4},{6,7},{7,6},{8,9},{9,8},{10,11... | collective-permute-start | bytes 983048 | tf_op jit(solution)/shard_map/ppermute | solution.py:379
  99.7 11.0 %collective-permute-start.2 = (bf16[256,640]{1,0:T(8,128)(2,1)}, bf16[256,640]{1,0:T(8,128)(2,1)S(1)}, u32[]{:S(2)}, u32[]{:S(2)}) collective-permute-start(bf16[256,640]{1,0:T(8,128)(2,1)} %project.4), channel_id=1, source_target_pairs={{0,1},{1,0},{2,3},{3,2},{4,5},{5,4},{6,7},{7,6},{8,9},{9,8},{10,11... | collective-permute-start | bytes 983048 | tf_op jit(solution)/shard_map/ppermute | solution.py:383
  99.7 0.7 copy-start.11
  106.5 11.2 %collective-permute-start.4 = (bf16[256,640]{1,0:T(8,128)(2,1)}, bf16[256,640]{1,0:T(8,128)(2,1)S(1)}, u32[]{:S(2)}, u32[]{:S(2)}) collective-permute-start(bf16[256,640]{1,0:T(8,128)(2,1)} %project.7), channel_id=1, source_target_pairs={{0,2},{2,0},{1,3},{3,1},{4,6},{6,4},{5,7},{7,5},{8,10},{10,8},{9,1... | collective-permute-start | bytes 983048 | tf_op jit(solution)/shard_map/ppermute | solution.py:381
  110.7 0.7 copy-start.10

commit v2 on v1

v2 whole, which is shorter than its diff:
```python
import functools

import jax
import jax.numpy as jnp
from jax import lax
from jax.experimental import pallas as pl
from jax.experimental.pallas import tpu as pltpu
from jax.sharding import PartitionSpec as P

HEAD_DIM = 64
STATE = 128
HALO = 16
TILE = 256
LANES = 128
epsilon = 1e-05
highest = lax.Precision.HIGHEST
f32 = jnp.float32
bf16 = jnp.bfloat16


def mm(a, b, precision=None):
    return jnp.dot(a, b, preferred_element_type=f32, precision=precision)


def iota(shape, dim):
    return lax.broadcasted_iota(jnp.int32, shape, dim)


def silu(v):
    return v * jax.nn.sigmoid(v)


def flip_matrix(n):
    return (iota((n, n), 0) + iota((n, n), 1) == n - 1).astype(bf16)


def hi_lo(v):
    hi = v.astype(bf16)
    return jnp.concatenate([hi, (v - hi.astype(f32)).astype(bf16)], axis=1)


def spread(first, width):
    rows = iota((2 * LANES, width), 0) % LANES
    return (rows == first + iota((2 * LANES, width), 1) // HEAD_DIM).astype(bf16)


def conv_pair(ext_ref, taps, rows):
    first, second = HALO - 3, HALO + rows
    fwd = bwd = None
    for k in range(4):
        tap = taps[k : k + 1]
        ahead = tap * ext_ref[first + k : first + k + rows]
        behind = tap * ext_ref[second + 3 - k : second + 3 - k + rows]
        fwd = ahead if fwd is None else fwd + ahead
        bwd = behind if bwd is None else bwd + behind
    return silu(fwd).astype(bf16), silu(bwd).astype(bf16)


def cumulate(matrix, v, lanes):
    v = jnp.where(iota(v.shape, 1) < lanes, v, 0.0)
    hi = v.astype(bf16).astype(f32)
    mid = (v - hi).astype(bf16).astype(f32)
    low = v - hi - mid
    packed = hi + pltpu.roll(mid, 32, 1) + pltpu.roll(low, 64, 1)
    out = mm(matrix, packed.astype(bf16))
    return out + pltpu.roll(out, LANES - 32, 1) + pltpu.roll(out, LANES - 64, 1)


def entry_kernel(
    h_ref, prev_ref, next_ref, gain_ref, xw_ref, bcw_ref, dtw_ref, xk_ref, bck_ref, dtb_ref, lr_ref,
    x_ref, xconv_ref, bc_ref, delta_ref, cum_ref, cumt_ref, pay_ref,
    ext_ref, xin_ref, st_ref, bt_ref, wend_ref, dec_ref, rs_ref, dtp_ref,
):
    rows, width = h_ref.shape
    heads = dtb_ref.shape[1]
    n = pl.program_id(0)
    steps = pl.num_programs(0) - 1
    groups = width // LANES

    def scale_of(v):
        return lax.rsqrt(jnp.mean(v * v, axis=-1, keepdims=True) + epsilon)

    def scaled(v, scale, first):
        parts = [
            (v[:, g * LANES : (g + 1) * LANES] * scale) * gain_ref[first + g : first + g + 1]
            for g in range(v.shape[1] // LANES)
        ]
        return jnp.concatenate(parts, axis=1).astype(bf16)

    def prelude():
        def forward(i, _):
            at = pl.ds(pl.multiple_of(i * 32, 32), 32)
            v = h_ref[at].astype(f32)
            scale = scale_of(v)
            rs_ref[at] = jnp.broadcast_to(scale, (32, LANES))
            ext_ref[pl.ds(pl.multiple_of(HALO + i * 32, HALO), 32)] = scaled(v, scale, 0)
            return 0

        lax.fori_loop(0, rows // 32, forward, 0)
        prev = prev_ref[...].astype(f32)
        ext_ref[0:HALO] = scaled(prev, scale_of(prev), 0)
        flip = flip_matrix(TILE)
        blocks = width // TILE
        after = next_ref[...]
        after_scale = scale_of(after.astype(f32))
        stacked = jnp.concatenate([after[:, b * TILE : (b + 1) * TILE] for b in range(blocks)], axis=0)
        stacked = mm(stacked, flip)
        scale = rs_ref[...]
        for b in range(blocks):
            mirror = blocks - 1 - b
            cols = slice(b * TILE, (b + 1) * TILE)
            turned = mm(h_ref[:, mirror * TILE : (mirror + 1) * TILE], flip)
            ext_ref[HALO + rows : HALO + 2 * rows, cols] = scaled(turned, scale, b * 2)
            ext_ref[HALO + 2 * rows :, cols] = scaled(
                stacked[mirror * HALO : (mirror + 1) * HALO], after_scale, b * 2
            )
        main = ext_ref[HALO : HALO + 2 * rows]
        x_ref[...] = main
        xin_ref[...] = mm(ext_ref[...], bcw_ref[...]).astype(bf16).astype(f32)
        dtp_ref[...] = jnp.zeros_like(dtp_ref)
        dtp_ref[0:heads] = dtw_ref[...]
        bias = jnp.concatenate([dtb_ref[...], jnp.zeros((1, LANES - heads), f32)], axis=1)
        rate = jnp.concatenate([lr_ref[...], jnp.zeros((1, LANES - heads), f32)], axis=1)
        dt = lax.dot_general(main, dtp_ref[...], (((1,), (1,)), ((), ())), preferred_element_type=f32)
        dt = dt + bias
        bc_pair = conv_pair(xin_ref, bck_ref[...], rows)
        delta = jnp.maximum(dt, 0.0) + jnp.log1p(jnp.exp(-jnp.abs(dt)))
        delta_ref[...] = delta
        log_decay = -delta * jnp.exp(rate)
        lower = (iota((rows, rows), 0) >= iota((rows, rows), 1)).astype(bf16)
        upper = (iota((rows, rows), 0) <= iota((rows, rows), 1)).astype(bf16)
        for d in range(2):
            at = slice(d * rows, (d + 1) * rows)
            bc_ref[at] = bc_pair[d]
            bt_ref[d] = jnp.transpose(bc_pair[d][:, :STATE].astype(f32)).astype(bf16)
            cum = cumulate(upper if d else lower, log_decay[at], heads)
            cum_ref[at] = cum
            cumt_ref[d] = jnp.transpose(cum)[: cumt_ref.shape[1]]
            last = cum[0:1] if d else cum[rows - 1 : rows]
            wend_ref[at] = hi_lo(jnp.exp(jnp.minimum(last - cum, 0.0)) * delta[at])
            dec_ref[d : d + 1] = jnp.exp(last)

    def product():
        return mm(ext_ref[...], xw_ref[...]).astype(bf16).astype(f32)

    def finish():
        tile = n - 1
        pair = conv_pair(xin_ref, xk_ref[...], rows)
        spread_n = spread(tile * (TILE // HEAD_DIM), TILE)
        for d in range(2):
            at = slice(d * rows, (d + 1) * rows)
            xconv_ref[at] = pair[d]
            weighted = (pair[d].astype(f32) * mm(wend_ref[at], spread_n)).astype(bf16)
            column = pl.multiple_of(d * steps * TILE + tile * TILE, TILE)
            st_ref[:, pl.ds(column, TILE)] = mm(bt_ref[d], weighted).astype(bf16)

    @pl.when(n == 0)
    def _():
        prelude()
        xin_ref[...] = product()

    @pl.when((n > 0) & (n < steps))
    def _():
        finish()
        xin_ref[...] = product()

    @pl.when(n == steps)
    def _():
        finish()
        slots = pay_ref.shape[0]
        row = iota((8, LANES), 0)
        tails = []
        for d in range(2):
            dec = jnp.broadcast_to(dec_ref[d : d + 1], (8, LANES))
            dec = jnp.where(iota((8, LANES), 1) < heads, dec, 0.0)
            hi = dec.astype(bf16).astype(f32)
            tails.append(jnp.where(row == 0, hi, jnp.where(row == 1, dec - hi, 0.0)).astype(bf16))
        for slot in range(slots):
            i, q = slot // 4, slot % 4
            for j in range(5):
                column = (5 * q + j) * LANES
                pay_ref[slot, 16 * j : 16 * j + 16] = st_ref[16 * i : 16 * i + 16, column : column + LANES]
            pay_ref[slot, 80:88] = tails[q // 2]


def entry(hidden, prev_rows, next_rows, gain, xw, bcw, dtw, xk, bck, dtb, lr, slots):
    rows, width = hidden.shape
    inner = xw.shape[1]
    heads = dtb.shape[1]
    steps = inner // TILE
    ahead = lambda n: jnp.minimum(n, steps - 1)
    behind = lambda n: jnp.maximum(n - 1, 0)
    whole = lambda *shape: pl.BlockSpec(shape, lambda n: (0,) * len(shape))
    once = lambda *shape: pl.BlockSpec(
        shape, lambda n: (0,) * len(shape), pipeline_mode=pl.Buffered(1)
    )
    return pl.pallas_call(
        entry_kernel,
        grid=(steps + 1,),
        in_specs=[
            once(rows, width), once(HALO, width), once(HALO, width), once(width // LANES, LANES),
            pl.BlockSpec((width, TILE), lambda n: (0, ahead(n))),
            once(width, 2 * STATE), once(heads, width),
            pl.BlockSpec((4, TILE), lambda n: (0, behind(n))),
            once(4, 2 * STATE), once(1, heads), once(1, heads),
        ],
        out_specs=[
            whole(2 * rows, width),
            pl.BlockSpec((2 * rows, TILE), lambda n: (0, behind(n))),
            whole(2 * rows, 2 * STATE), whole(2 * rows, LANES), whole(2 * rows, LANES),
            whole(2, 24, rows), whole(slots, 88, LANES),
        ],
        out_shape=[
            jax.ShapeDtypeStruct((2 * rows, width), bf16),
            jax.ShapeDtypeStruct((2 * rows, inner), bf16),
            jax.ShapeDtypeStruct((2 * rows, 2 * STATE), bf16),
            jax.ShapeDtypeStruct((2 * rows, LANES), f32),
            jax.ShapeDtypeStruct((2 * rows, LANES), f32),
            jax.ShapeDtypeStruct((2, 24, rows), f32),
            jax.ShapeDtypeStruct((slots, 88, LANES), bf16),
        ],
        scratch_shapes=[
            pltpu.VMEM((2 * rows + 2 * HALO, width), bf16),
            pltpu.VMEM((2 * rows + 2 * HALO, TILE), f32),
            pltpu.VMEM((STATE, 2 * inner), bf16),
            pltpu.VMEM((2, STATE, rows), bf16),
            pltpu.VMEM((2 * rows, 2 * LANES), bf16),
            pltpu.VMEM((8, LANES), f32),
            pltpu.VMEM((rows, LANES), f32),
            pltpu.VMEM((LANES, width), bf16),
        ],
        compiler_params=pltpu.CompilerParams(
            dimension_semantics=("arbitrary",), vmem_limit_bytes=30 << 20
        ),
        cost_estimate=pl.CostEstimate(
            flops=2 * 544 * width * (inner + 384), bytes_accessed=16 << 20, transcendentals=0
        ),
        name="entry",
    )(hidden, prev_rows, next_rows, gain, xw, bcw, dtw, xk, bck, dtb, lr)


def within_kernel(x_ref, bc_ref, cum_ref, cumt_ref, delta_ref, y_ref, gram_ref):
    d, n = pl.program_id(0), pl.program_id(1)
    rows = x_ref.shape[0]
    heads = TILE // HEAD_DIM

    @pl.when(n == 0)
    def _():
        gram = lax.dot_general(
            bc_ref[:, STATE:], bc_ref[:, :STATE], (((1,), (1,)), ((), ())), preferred_element_type=f32
        )
        t, s = iota((rows, rows), 0), iota((rows, rows), 1)
        seen = jnp.where(d == 0, t - s, s - t) >= 0
        gram_ref[...] = jnp.where(seen, gram, 0.0)

    weighted = x_ref[...].astype(f32) * mm(hi_lo(delta_ref[...]), spread(n * heads, TILE))
    cum = pltpu.roll(cum_ref[...], (LANES - n * heads) % LANES, 1)
    owner = iota((rows, TILE), 1) // HEAD_DIM
    total = jnp.zeros((rows, TILE), f32)
    for k in range(heads):
        behind = cumt_ref[0, pl.ds(n * heads + k, 1), :]
        decay = jnp.exp(jnp.minimum(cum[:, k : k + 1] - behind, 0.0)) * gram_ref[...]
        total = total + mm(decay.astype(bf16), jnp.where(owner == k, weighted, 0.0).astype(bf16))
    y_ref[...] = total


def within(xconv, bc, cum, cumt, delta):
    rows = xconv.shape[0] // 2
    inner = xconv.shape[1]
    return pl.pallas_call(
        within_kernel,
        grid=(2, inner // TILE),
        in_specs=[
            pl.BlockSpec((rows, TILE), lambda d, n: (d, n)),
            pl.BlockSpec((rows, 2 * STATE), lambda d, n: (d, 0)),
            pl.BlockSpec((rows, LANES), lambda d, n: (d, 0)),
            pl.BlockSpec((1, 24, rows), lambda d, n: (d, 0, 0)),
            pl.BlockSpec((rows, LANES), lambda d, n: (d, 0)),
        ],
        out_specs=pl.BlockSpec((rows, TILE), lambda d, n: (d, n)),
        out_shape=jax.ShapeDtypeStruct((2 * rows, inner), f32),
        scratch_shapes=[pltpu.VMEM((rows, rows), f32)],
        compiler_params=pltpu.CompilerParams(
            dimension_semantics=("arbitrary", "arbitrary"), vmem_limit_bytes=12 << 20
        ),
        cost_estimate=pl.CostEstimate(flops=3 << 30, bytes_accessed=5 << 20, transcendentals=3 << 20),
        name="within",
    )(xconv, bc, cum, cumt, delta)


def scan_kernel(q_ref, pay_ref, out_ref, carry_ref):
    q = q_ref[0]
    half, turned = q % 2, q // 2
    depth = pay_ref.shape[0]

    @pl.when(pl.program_id(0) == 0)
    def _():
        carry_ref[...] = jnp.zeros_like(carry_ref)

    first = half * (5 * LANES // HEAD_DIM)
    place = iota((LANES, 5 * LANES), 0) == first + iota((LANES, 5 * LANES), 1) // HEAD_DIM
    place = place.astype(bf16)
    carry = [carry_ref[16 * j : 16 * j + 16] for j in range(5)]
    for i in range(depth):
        at = jnp.where(turned == 1, depth - 1 - i, i)
        decays = mm(pay_ref[at, 80:88], place)
        decay = decays[0:1] + decays[1:2]
        for j in range(5):
            rows = slice(16 * j, 16 * j + 16)
            out_ref[at, rows] = carry[j].astype(bf16)
            carry[j] = carry[j] * decay[:, j * LANES : (j + 1) * LANES] + pay_ref[at, rows].astype(f32)
    for j in range(5):
        carry_ref[16 * j : 16 * j + 16] = carry[j]


def scan(q, pay):
    slots = pay.shape[0]
    depth = 8
    steps = slots // depth
    chunk = lambda i, q: (jnp.where(q[0] // 2 == 1, steps - 1 - i, i), 0, 0)
    return pl.pallas_call(
        scan_kernel,
        grid_spec=pltpu.PrefetchScalarGridSpec(
            num_scalar_prefetch=1,
            grid=(steps,),
            in_specs=[pl.BlockSpec((depth, 88, LANES), chunk)],
            out_specs=pl.BlockSpec((depth, 80, LANES), chunk),
            scratch_shapes=[pltpu.VMEM((80, LANES), f32)],
        ),
        out_shape=jax.ShapeDtypeStruct((slots, 80, LANES), bf16),
        compiler_params=pltpu.CompilerParams(
            dimension_semantics=("arbitrary",), vmem_limit_bytes=6 << 20
        ),
        name="scan",
    )(q, pay)


def gate_kernel(y_ref, z_ref, bc_ref, cum_ref, st_ref, gain_ref, out_ref):
    q = pl.program_id(0)
    rows, lanes = y_ref.shape
    groups = lanes // LANES
    state = jnp.concatenate([st_ref[:, 0, j].reshape(STATE, LANES) for j in range(groups)], axis=1)
    carried = mm(bc_ref[:, STATE:], state)
    reach = mm(hi_lo(jnp.exp(cum_ref[...])), spread((q % 2) * (lanes // HEAD_DIM), lanes))
    same = (iota((2 * LANES, LANES), 0) % LANES) // HEAD_DIM == iota((2 * LANES, LANES), 1) // HEAD_DIM
    same = same.astype(bf16)
    for b in range(groups):
        at = slice(b * LANES, (b + 1) * LANES)
        y = y_ref[:, at] + carried[:, at] * reach[:, at]
        part = y * silu(z_ref[:, at].astype(f32))
        mean_sq = mm(hi_lo(part * part), same) * (1.0 / HEAD_DIM)
        gain = gain_ref[pl.ds((q % 2) * groups + b, 1), :]
        out_ref[:, at] = (part * lax.rsqrt(mean_sq + epsilon) * gain).astype(bf16)


def gate(y, z, bc, cum, state, gain):
    rows = y.shape[0] // 2
    inner = y.shape[1]
    lanes = inner // 2
    groups = lanes // LANES
    return pl.pallas_call(
        gate_kernel,
        grid=(4,),
        in_specs=[
            pl.BlockSpec((rows, lanes), lambda q: (q // 2, q % 2)),
            pl.BlockSpec((rows, lanes), lambda q: (q // 2, q % 2)),
            pl.BlockSpec((rows, 2 * STATE), lambda q: (q // 2, 0)),
            pl.BlockSpec((rows, LANES), lambda q: (q // 2, 0)),
            pl.BlockSpec((8, 1, groups, 16, LANES), lambda q: (0, q, 0, 0, 0)),
            pl.BlockSpec((2 * groups, LANES), lambda q: (0, 0)),
        ],
        out_specs=pl.BlockSpec((rows, lanes), lambda q: (0, q)),
        out_shape=jax.ShapeDtypeStruct((rows, 2 * inner), bf16),
        compiler_params=pltpu.CompilerParams(
            dimension_semantics=("arbitrary",), vmem_limit_bytes=14 << 20
        ),
        name="gate",
    )(y, z, bc, cum, state.reshape(8, 4, groups, 16, LANES), gain)


def project_kernel(has_add, q_ref, g_ref, w_ref, *rest):
    adds, (out_ref,) = rest[:has_add], rest[has_add:]
    inner = w_ref.shape[0]
    lanes = out_ref.shape[1]
    q = q_ref[0]
    near = pl.ds(pl.multiple_of(q * lanes, LANES), lanes)
    far = pl.ds(pl.multiple_of((3 - q) * lanes, LANES), lanes)
    ahead = mm(g_ref[:, :inner], w_ref[:, near])
    behind = mm(g_ref[:, inner:], w_ref[:, far])
    one = flip_matrix(LANES)
    flip = jnp.concatenate([one, one], axis=0)
    blocks = lanes // LANES
    for b in range(blocks):
        at = slice(b * LANES, (b + 1) * LANES)
        source = slice((blocks - 1 - b) * LANES, (blocks - b) * LANES)
        total = ahead[:, at] + mm(hi_lo(behind[:, source]), flip)
        for add in adds:
            total = total + add[:, at].astype(f32)
        out_ref[:, at] = total.astype(out_ref.dtype)


def project(q, gated, weight, dtype, *adds):
    rows = gated.shape[0]
    inner, width = weight.shape
    lanes = width // 4
    vmem = pl.BlockSpec(memory_space=pltpu.VMEM)
    return pl.pallas_call(
        functools.partial(project_kernel, len(adds)),
        in_specs=[pl.BlockSpec(memory_space=pltpu.SMEM), vmem, vmem] + [vmem for _ in adds],
        out_specs=vmem,
        out_shape=jax.ShapeDtypeStruct((rows, lanes), dtype),
        compiler_params=pltpu.CompilerParams(vmem_limit_bytes=16 << 20),
        cost_estimate=pl.CostEstimate(
            flops=4 * rows * inner * lanes, bytes_accessed=5 << 20, transcendentals=0
        ),
        name="project",
    )(q, gated, weight, *adds)


def per_device(
    hidden, norm_gain, x_weight, z_weight, bc_weight, dt_weight, x_kernel, bc_kernel,
    dt_bias, log_rate, out_gain, out_weight,
):
    blocks = lax.axis_size("ctx")
    place = lax.axis_index("ctx")
    head = lax.axis_index("head")
    prev_rows = lax.ppermute(hidden[-HALO:], "ctx", [(i, i + 1) for i in range(blocks - 1)])
    next_rows = lax.ppermute(hidden[:HALO], "ctx", [(i + 1, i) for i in range(blocks - 1)])
    normed, xconv, bc, delta, cum, cumt, pay = entry(
        hidden, prev_rows, next_rows, norm_gain.reshape(-1, LANES), x_weight, bc_weight,
        dt_weight.T, x_kernel, bc_kernel, dt_bias[None], log_rate[None], blocks,
    )
    pay = lax.all_to_all(pay, "ctx", 0, 0, tiled=True)
    z_in = jnp.dot(normed, z_weight, preferred_element_type=f32).astype(bf16)
    y = within(xconv, bc, cum, cumt, delta)
    state = scan((place % 4)[None], pay)
    state = lax.all_to_all(state, "ctx", 0, 0, tiled=True)
    gated = gate(y, z_in, bc, cum, state, out_gain.reshape(-1, LANES))
    core, far = head % 2, head // 2
    quarter = lambda f, c: (2 * f + c)[None]
    core_swap = [(0, 1), (1, 0), (2, 3), (3, 2)]
    far_swap = [(0, 2), (2, 0), (1, 3), (3, 1)]
    first = project(quarter(1 - far, 1 - core), gated, out_weight, bf16)
    first = lax.ppermute(first, "head", core_swap)
    second = project(quarter(1 - far, core), gated, out_weight, bf16, first)
    second = lax.ppermute(second, "head", far_swap)
    third = project(quarter(far, 1 - core), gated, out_weight, bf16)
    third = lax.ppermute(third, "head", core_swap)
    lanes = hidden.shape[1] // 4
    residual = lax.dynamic_slice_in_dim(hidden, head * lanes, lanes, 1)
    own = project(quarter(far, core), gated, out_weight, f32, third, residual)
    return (own + second.astype(f32)).astype(bf16)


def solution(mesh):
    return jax.shard_map(
        per_device,
        mesh=mesh,
        in_specs=(
            P("ctx", None), P(), P(None, "head"), P(None, "head"), P(), P(None, "head"),
            P(None, "head"), P(), P("head"), P("head"), P("head"), P("head", None),
        ),
        out_specs=P("ctx", "head"),
        check_vma=False,
    )
```

time: 121 us -> 110 us (0.909)
  Pallas kernels: 59.7 us -> 31 us
  local copies, waits for them, and re-layouts: 15.8 us -> 28.9 us
  waiting for transfers between devices: 8.16 us -> 15.6 us
    pallas_call x6, Pallas kernels: 44.2 us -> 21.5 us  [the longest x1 13.2 us: entry(): pl.pallas_call(entry_kernel, grid=(steps + 1,), in_specs=[once(rows, widt...]
    unnamed x29 -> x38, local copies, waits for them, and re-layouts: 11 us -> 27 us
    pallas_call x1, Pallas kernels: 9.85 us -> 6.18 us  [within(): pl.pallas_call(within_kernel, grid=(2, inner // TILE), in_specs=[pl.Block...]
    ppermute x1, waiting for transfers between devices: 1.33 us -> 3.96 us  [per_device(): lax.ppermute(hidden[:HALO], 'ctx', [(i + 1, i) for i in range(blocks - 1)])]
    ppermute x1, waiting for transfers between devices: 0.01 us -> 2.4 us  [per_device(): second = lax.ppermute(second, 'head', far_swap)]
    pallas_call x1, Pallas kernels: 5.66 us -> 3.27 us  [gate(): pl.pallas_call(gate_kernel, grid=(4,), in_specs=[pl.BlockSpec((rows, lane...]
    broadcast_in_dim x3 -> x0, local copies, waits for them, and re-layouts: 1.99 us -> none  [the longest x1 0.71 us: per_device(): norm_gain[None]]
    all_to_all x1, waiting for transfers between devices: 2.89 us -> 4.85 us  [per_device(): pay = lax.all_to_all(pay, 'ctx', 0, 0, tiled=True)]
  transfers between devices with their start and end apart: 7 -> 7, of which waited for: 3 -> 5; matrix products, arithmetic and copies ran while one was open for 11% -> 7% of each run, Pallas kernels for 23% -> 10%
where the time goes in v2:
time: 110 us; the launch traced here: 109 us
  Pallas kernels  31 us (28%)
  local copies, waits for them, and re-layouts  28.9 us (26%)
  starting transfers between devices  25.8 us (23%)
  waiting for transfers between devices  15.6 us (14%)
  matrix products  7.2 us (7%)
    unnamed x38, local copies, waits for them, and re-layouts  27 us
    pallas_call x1, Pallas kernels, entry(): pl.pallas_call(entry_kernel, grid=(steps + 1,), in_specs=[once(rows, widt...  13.2 us
    all_to_all x1, starting transfers between devices, per_device(): pay = lax.all_to_all(pay, 'ctx', 0, 0, tiled=True)  10.6 us
    dot_general x1, matrix products, per_device(): z_in = jnp.dot(normed, z_weight, preferred_element_type=f32).astype(bf16)  7.2 us
    pallas_call x1, Pallas kernels, within(): pl.pallas_call(within_kernel, grid=(2, inner // TILE), in_specs=[pl.Block...  6.18 us
    pallas_call x4, Pallas kernels, project(): pl.pallas_call(functools.partial(project_kernel, len(adds)), in_specs=[pl...  6 us
    all_to_all x1, waiting for transfers between devices, per_device(): pay = lax.all_to_all(pay, 'ctx', 0, 0, tiled=True)  4.85 us
    all_to_all x1, waiting for transfers between devices, per_device(): state = lax.all_to_all(state, 'ctx', 0, 0, tiled=True)  4.21 us
  transfers between devices with their start and end apart: 7, of which 5 were waited for; matrix products, arithmetic and copies ran while one was open for 7% of the time, Pallas kernels for 10%

profile of v2, /device:TPU:1, one launch (start us, length us, event | category | flops | bytes accessed | tf_op | source)
XLA Modules:
  0.0 109.5 jit_solution(17301945469679515831)
XLA Ops:
  0.9 3.9 %collective-permute-start = (bf16[16,2560]{1,0:T(8,128)(2,1)S(1)}, bf16[16,2560]{1,0:T(8,128)(2,1)S(1)}, u32[]{:S(2)}, u32[]{:S(2)}) collective-permute-start(bf16[16,2560]{1,0:T(8,128)(2,1)S(1)} %get-tuple-element.20), channel_id=1, source_target_pairs={{0,4},{4,8},{8,12},{12,16},{16,20},{20,24},{24,28},{28,32},{32,36}... | collective-permute-start | bytes 245768 | tf_op jit(solution)/shard_map/ppermute | solution.py:427
  6.4 4.0 %collective-permute-done.1.next_ref = bf16[16,2560]{1,0:T(8,128)(2,1)S(1)} collective-permute-done((bf16[16,2560]{1,0:T(8,128)(2,1)S(1)}, bf16[16,2560]{1,0:T(8,128)(2,1)S(1)}, u32[]{:S(2)}, u32[]{:S(2)}) %collective-permute-start.1) | collective-permute-done | bytes 81952 | tf_op jit(solution)/shard_map/ppermute | solution.py:428
  11.6 2.9 %copy-done.10 = bf16[2560,1280]{1,0:T(8,128)(2,1)S(1)} copy-done((bf16[2560,1280]{1,0:T(8,128)(2,1)S(1)}, bf16[2560,1280]{1,0:T(8,128)(2,1)}, u32[]{:S(2)}) %copy-start.10) | copy-done | bytes 6553624
  20.1 13.2 %entry.1 = (bf16[512,2560]{1,0:T(8,128)(2,1)S(1)}, bf16[512,1280]{1,0:T(8,128)(2,1)S(1)}, bf16[512,256]{1,0:T(8,128)(2,1)S(1)}, f32[512,128]{1,0:T(8,128)S(1)}, ...) custom-call(bf16[256,2560]{1,0:T(8,128)(2,1)S(1)} %copy-done.8, ...), custom_call_target="tpu_custom_call" | custom-call | flops 4634705920 | bytes 16777216 | tf_op jit(solution)/shard_map/entry/pallas_call | solution.py:197
  33.3 1.5 %copy-done.18 = bf16[512,2560]{1,0:T(8,128)(2,1)} copy-done((bf16[512,2560]{1,0:T(8,128)(2,1)}, bf16[512,2560]{1,0:T(8,128)(2,1)S(1)}, u32[]{:S(2)}) %copy-start.18) | copy-done | bytes 2621464
  34.9 10.6 %all-to-all-start = ((bf16[32,88,128]{2,1,0:T(8,128)(2,1)}), bf16[32,88,128]{2,1,0:T(8,128)(2,1)S(1)}, u32[]{:S(2)}, u32[]{:S(2)}) async-start(bf16[32,88,128]{2,1,0:T(8,128)(2,1)} %get-tuple-element.18), calls=%async_computation | async-start | bytes 1441792 | tf_op jit(solution)/shard_map/all_to_all | solution.py:433
  45.5 6.2 %within.1.y_ref = f32[512,1280]{1,0:T(8,128)S(1)} custom-call(bf16[512,1280]{1,0:T(8,128)(2,1)S(1)} %get-tuple-element.12.x_ref, bf16[512,256]{1,0:T(8,128)(2,1)S(1)} %get-tuple-element.13.bc_ref, f32[512,128]{1,0:T(8,128)S(1)} %get-tuple-element.14.cum_ref, f32[2,24,256]{2,1,0:T(8,128)S(1)} %get-tuple-element.15.cumt_ref, ...), custom_call_target="tpu_custom_call" | custom-call | flops 3221225472 | bytes 5242880 | tf_op jit(solution)/shard_map/within/pallas_call | solution.py:270
  51.7 1.5 %copy-done.4 = f32[512,1280]{1,0:T(8,128)} copy-done((f32[512,1280]{1,0:T(8,128)}, f32[512,1280]{1,0:T(8,128)S(1)}, u32[]{:S(2)}) %copy-start.4) | copy-done | bytes 2621464
  53.2 4.8 %all-to-all-done.pay_ref = bf16[32,88,128]{2,1,0:T(8,128)(2,1)S(1)} async-done(((bf16[32,88,128]{2,1,0:T(8,128)(2,1)}), bf16[32,88,128]{2,1,0:T(8,128)(2,1)S(1)}, u32[]{:S(2)}, u32[]{:S(2)}) %all-to-all-start) | async-done | bytes 720928 | tf_op jit(solution)/shard_map/all_to_all | solution.py:433
  58.1 2.3 %scan.1 = bf16[32,80,128]{2,1,0:T(8,128)(2,1)} custom-call(s32[1]{0:T(128)} %bitcast.5.q_ref, bf16[32,88,128]{2,1,0:T(8,128)(2,1)S(1)} %all-to-all-done.pay_ref), custom_call_target="tpu_custom_call" | custom-call | tf_op jit(solution)/shard_map/scan/pallas_call | solution.py:321
  60.4 3.9 %all-to-all-start.1 = ((bf16[32,80,128]{2,1,0:T(8,128)(2,1)}), bf16[32,80,128]{2,1,0:T(8,128)(2,1)S(1)}, u32[]{:S(2)}, u32[]{:S(2)}) async-start(bf16[32,80,128]{2,1,0:T(8,128)(2,1)} %scan.1), calls=%async_computation.1 | async-start | bytes 1310720 | tf_op jit(solution)/shard_map/all_to_all | solution.py:437
  64.3 7.2 %convolution_convert_fusion.z_ref = bf16[512,1280]{1,0:T(8,128)(2,1)S(1)} fusion(bf16[512,2560]{1,0:T(8,128)(2,1)} %copy-done.18, bf16[2560,1280]{1,0:T(8,128)(2,1)} %param.15), kind=kOutput, calls=%fused_computation | convolution fusion | flops 3356098560 | bytes 10485760 | tf_op jit(solution)/shard_map/dot_general | solution.py:434
  71.5 4.2 %all-to-all-done.1 = bf16[32,80,128]{2,1,0:T(8,128)(2,1)S(1)} async-done(((bf16[32,80,128]{2,1,0:T(8,128)(2,1)}), bf16[32,80,128]{2,1,0:T(8,128)(2,1)S(1)}, u32[]{:S(2)}, u32[]{:S(2)}) %all-to-all-start.1) | async-done | bytes 655392 | tf_op jit(solution)/shard_map/all_to_all | solution.py:437
  75.7 1.7 %copy-done.5 = f32[512,1280]{1,0:T(8,128)S(1)} copy-done((f32[512,1280]{1,0:T(8,128)S(1)}, f32[512,1280]{1,0:T(8,128)}, u32[]{:S(2)}) %copy-start.5) | copy-done | bytes 2621464
  78.4 3.3 %gate.1.g_ref = bf16[256,2560]{1,0:T(8,128)(2,1)S(1)} custom-call(f32[512,1280]{1,0:T(8,128)S(1)} %copy-done.5, bf16[512,1280]{1,0:T(8,128)(2,1)S(1)} %convolution_convert_fusion.z_ref, bf16[512,256]{1,0:T(8,128)(2,1)S(1)} %get-tuple-element.13.bc_ref, f32[512,128]{1,0:T(8,128)S(1)} %copy-done.7, bf16[8,4,5,16,128]{4,3,2,1,0:T(8,128)(2,1)S(1)} %bitcast.13, ...), custom_call_target="tpu_custom_call" | custom-call | tf_op jit(solution)/shard_map/gate/pallas_call | solution.py:361
  81.7 2.9 %copy-done = bf16[1280,2560]{1,0:T(8,128)(2,1)S(1)} copy-done((bf16[1280,2560]{1,0:T(8,128)(2,1)S(1)}, bf16[1280,2560]{1,0:T(8,128)(2,1)}, u32[]{:S(2)}) %copy-start) | copy-done | bytes 6553624
  84.5 1.5 %project.6 = bf16[256,640]{1,0:T(8,128)(2,1)S(1)} custom-call(s32[1]{0:T(128)} %bitcast.10.q_ref, bf16[256,2560]{1,0:T(8,128)(2,1)S(1)} %gate.1.g_ref, bf16[1280,2560]{1,0:T(8,128)(2,1)S(1)} %copy-done), custom_call_target="tpu_custom_call" | custom-call | flops 838860800 | bytes 5242880 | tf_op jit(solution)/shard_map/project/pallas_call | solution.py:407
  86.1 3.4 %collective-permute-start.3 = (bf16[256,640]{1,0:T(8,128)(2,1)S(1)}, bf16[256,640]{1,0:T(8,128)(2,1)S(1)}, u32[]{:S(2)}, u32[]{:S(2)}) collective-permute-start(bf16[256,640]{1,0:T(8,128)(2,1)S(1)} %project.6), channel_id=1, source_target_pairs={{0,1},{1,0},{2,3},{3,2},{4,5},{5,4},{6,7},{7,6},{8,9},{9,8},{10,11... | collective-permute-start | bytes 983048 | tf_op jit(solution)/shard_map/ppermute | solution.py:444
  89.5 2.9 %copy-done.1 = bf16[1280,2560]{1,0:T(8,128)(2,1)S(1)} copy-done((bf16[1280,2560]{1,0:T(8,128)(2,1)S(1)}, bf16[1280,2560]{1,0:T(8,128)(2,1)}, u32[]{:S(2)}) %copy-start.1) | copy-done | bytes 6553624
  94.0 2.9 %copy-done.2 = bf16[1280,2560]{1,0:T(8,128)(2,1)S(1)} copy-done((bf16[1280,2560]{1,0:T(8,128)(2,1)S(1)}, bf16[1280,2560]{1,0:T(8,128)(2,1)}, u32[]{:S(2)}) %copy-start.2) | copy-done | bytes 6553624
  98.3 2.6 %collective-permute-start.4 = (bf16[256,640]{1,0:T(8,128)(2,1)S(1)}, bf16[256,640]{1,0:T(8,128)(2,1)S(1)}, u32[]{:S(2)}, u32[]{:S(2)}) collective-permute-start(bf16[256,640]{1,0:T(8,128)(2,1)S(1)} %project.7), channel_id=1, source_target_pairs={{0,2},{2,0},{1,3},{3,1},{4,6},{6,4},{5,7},{7,5},{8,10},{10,8},{9,1... | collective-permute-start | bytes 983048 | tf_op jit(solution)/shard_map/ppermute | solution.py:446
  101.9 2.9 %copy-done.3 = bf16[1280,2560]{1,0:T(8,128)(2,1)S(1)} copy-done((bf16[1280,2560]{1,0:T(8,128)(2,1)S(1)}, bf16[1280,2560]{1,0:T(8,128)(2,1)}, u32[]{:S(2)}) %copy-start.3) | copy-done | bytes 6553624
  104.8 1.5 %project.5 = f32[256,640]{1,0:T(8,128)S(1)} custom-call(s32[1]{0:T(128)} %bitcast.q_ref, bf16[256,2560]{1,0:T(8,128)(2,1)S(1)} %gate.1.g_ref, bf16[1280,2560]{1,0:T(8,128)(2,1)S(1)} %copy-done.3, bf16[256,640]{1,0:T(8,128)(2,1)S(1)} %collective-permute-done.2.rest_0_, bf16[256,640]{1,0:T(8,128)(2,1)S(1)} %constant_dynamic-slice_fusion.rest_1_), custom_call_target="tpu_custom_call" | custom-call | flops 838860800 | bytes 5242880 | tf_op jit(solution)/shard_map/project/pallas_call | solution.py:407
  106.3 2.4 %collective-permute-done.4 = bf16[256,640]{1,0:T(8,128)(2,1)S(1)} collective-permute-done((bf16[256,640]{1,0:T(8,128)(2,1)S(1)}, bf16[256,640]{1,0:T(8,128)(2,1)S(1)}, u32[]{:S(2)}, u32[]{:S(2)}) %collective-permute-start.4) | collective-permute-done | bytes 327712 | tf_op jit(solution)/shard_map/ppermute | solution.py:446
  (40 shorter events, 15.2 us)
Async XLA Ops:
  0.9 5.4 %collective-permute-start = (bf16[16,2560]{1,0:T(8,128)(2,1)S(1)}, bf16[16,2560]{1,0:T(8,128)(2,1)S(1)}, u32[]{:S(2)}, u32[]{:S(2)}) collective-permute-start(bf16[16,2560]{1,0:T(8,128)(2,1)S(1)} %get-tuple-element.20), channel_id=1, source_target_pairs={{0,4},{4,8},{8,12},{12,16},{16,20},{20,24},{24,28},{28,32},{32,36}... | collective-permute-start | bytes 245768 | tf_op jit(solution)/shard_map/ppermute | solution.py:427
  4.9 5.4 %collective-permute-start.1 = (bf16[16,2560]{1,0:T(8,128)(2,1)S(1)}, bf16[16,2560]{1,0:T(8,128)(2,1)S(1)}, u32[]{:S(2)}, u32[]{:S(2)}) collective-permute-start(bf16[16,2560]{1,0:T(8,128)(2,1)S(1)} %get-tuple-element.19), channel_id=1, source_target_pairs={{4,0},{8,4},{12,8},{16,12},{20,16},{24,20},{28,24},{32,28},{36,32}... | collective-permute-start | bytes 245768 | tf_op jit(solution)/shard_map/ppermute | solution.py:428
  10.3 1.3 %copy-start.8 = (bf16[256,2560]{1,0:T(8,128)(2,1)S(1)}, bf16[256,2560]{1,0:T(8,128)(2,1)}, u32[]{:S(2)}) copy-start(bf16[256,2560]{1,0:T(8,128)(2,1)} %h_ref.1) | copy-start | bytes 3932164
  11.6 2.9 %copy-start.10 = (bf16[2560,1280]{1,0:T(8,128)(2,1)S(1)}, bf16[2560,1280]{1,0:T(8,128)(2,1)}, u32[]{:S(2)}) copy-start(bf16[2560,1280]{1,0:T(8,128)(2,1)} %xw_ref.1) | copy-start | bytes 19660804
  14.5 1.3 %copy-start.11 = (bf16[2560,256]{1,0:T(8,128)(2,1)S(1)}, bf16[2560,256]{1,0:T(8,128)(2,1)}, u32[]{:S(2)}) copy-start(bf16[2560,256]{1,0:T(8,128)(2,1)} %bcw_ref.1) | copy-start | bytes 3932164
  15.8 0.9 copy-start.12
  16.7 0.7 copy-start.13
  17.4 0.7 copy-start.14
  18.1 0.7 copy-start.15
  33.3 1.5 %copy-start.18 = (bf16[512,2560]{1,0:T(8,128)(2,1)}, bf16[512,2560]{1,0:T(8,128)(2,1)S(1)}, u32[]{:S(2)}) copy-start(bf16[512,2560]{1,0:T(8,128)(2,1)S(1)} %get-tuple-element.17) | copy-start | bytes 7864324
  34.9 16.8 %copy-start.6 = (f32[512,128]{1,0:T(8,128)}, f32[512,128]{1,0:T(8,128)S(1)}, u32[]{:S(2)}) copy-start(f32[512,128]{1,0:T(8,128)S(1)} %get-tuple-element.14.cum_ref) | copy-start | bytes 786436
  34.9 23.2 %all-to-all-start = ((bf16[32,88,128]{2,1,0:T(8,128)(2,1)}), bf16[32,88,128]{2,1,0:T(8,128)(2,1)S(1)}, u32[]{:S(2)}, u32[]{:S(2)}) async-start(bf16[32,88,128]{2,1,0:T(8,128)(2,1)} %get-tuple-element.18), calls=%async_computation | async-start | bytes 1441792 | tf_op jit(solution)/shard_map/all_to_all | solution.py:433
  51.7 1.5 %copy-start.4 = (f32[512,1280]{1,0:T(8,128)}, f32[512,1280]{1,0:T(8,128)S(1)}, u32[]{:S(2)}) copy-start(f32[512,1280]{1,0:T(8,128)S(1)} %within.1.y_ref) | copy-start | bytes 7864324
  60.4 15.3 %all-to-all-start.1 = ((bf16[32,80,128]{2,1,0:T(8,128)(2,1)}), bf16[32,80,128]{2,1,0:T(8,128)(2,1)S(1)}, u32[]{:S(2)}, u32[]{:S(2)}) async-start(bf16[32,80,128]{2,1,0:T(8,128)(2,1)} %scan.1), calls=%async_computation.1 | async-start | bytes 1310720 | tf_op jit(solution)/shard_map/all_to_all | solution.py:437
  64.3 11.4 %copy-start.9 = (f32[1280]{0:T(1024)S(1)}, f32[1280]{0:T(1024)}, u32[]{:S(2)}) copy-start(f32[1280]{0:T(1024)} %param.22) | copy-start | bytes 15364
  75.7 1.7 %copy-start.5 = (f32[512,1280]{1,0:T(8,128)S(1)}, f32[512,1280]{1,0:T(8,128)}, u32[]{:S(2)}) copy-start(f32[512,1280]{1,0:T(8,128)} %copy-done.4) | copy-start | bytes 7864324
  77.5 0.9 copy-start.7
  81.7 2.9 %copy-start = (bf16[1280,2560]{1,0:T(8,128)(2,1)S(1)}, bf16[1280,2560]{1,0:T(8,128)(2,1)}, u32[]{:S(2)}) copy-start(bf16[1280,2560]{1,0:T(8,128)(2,1)} %w_ref.7) | copy-start | bytes 19660804
  86.1 7.9 %collective-permute-start.3 = (bf16[256,640]{1,0:T(8,128)(2,1)S(1)}, bf16[256,640]{1,0:T(8,128)(2,1)S(1)}, u32[]{:S(2)}, u32[]{:S(2)}) collective-permute-start(bf16[256,640]{1,0:T(8,128)(2,1)S(1)} %project.6), channel_id=1, source_target_pairs={{0,1},{1,0},{2,3},{3,2},{4,5},{5,4},{6,7},{7,6},{8,9},{9,8},{10,11... | collective-permute-start | bytes 983048 | tf_op jit(solution)/shard_map/ppermute | solution.py:444
  89.5 2.9 %copy-start.1 = (bf16[1280,2560]{1,0:T(8,128)(2,1)S(1)}, bf16[1280,2560]{1,0:T(8,128)(2,1)}, u32[]{:S(2)}) copy-start(bf16[1280,2560]{1,0:T(8,128)(2,1)} %w_ref.7) | copy-start | bytes 19660804
  93.8 8.1 %collective-permute-start.2 = (bf16[256,640]{1,0:T(8,128)(2,1)S(1)}, bf16[256,640]{1,0:T(8,128)(2,1)S(1)}, u32[]{:S(2)}, u32[]{:S(2)}) collective-permute-start(bf16[256,640]{1,0:T(8,128)(2,1)S(1)} %project.4), channel_id=1, source_target_pairs={{0,1},{1,0},{2,3},{3,2},{4,5},{5,4},{6,7},{7,6},{8,9},{9,8},{10,11... | collective-permute-start | bytes 983048 | tf_op jit(solution)/shard_map/ppermute | solution.py:448
  94.0 2.9 %copy-start.2 = (bf16[1280,2560]{1,0:T(8,128)(2,1)S(1)}, bf16[1280,2560]{1,0:T(8,128)(2,1)}, u32[]{:S(2)}) copy-start(bf16[1280,2560]{1,0:T(8,128)(2,1)} %w_ref.7) | copy-start | bytes 19660804
  98.3 10.4 %collective-permute-start.4 = (bf16[256,640]{1,0:T(8,128)(2,1)S(1)}, bf16[256,640]{1,0:T(8,128)(2,1)S(1)}, u32[]{:S(2)}, u32[]{:S(2)}) collective-permute-start(bf16[256,640]{1,0:T(8,128)(2,1)S(1)} %project.7), channel_id=1, source_target_pairs={{0,2},{2,0},{1,3},{3,1},{4,6},{6,4},{5,7},{7,5},{8,10},{10,8},{9,1... | collective-permute-start | bytes 983048 | tf_op jit(solution)/shard_map/ppermute | solution.py:446
  101.9 2.9 %copy-start.3 = (bf16[1280,2560]{1,0:T(8,128)(2,1)S(1)}, bf16[1280,2560]{1,0:T(8,128)(2,1)}, u32[]{:S(2)}) copy-start(bf16[1280,2560]{1,0:T(8,128)(2,1)} %w_ref.7) | copy-start | bytes 19660804
  (2 other events, 1.3 us)

commit v3 on v2

v3 whole, which is shorter than its diff:
```python
import functools

import jax
import jax.numpy as jnp
from jax import lax
from jax.experimental import pallas as pl
from jax.experimental.pallas import tpu as pltpu
from jax.sharding import PartitionSpec as P

HEAD_DIM = 64
STATE = 128
HALO = 16
TILE = 256
LANES = 128
epsilon = 1e-05
highest = lax.Precision.HIGHEST
f32 = jnp.float32
bf16 = jnp.bfloat16


def mm(a, b, precision=None):
    return jnp.dot(a, b, preferred_element_type=f32, precision=precision)


def iota(shape, dim):
    return lax.broadcasted_iota(jnp.int32, shape, dim)


def silu(v):
    return v * jax.nn.sigmoid(v)


def flip_matrix(n):
    return (iota((n, n), 0) + iota((n, n), 1) == n - 1).astype(bf16)


def hi_lo(v):
    hi = v.astype(bf16)
    return jnp.concatenate([hi, (v - hi.astype(f32)).astype(bf16)], axis=1)


def spread(first, width):
    rows = iota((2 * LANES, width), 0) % LANES
    return (rows == first + iota((2 * LANES, width), 1) // HEAD_DIM).astype(bf16)


def conv_pair(ext_ref, taps, rows):
    first, second = HALO - 3, HALO + rows
    fwd = bwd = None
    for k in range(4):
        tap = taps[k : k + 1]
        ahead = tap * ext_ref[first + k : first + k + rows]
        behind = tap * ext_ref[second + 3 - k : second + 3 - k + rows]
        fwd = ahead if fwd is None else fwd + ahead
        bwd = behind if bwd is None else bwd + behind
    return silu(fwd).astype(bf16), silu(bwd).astype(bf16)


def cumulate(matrix, v, lanes):
    v = jnp.where(iota(v.shape, 1) < lanes, v, 0.0)
    hi = v.astype(bf16).astype(f32)
    mid = (v - hi).astype(bf16).astype(f32)
    low = v - hi - mid
    packed = hi + pltpu.roll(mid, 32, 1) + pltpu.roll(low, 64, 1)
    out = mm(matrix, packed.astype(bf16))
    return out + pltpu.roll(out, LANES - 32, 1) + pltpu.roll(out, LANES - 64, 1)


def off_chip(x):
    return pltpu.with_memory_space_constraint(x, pltpu.HBM)


def fixed(*shape):
    return pl.BlockSpec(shape, lambda *_: (0,) * len(shape), pipeline_mode=pl.Buffered(1))


def scale_of(v):
    return lax.rsqrt(jnp.mean(v * v, axis=-1, keepdims=True) + epsilon)


def scaled(v, scale, gain_ref, first):
    parts = [
        (v[:, g * LANES : (g + 1) * LANES] * scale) * gain_ref[first + g : first + g + 1]
        for g in range(v.shape[1] // LANES)
    ]
    return jnp.concatenate(parts, axis=1).astype(bf16)


def norm_kernel(
    h_ref, gain_ref, dtw_ref, dtb_ref, lr_ref,
    x_ref, delta_ref, cum_ref, cumt_ref, wend_ref, dec_ref,
    rs_ref, dtp_ref,
):
    rows, width = h_ref.shape
    heads = dtb_ref.shape[1]

    def forward(i, _):
        at = pl.ds(pl.multiple_of(i * 32, 32), 32)
        v = h_ref[at].astype(f32)
        scale = scale_of(v)
        rs_ref[at] = jnp.broadcast_to(scale, (32, LANES))
        x_ref[at] = scaled(v, scale, gain_ref, 0)
        return 0

    lax.fori_loop(0, rows // 32, forward, 0)
    flip = flip_matrix(TILE)
    blocks = width // TILE
    scale = rs_ref[...]
    for b in range(blocks):
        mirror = blocks - 1 - b
        turned = mm(h_ref[:, mirror * TILE : (mirror + 1) * TILE], flip)
        x_ref[rows:, b * TILE : (b + 1) * TILE] = scaled(turned, scale, gain_ref, b * 2)
    dtp_ref[...] = jnp.zeros_like(dtp_ref)
    dtp_ref[0:heads] = dtw_ref[...]
    bias = jnp.concatenate([dtb_ref[...], jnp.zeros((1, LANES - heads), f32)], axis=1)
    rate = jnp.concatenate([lr_ref[...], jnp.zeros((1, LANES - heads), f32)], axis=1)
    dt = lax.dot_general(
        x_ref[...], dtp_ref[...], (((1,), (1,)), ((), ())), preferred_element_type=f32
    )
    dt = dt + bias
    delta = jnp.maximum(dt, 0.0) + jnp.log1p(jnp.exp(-jnp.abs(dt)))
    delta_ref[...] = delta
    log_decay = -delta * jnp.exp(rate)
    lower = (iota((rows, rows), 0) >= iota((rows, rows), 1)).astype(bf16)
    upper = (iota((rows, rows), 0) <= iota((rows, rows), 1)).astype(bf16)
    for d in range(2):
        at = slice(d * rows, (d + 1) * rows)
        cum = cumulate(upper if d else lower, log_decay[at], heads)
        cum_ref[at] = cum
        cumt_ref[d] = jnp.transpose(cum)[: cumt_ref.shape[1]]
        last = cum[0:1] if d else cum[rows - 1 : rows]
        wend_ref[at] = hi_lo(jnp.exp(jnp.minimum(last - cum, 0.0)) * delta[at])
        dec = jnp.where(iota((1, LANES), 1) < heads, jnp.exp(last), 0.0)
        dec_ref[d : d + 1] = dec


def norm(hidden, gain, dtw, dtb, lr):
    rows, width = hidden.shape
    heads = dtb.shape[1]
    return pl.pallas_call(
        norm_kernel,
        grid=(1,),
        in_specs=[
            fixed(rows, width), fixed(width // LANES, LANES), fixed(heads, width),
            fixed(1, heads), fixed(1, heads),
        ],
        out_specs=[
            fixed(2 * rows, width), fixed(2 * rows, LANES), fixed(2 * rows, LANES),
            fixed(2, 24, rows), fixed(2 * rows, 2 * LANES), fixed(8, LANES),
        ],
        out_shape=[
            jax.ShapeDtypeStruct((2 * rows, width), bf16),
            jax.ShapeDtypeStruct((2 * rows, LANES), f32),
            jax.ShapeDtypeStruct((2 * rows, LANES), f32),
            jax.ShapeDtypeStruct((2, 24, rows), f32),
            jax.ShapeDtypeStruct((2 * rows, 2 * LANES), bf16),
            jax.ShapeDtypeStruct((8, LANES), f32),
        ],
        scratch_shapes=[pltpu.VMEM((rows, LANES), f32), pltpu.VMEM((LANES, width), bf16)],
        compiler_params=pltpu.CompilerParams(vmem_limit_bytes=16 << 20),
        cost_estimate=pl.CostEstimate(flops=4 << 30, bytes_accessed=5 << 20, transcendentals=0),
        name="norm",
    )(off_chip(hidden), off_chip(gain), off_chip(dtw), off_chip(dtb), off_chip(lr))


def entry_kernel(
    x_ref, prev_ref, next_ref, gain_ref, xw_ref, bcw_ref, xk_ref, bck_ref, wend_ref, dec_ref,
    xconv_ref, bc_ref, pay_ref,
    ext_ref, xin_ref, bcin_ref, st_ref, bt_ref,
):
    width = x_ref.shape[1]
    rows = x_ref.shape[0] // 2
    n = pl.program_id(0)
    steps = pl.num_programs(0) - 1

    def prelude():
        ext_ref[HALO : HALO + 2 * rows] = x_ref[...]
        prev = prev_ref[...].astype(f32)
        ext_ref[0:HALO] = scaled(prev, scale_of(prev), gain_ref, 0)
        flip = flip_matrix(TILE)
        blocks = width // TILE
        after = next_ref[...]
        after_scale = scale_of(after.astype(f32))
        stacked = jnp.concatenate([after[:, b * TILE : (b + 1) * TILE] for b in range(blocks)], axis=0)
        stacked = mm(stacked, flip)
        for b in range(blocks):
            mirror = blocks - 1 - b
            ext_ref[HALO + 2 * rows :, b * TILE : (b + 1) * TILE] = scaled(
                stacked[mirror * HALO : (mirror + 1) * HALO], after_scale, gain_ref, b * 2
            )
        bcin_ref[...] = mm(ext_ref[...], bcw_ref[...]).astype(bf16).astype(f32)
        bc_pair = conv_pair(bcin_ref, bck_ref[...], rows)
        for d in range(2):
            at = slice(d * rows, (d + 1) * rows)
            bc_ref[at] = bc_pair[d]
            bt_ref[d] = jnp.transpose(bc_pair[d][:, :STATE].astype(f32)).astype(bf16)

    def product():
        return mm(ext_ref[...], xw_ref[...]).astype(bf16).astype(f32)

    def finish():
        tile = n - 1
        pair = conv_pair(xin_ref, xk_ref[...], rows)
        spread_n = spread(tile * (TILE // HEAD_DIM), TILE)
        for d in range(2):
            at = slice(d * rows, (d + 1) * rows)
            xconv_ref[at] = pair[d]
            weighted = (pair[d].astype(f32) * mm(wend_ref[at], spread_n)).astype(bf16)
            column = pl.multiple_of(d * steps * TILE + tile * TILE, TILE)
            st_ref[:, pl.ds(column, TILE)] = mm(bt_ref[d], weighted).astype(bf16)

    @pl.when(n == 0)
    def _():
        prelude()
        xin_ref[...] = product()

    @pl.when((n > 0) & (n < steps))
    def _():
        finish()
        xin_ref[...] = product()

    @pl.when(n == steps)
    def _():
        finish()
        slots = pay_ref.shape[0]
        row = iota((8, LANES), 0)
        tails = []
        for d in range(2):
            dec = jnp.broadcast_to(dec_ref[d : d + 1], (8, LANES))
            hi = dec.astype(bf16).astype(f32)
            tails.append(jnp.where(row == 0, hi, jnp.where(row == 1, dec - hi, 0.0)).astype(bf16))
        for slot in range(slots):
            i, q = slot // 4, slot % 4
            for j in range(5):
                column = (5 * q + j) * LANES
                pay_ref[slot, 16 * j : 16 * j + 16] = st_ref[16 * i : 16 * i + 16, column : column + LANES]
            pay_ref[slot, 80:88] = tails[q // 2]


def entry(x, prev_rows, next_rows, gain, xw, bcw, xk, bck, wend, dec, slots):
    width = x.shape[1]
    rows = x.shape[0] // 2
    inner = xw.shape[1]
    steps = inner // TILE
    ahead = lambda n: jnp.minimum(n, steps - 1)
    behind = lambda n: jnp.maximum(n - 1, 0)
    whole = lambda *shape: pl.BlockSpec(shape, lambda n: (0,) * len(shape))
    once = lambda *shape: pl.BlockSpec(
        shape, lambda n: (0,) * len(shape), pipeline_mode=pl.Buffered(1)
    )
    vmem = pl.BlockSpec(memory_space=pltpu.VMEM)
    return pl.pallas_call(
        entry_kernel,
        grid=(steps + 1,),
        in_specs=[
            vmem, vmem, vmem, once(width // LANES, LANES),
            pl.BlockSpec((width, TILE), lambda n: (0, ahead(n))),
            once(width, 2 * STATE),
            pl.BlockSpec((4, TILE), lambda n: (0, behind(n))),
            once(4, 2 * STATE), vmem, vmem,
        ],
        out_specs=[
            pl.BlockSpec((2 * rows, TILE), lambda n: (0, behind(n))),
            whole(2 * rows, 2 * STATE), whole(slots, 88, LANES),
        ],
        out_shape=[
            pltpu.HBM((2 * rows, inner), bf16),
            pltpu.HBM((2 * rows, 2 * STATE), bf16),
            pltpu.HBM((slots, 88, LANES), bf16),
        ],
        scratch_shapes=[
            pltpu.VMEM((2 * rows + 2 * HALO, width), bf16),
            pltpu.VMEM((2 * rows + 2 * HALO, TILE), f32),
            pltpu.VMEM((2 * rows + 2 * HALO, TILE), f32),
            pltpu.VMEM((STATE, 2 * inner), bf16),
            pltpu.VMEM((2, STATE, rows), bf16),
        ],
        compiler_params=pltpu.CompilerParams(
            dimension_semantics=("arbitrary",), vmem_limit_bytes=26 << 20
        ),
        cost_estimate=pl.CostEstimate(
            flops=2 * 544 * width * (inner + 256), bytes_accessed=12 << 20, transcendentals=0
        ),
        name="entry",
    )(x, prev_rows, next_rows, off_chip(gain), off_chip(xw), off_chip(bcw), off_chip(xk), off_chip(bck), wend, dec)


def open_gate_kernel(x_ref, zw_ref, z_ref):
    z = mm(x_ref[...], zw_ref[...]).astype(bf16).astype(f32)
    z_ref[...] = silu(z).astype(bf16)


def open_gate(x, zw):
    height, width = x.shape
    inner = zw.shape[1]
    return pl.pallas_call(
        open_gate_kernel,
        grid=(inner // TILE,),
        in_specs=[fixed(height, width), pl.BlockSpec((width, TILE), lambda n: (0, n))],
        out_specs=pl.BlockSpec((height, TILE), lambda n: (0, n)),
        out_shape=jax.ShapeDtypeStruct((height, inner), bf16),
        compiler_params=pltpu.CompilerParams(
            dimension_semantics=("arbitrary",), vmem_limit_bytes=16 << 20
        ),
        cost_estimate=pl.CostEstimate(
            flops=2 * height * width * inner, bytes_accessed=16 << 20, transcendentals=0
        ),
        name="open_gate",
    )(off_chip(x), off_chip(zw))


def within_kernel(x_ref, bc_ref, cum_ref, cumt_ref, delta_ref, y_ref, gram_ref):
    d, n = pl.program_id(0), pl.program_id(1)
    rows = x_ref.shape[0]
    heads = TILE // HEAD_DIM

    @pl.when(n == 0)
    def _():
        gram = lax.dot_general(
            bc_ref[:, STATE:], bc_ref[:, :STATE], (((1,), (1,)), ((), ())), preferred_element_type=f32
        )
        t, s = iota((rows, rows), 0), iota((rows, rows), 1)
        seen = jnp.where(d == 0, t - s, s - t) >= 0
        gram_ref[...] = jnp.where(seen, gram, 0.0)

    weighted = x_ref[...].astype(f32) * mm(hi_lo(delta_ref[...]), spread(n * heads, TILE))
    cum = pltpu.roll(cum_ref[...], (LANES - n * heads) % LANES, 1)
    owner = iota((rows, TILE), 1) // HEAD_DIM
    total = jnp.zeros((rows, TILE), f32)
    for k in range(heads):
        behind = cumt_ref[0, pl.ds(n * heads + k, 1), :]
        decay = jnp.exp(jnp.minimum(cum[:, k : k + 1] - behind, 0.0)) * gram_ref[...]
        total = total + mm(decay.astype(bf16), jnp.where(owner == k, weighted, 0.0).astype(bf16))
    y_ref[...] = total


def within(xconv, bc, cum, cumt, delta):
    rows = xconv.shape[0] // 2
    inner = xconv.shape[1]
    return pl.pallas_call(
        within_kernel,
        grid=(2, inner // TILE),
        in_specs=[
            pl.BlockSpec((rows, TILE), lambda d, n: (d, n)),
            pl.BlockSpec((rows, 2 * STATE), lambda d, n: (d, 0)),
            pl.BlockSpec((rows, LANES), lambda d, n: (d, 0)),
            pl.BlockSpec((1, 24, rows), lambda d, n: (d, 0, 0)),
            pl.BlockSpec((rows, LANES), lambda d, n: (d, 0)),
        ],
        out_specs=pl.BlockSpec((rows, TILE), lambda d, n: (d, n)),
        out_shape=pltpu.HBM((2 * rows, inner), f32),
        scratch_shapes=[pltpu.VMEM((rows, rows), f32)],
        compiler_params=pltpu.CompilerParams(
            dimension_semantics=("arbitrary", "arbitrary"), vmem_limit_bytes=12 << 20
        ),
        cost_estimate=pl.CostEstimate(flops=3 << 30, bytes_accessed=5 << 20, transcendentals=3 << 20),
        name="within",
    )(off_chip(xconv), off_chip(bc), cum, cumt, delta)


def scan_kernel(q_ref, pay_ref, out_ref, carry_ref):
    q = q_ref[0]
    half, turned = q % 2, q // 2
    depth = pay_ref.shape[0]

    @pl.when(pl.program_id(0) == 0)
    def _():
        carry_ref[...] = jnp.zeros_like(carry_ref)

    first = half * (5 * LANES // HEAD_DIM)
    place = iota((LANES, 5 * LANES), 0) == first + iota((LANES, 5 * LANES), 1) // HEAD_DIM
    place = place.astype(bf16)
    carry = [carry_ref[16 * j : 16 * j + 16] for j in range(5)]
    for i in range(depth):
        at = jnp.where(turned == 1, depth - 1 - i, i)
        decays = mm(pay_ref[at, 80:88], place)
        decay = decays[0:1] + decays[1:2]
        for j in range(5):
            rows = slice(16 * j, 16 * j + 16)
            out_ref[at, rows] = carry[j].astype(bf16)
            carry[j] = carry[j] * decay[:, j * LANES : (j + 1) * LANES] + pay_ref[at, rows].astype(f32)
    for j in range(5):
        carry_ref[16 * j : 16 * j + 16] = carry[j]


def scan(q, pay):
    slots = pay.shape[0]
    depth = 8
    steps = slots // depth
    chunk = lambda i, q: (jnp.where(q[0] // 2 == 1, steps - 1 - i, i), 0, 0)
    return pl.pallas_call(
        scan_kernel,
        grid_spec=pltpu.PrefetchScalarGridSpec(
            num_scalar_prefetch=1,
            grid=(steps,),
            in_specs=[pl.BlockSpec((depth, 88, LANES), chunk)],
            out_specs=pl.BlockSpec((depth, 80, LANES), chunk),
            scratch_shapes=[pltpu.VMEM((80, LANES), f32)],
        ),
        out_shape=jax.ShapeDtypeStruct((slots, 80, LANES), bf16),
        compiler_params=pltpu.CompilerParams(
            dimension_semantics=("arbitrary",), vmem_limit_bytes=6 << 20
        ),
        name="scan",
    )(q, pay)


def weight_fetches(q, w_ref, near_ref, far_ref, sems):
    chunks, depth, lanes = near_ref.shape
    near = pl.ds(pl.multiple_of(q * lanes, LANES), lanes)
    far = pl.ds(pl.multiple_of((3 - q) * lanes, LANES), lanes)
    copies = []
    for k in range(chunks):
        rows = slice(k * depth, (k + 1) * depth)
        copies.append(
            (
                pltpu.make_async_copy(w_ref.at[rows, near], near_ref.at[k], sems.at[0, k]),
                pltpu.make_async_copy(w_ref.at[rows, far], far_ref.at[k], sems.at[1, k]),
            )
        )
    return copies


def project_into(out_ref, g_ref, copies, near_ref, far_ref, adds):
    chunks, depth, lanes = near_ref.shape
    ahead = behind = None
    for k in range(chunks):
        for copy in copies[k]:
            copy.wait()
        one = mm(g_ref[:, k * depth : (k + 1) * depth], near_ref[k])
        two = mm(g_ref[:, (chunks + k) * depth : (chunks + k + 1) * depth], far_ref[k])
        ahead = one if ahead is None else ahead + one
        behind = two if behind is None else behind + two
    flip = flip_matrix(LANES)
    flip = jnp.concatenate([flip, flip], axis=0)
    blocks = lanes // LANES
    for b in range(blocks):
        at = slice(b * LANES, (b + 1) * LANES)
        source = slice((blocks - 1 - b) * LANES, (blocks - b) * LANES)
        total = ahead[:, at] + mm(hi_lo(behind[:, source]), flip)
        for add in adds:
            total = total + add[:, at].astype(f32)
        out_ref[:, at] = total.astype(out_ref.dtype)


def weight_scratch(inner, lanes):
    chunks = inner // TILE
    return [
        pltpu.VMEM((chunks, TILE, lanes), bf16),
        pltpu.VMEM((chunks, TILE, lanes), bf16),
        pltpu.SemaphoreType.DMA((2, chunks)),
    ]


def gate_kernel(
    target_ref, y_ref, z_ref, bc_ref, cum_ref, st_ref, gain_ref, w_ref,
    g_ref, out_ref,
    near_ref, far_ref, sems,
):
    q = pl.program_id(0)
    rows, lanes = y_ref.shape
    groups = lanes // LANES
    copies = weight_fetches(target_ref[0], w_ref, near_ref, far_ref, sems)

    @pl.when(q == 0)
    def _():
        for pair in copies:
            for copy in pair:
                copy.start()

    state = jnp.concatenate([st_ref[:, 0, j].reshape(STATE, LANES) for j in range(groups)], axis=1)
    carried = mm(bc_ref[:, STATE:], state)
    reach = mm(hi_lo(jnp.exp(cum_ref[...])), spread((q % 2) * (lanes // HEAD_DIM), lanes))
    same = (iota((2 * LANES, LANES), 0) % LANES) // HEAD_DIM == iota((2 * LANES, LANES), 1) // HEAD_DIM
    same = same.astype(bf16)
    for b in range(groups):
        at = slice(b * LANES, (b + 1) * LANES)
        y = y_ref[:, at] + carried[:, at] * reach[:, at]
        part = y * z_ref[:, at].astype(f32)
        mean_sq = mm(hi_lo(part * part), same) * (1.0 / HEAD_DIM)
        gain = gain_ref[pl.ds((q % 2) * groups + b, 1), :]
        column = pl.multiple_of((q * groups + b) * LANES, LANES)
        g_ref[:, pl.ds(column, LANES)] = (part * lax.rsqrt(mean_sq + epsilon) * gain).astype(bf16)

    @pl.when(q == pl.num_programs(0) - 1)
    def _():
        project_into(out_ref, g_ref, copies, near_ref, far_ref, ())


def gate(target, y, z, bc, cum, state, gain, weight):
    rows = y.shape[0] // 2
    inner = y.shape[1]
    lanes = inner // 2
    groups = lanes // LANES
    columns = weight.shape[1] // 4
    return pl.pallas_call(
        gate_kernel,
        grid_spec=pltpu.PrefetchScalarGridSpec(
            num_scalar_prefetch=1,
            grid=(4,),
            in_specs=[
                pl.BlockSpec((rows, lanes), lambda q, t: (q // 2, q % 2)),
                pl.BlockSpec((rows, lanes), lambda q, t: (q // 2, q % 2)),
                pl.BlockSpec((rows, 2 * STATE), lambda q, t: (q // 2, 0)),
                pl.BlockSpec((rows, LANES), lambda q, t: (q // 2, 0)),
                pl.BlockSpec((8, 1, groups, 16, LANES), lambda q, t: (0, q, 0, 0, 0)),
                fixed(2 * groups, LANES),
                pl.BlockSpec(memory_space=pltpu.HBM),
            ],
            out_specs=[fixed(rows, 2 * inner), fixed(rows, columns)],
            scratch_shapes=weight_scratch(inner, columns),
        ),
        out_shape=[
            jax.ShapeDtypeStruct((rows, 2 * inner), bf16),
            jax.ShapeDtypeStruct((rows, columns), bf16),
        ],
        compiler_params=pltpu.CompilerParams(
            dimension_semantics=("arbitrary",), vmem_limit_bytes=20 << 20
        ),
        name="gate",
    )(target, off_chip(y), z, off_chip(bc), cum, state.reshape(8, 4, groups, 16, LANES), off_chip(gain), off_chip(weight))


def project_kernel(has_add, q_ref, g_ref, w_ref, *rest):
    adds, (out_ref, near_ref, far_ref, sems) = rest[:has_add], rest[has_add:]
    copies = weight_fetches(q_ref[0], w_ref, near_ref, far_ref, sems)
    for pair in copies:
        for copy in pair:
            copy.start()
    project_into(out_ref, g_ref, copies, near_ref, far_ref, adds)


def project(q, gated, weight, dtype, *adds):
    rows = gated.shape[0]
    inner, width = weight.shape
    lanes = width // 4
    vmem = pl.BlockSpec(memory_space=pltpu.VMEM)
    return pl.pallas_call(
        functools.partial(project_kernel, len(adds)),
        in_specs=[pl.BlockSpec(memory_space=pltpu.SMEM), vmem, pl.BlockSpec(memory_space=pltpu.HBM)]
        + [vmem for _ in adds],
        out_specs=vmem,
        out_shape=jax.ShapeDtypeStruct((rows, lanes), dtype),
        scratch_shapes=weight_scratch(inner, lanes),
        compiler_params=pltpu.CompilerParams(vmem_limit_bytes=16 << 20),
        cost_estimate=pl.CostEstimate(
            flops=4 * rows * inner * lanes, bytes_accessed=5 << 20, transcendentals=0
        ),
        name="project",
    )(q, gated, off_chip(weight), *adds)


def per_device(
    hidden, norm_gain, x_weight, z_weight, bc_weight, dt_weight, x_kernel, bc_kernel,
    dt_bias, log_rate, out_gain, out_weight,
):
    blocks = lax.axis_size("ctx")
    place = lax.axis_index("ctx")
    head = lax.axis_index("head")
    prev_rows = lax.ppermute(hidden[-HALO:], "ctx", [(i, i + 1) for i in range(blocks - 1)])
    next_rows = lax.ppermute(hidden[:HALO], "ctx", [(i + 1, i) for i in range(blocks - 1)])
    gain = norm_gain.reshape(-1, LANES)
    normed, delta, cum, cumt, wend, dec = norm(hidden, gain, dt_weight.T, dt_bias[None], log_rate[None])
    xconv, bc, pay = entry(
        normed, prev_rows, next_rows, gain, x_weight, bc_weight, x_kernel, bc_kernel, wend, dec, blocks
    )
    pay = lax.all_to_all(pay, "ctx", 0, 0, tiled=True)
    y = within(xconv, bc, cum, cumt, delta)
    pay, y = lax.optimization_barrier((pay, y))
    state = scan((place % 4)[None], pay)
    state = lax.all_to_all(state, "ctx", 0, 0, tiled=True)
    open_z = open_gate(normed, z_weight)
    core, far = head % 2, head // 2
    quarter = lambda f, c: (2 * f + c)[None]
    core_swap = [(0, 1), (1, 0), (2, 3), (3, 2)]
    far_swap = [(0, 2), (2, 0), (1, 3), (3, 1)]
    gated, first = gate(
        quarter(1 - far, 1 - core), y, open_z, bc, cum, state, out_gain.reshape(-1, LANES), out_weight
    )
    first = lax.ppermute(first, "head", core_swap)
    second = project(quarter(1 - far, core), gated, out_weight, bf16, first)
    second, gated = lax.optimization_barrier((second, gated))
    second = lax.ppermute(second, "head", far_swap)
    third = project(quarter(far, 1 - core), gated, out_weight, bf16)
    third = lax.ppermute(third, "head", core_swap)
    lanes = hidden.shape[1] // 4
    residual = lax.dynamic_slice_in_dim(hidden, head * lanes, lanes, 1)
    own = project(quarter(far, core), gated, out_weight, f32, third, residual)
    return (own + second.astype(f32)).astype(bf16)


def solution(mesh):
    return jax.shard_map(
        per_device,
        mesh=mesh,
        in_specs=(
            P("ctx", None), P(), P(None, "head"), P(None, "head"), P(), P(None, "head"),
            P(None, "head"), P(), P("head"), P("head"), P("head"), P("head", None),
        ),
        out_specs=P("ctx", "head"),
        check_vma=False,
    )
```

time: 110 us -> 100 us (0.909)
  local copies, waits for them, and re-layouts: 28.9 us -> 1.94 us
  Pallas kernels: 31 us -> 55.2 us
  matrix products: 7.2 us -> 0 us
  waiting for transfers between devices: 15.6 us -> 12.7 us
  starting transfers between devices: 25.8 us -> 28.6 us
    unnamed x38 -> x2, local copies, waits for them, and re-layouts: 27 us -> 0.01 us
    pallas_call x2 -> x4, Pallas kernels: 16.5 us -> 33.1 us  [the longest x1 13.3 us: entry(): pl.pallas_call(entry_kernel, grid=(steps + 1,), in_specs=[vmem, vmem, vme...]
    dot_general x1 -> x0, matrix products: 7.2 us -> none  [per_device(): z_in = jnp.dot(normed, z_weight, preferred_element_type=f32).astype(bf16)]
    pallas_call x4 -> x3, Pallas kernels: 6 us -> 10.1 us  [project(): pl.pallas_call(functools.partial(project_kernel, len(adds)), in_specs=[pl...]
    ppermute x1, waiting for transfers between devices: 3.96 us -> 0.01 us  [per_device(): lax.ppermute(hidden[:HALO], 'ctx', [(i + 1, i) for i in range(blocks - 1)])]
    pallas_call x1, Pallas kernels: 6.18 us -> 9.59 us  [within(): pl.pallas_call(within_kernel, grid=(2, inner // TILE), in_specs=[pl.Block...]
    all_to_all x1, waiting for transfers between devices: 4.85 us -> 3.12 us  [per_device(): pay = lax.all_to_all(pay, 'ctx', 0, 0, tiled=True)]
    all_to_all x1, starting transfers between devices: 10.6 us -> 12.2 us  [per_device(): pay = lax.all_to_all(pay, 'ctx', 0, 0, tiled=True)]
  transfers between devices with their start and end apart: 7 -> 7, of which waited for: 5 -> 4; matrix products, arithmetic and copies ran while one was open for 7% -> 1% of each run, Pallas kernels for 10% -> 25%
where the time goes in v3:
time: 100 us; the launch traced here: 99.4 us
  Pallas kernels  55.2 us (55%)
  starting transfers between devices  28.6 us (29%)
  waiting for transfers between devices  12.7 us (13%)
  local copies, waits for them, and re-layouts  1.94 us (2%)
    pallas_call x1, Pallas kernels, entry(): pl.pallas_call(entry_kernel, grid=(steps + 1,), in_specs=[vmem, vmem, vme...  13.3 us
    all_to_all x1, starting transfers between devices, per_device(): pay = lax.all_to_all(pay, 'ctx', 0, 0, tiled=True)  12.2 us
    pallas_call x3, Pallas kernels, project(): pl.pallas_call(functools.partial(project_kernel, len(adds)), in_specs=[pl...  10.1 us
    pallas_call x1, Pallas kernels, within(): pl.pallas_call(within_kernel, grid=(2, inner // TILE), in_specs=[pl.Block...  9.59 us
    pallas_call x1, Pallas kernels, gate(): pl.pallas_call(gate_kernel, grid_spec=pltpu.PrefetchScalarGridSpec(num_sc...  8.06 us
    pallas_call x1, Pallas kernels, open_gate(): pl.pallas_call(open_gate_kernel, grid=(inner // TILE,), in_specs=[fixed(h...  7.45 us
    all_to_all x1, starting transfers between devices, per_device(): state = lax.all_to_all(state, 'ctx', 0, 0, tiled=True)  4.61 us
    ppermute x1, starting transfers between devices, per_device(): lax.ppermute(hidden[-HALO:], 'ctx', [(i, i + 1) for i in range(blocks - 1)])  4.57 us
  transfers between devices with their start and end apart: 7, of which 4 were waited for; matrix products, arithmetic and copies ran while one was open for 1% of the time, Pallas kernels for 25%

profile of v3, /device:TPU:1, one launch (start us, length us, event | category | flops | bytes accessed | tf_op | source)
XLA Modules:
  0.0 99.4 jit_solution(6113606056456677603)
XLA Ops:
  0.0 0.9 fusion
  0.9 1.3 %collective-permute-start.1 = (bf16[16,2560]{1,0:T(8,128)(2,1)S(1)}, bf16[16,2560]{1,0:T(8,128)(2,1)S(1)}, u32[]{:S(2)}, u32[]{:S(2)}) collective-permute-start(bf16[16,2560]{1,0:T(8,128)(2,1)S(1)} %get-tuple-element.35), channel_id=1, source_target_pairs={{4,0},{8,4},{12,8},{16,12},{20,16},{24,20},{28,24},{32,28},{36,32}... | collective-permute-start | bytes 245768 | tf_op jit(solution)/shard_map/ppermute | solution.py:561
  2.2 4.6 %collective-permute-start = (bf16[16,2560]{1,0:T(8,128)(2,1)S(1)}, bf16[16,2560]{1,0:T(8,128)(2,1)S(1)}, u32[]{:S(2)}, u32[]{:S(2)}) collective-permute-start(bf16[16,2560]{1,0:T(8,128)(2,1)S(1)} %get-tuple-element.36), channel_id=1, source_target_pairs={{0,4},{4,8},{8,12},{12,16},{16,20},{20,24},{24,28},{28,32},{32,36}... | collective-permute-start | bytes 245768 | tf_op jit(solution)/shard_map/ppermute | solution.py:560
  6.8 4.3 %norm.1 = (bf16[512,2560]{1,0:T(8,128)(2,1)S(1)}, f32[512,128]{1,0:T(8,128)S(1)}, f32[512,128]{1,0:T(8,128)S(1)}, f32[2,24,256]{2,1,0:T(8,128)S(1)}, bf16[512,256]{1,0:T(8,128)(2,1)S(1)}, /*index=5*/f32[8,128]{1,0:T(8,128)S(1)}) custom-call(bf16[256,2560]{1,0:T(8,128)(2,1)} %h_ref.1, f32[20,128]{1,0:T(8,128)} %bitcast.14, bf16[20,2560]{1,0:T(8,128)(2,1)} %bitcast.13, ...), custom_call_target="tpu_custom_call" | custom-call | flops 4294967296 | bytes 5242880 | tf_op jit(solution)/shard_map/norm/pallas_call | solution.py:140
  11.1 0.0 collective-permute-done.1.next_ref
  11.1 13.3 %entry.1 = (bf16[512,1280]{1,0:T(8,128)(2,1)}, bf16[512,256]{1,0:T(8,128)(2,1)}, bf16[32,88,128]{2,1,0:T(8,128)(2,1)}) custom-call(bf16[512,2560]{1,0:T(8,128)(2,1)S(1)} %get-tuple-element.20.x_ref, bf16[16,2560]{1,0:T(8,128)(2,1)S(1)} %collective-permute-done.prev_ref, bf16[16,2560]{1,0:T(8,128)(2,1)S(1)} %collective-permute-done.1.next_ref, ...), custom_call_target="tpu_custom_call" | custom-call | flops 4278190080 | bytes 12582912 | tf_op jit(solution)/shard_map/entry/pallas_call | solution.py:252
  24.4 12.2 %all-to-all-start = ((bf16[32,88,128]{2,1,0:T(8,128)(2,1)}), bf16[32,88,128]{2,1,0:T(8,128)(2,1)S(1)}, u32[]{:S(2)}, u32[]{:S(2)}) async-start(bf16[32,88,128]{2,1,0:T(8,128)(2,1)} %get-tuple-element.23), calls=%async_computation | async-start | bytes 1441792 | tf_op jit(solution)/shard_map/all_to_all | solution.py:567
  36.7 9.6 %within.1.y_ref = f32[512,1280]{1,0:T(8,128)} custom-call(bf16[512,1280]{1,0:T(8,128)(2,1)} %get-tuple-element.24.x_ref, bf16[512,256]{1,0:T(8,128)(2,1)} %get-tuple-element.25.bc_ref, f32[512,128]{1,0:T(8,128)S(1)} %get-tuple-element.26.cum_ref, f32[2,24,256]{2,1,0:T(8,128)S(1)} %get-tuple-element.27.cumt_ref, f32[512,128]{1,0:T(8,128)S(1)} %get-tuple-element.28.delta_ref), custom_call_target="tpu_custom_call" | custom-call | flops 3221225472 | bytes 5242880 | tf_op jit(solution)/shard_map/within/pallas_call | solution.py:340
  46.3 3.1 %all-to-all-done.pay_ref = bf16[32,88,128]{2,1,0:T(8,128)(2,1)S(1)} async-done(((bf16[32,88,128]{2,1,0:T(8,128)(2,1)}), bf16[32,88,128]{2,1,0:T(8,128)(2,1)S(1)}, u32[]{:S(2)}, u32[]{:S(2)}) %all-to-all-start) | async-done | bytes 720928 | tf_op jit(solution)/shard_map/all_to_all | solution.py:567
  49.4 2.3 %scan.1 = bf16[32,80,128]{2,1,0:T(8,128)(2,1)} custom-call(s32[1]{0:T(128)} %bitcast.7.q_ref, bf16[32,88,128]{2,1,0:T(8,128)(2,1)S(1)} %all-to-all-done.pay_ref), custom_call_target="tpu_custom_call" | custom-call | tf_op jit(solution)/shard_map/scan/pallas_call | solution.py:391
  51.7 4.6 %all-to-all-start.1 = ((bf16[32,80,128]{2,1,0:T(8,128)(2,1)}), bf16[32,80,128]{2,1,0:T(8,128)(2,1)S(1)}, u32[]{:S(2)}, u32[]{:S(2)}) async-start(bf16[32,80,128]{2,1,0:T(8,128)(2,1)} %scan.1), calls=%async_computation.1 | async-start | bytes 1310720 | tf_op jit(solution)/shard_map/all_to_all | solution.py:571
  56.4 7.5 %open_gate.1.z_ref = bf16[512,1280]{1,0:T(8,128)(2,1)S(1)} custom-call(bf16[512,2560]{1,0:T(8,128)(2,1)} %copy-done, bf16[2560,1280]{1,0:T(8,128)(2,1)} %zw_ref.1), custom_call_target="tpu_custom_call" | custom-call | flops 3355443200 | bytes 16777216 | tf_op jit(solution)/shard_map/open_gate/pallas_call | solution.py:296
  63.8 4.3 %all-to-all-done.1 = bf16[32,80,128]{2,1,0:T(8,128)(2,1)S(1)} async-done(((bf16[32,80,128]{2,1,0:T(8,128)(2,1)}), bf16[32,80,128]{2,1,0:T(8,128)(2,1)S(1)}, u32[]{:S(2)}, u32[]{:S(2)}) %all-to-all-start.1) | async-done | bytes 655392 | tf_op jit(solution)/shard_map/all_to_all | solution.py:571
  68.2 8.1 %gate.1 = (bf16[256,2560]{1,0:T(8,128)(2,1)S(1)}, bf16[256,640]{1,0:T(8,128)(2,1)}) custom-call(s32[1]{0:T(128)} %bitcast.2.target_ref, f32[512,1280]{1,0:T(8,128)} %within.1.y_ref, bf16[512,1280]{1,0:T(8,128)(2,1)S(1)} %open_gate.1.z_ref, bf16[512,256]{1,0:T(8,128)(2,1)} %get-tuple-element.25.bc_ref, f32[512,128]{1,0:T(8,128)S(1)} %get-tuple-element.26.cum_ref, ...), custom_call_target="tpu_custom_call" | custom-call | tf_op jit(solution)/shard_map/gate/pallas_call | solution.py:496
  76.2 3.0 %collective-permute-start.2 = (bf16[256,640]{1,0:T(8,128)(2,1)}, bf16[256,640]{1,0:T(8,128)(2,1)S(1)}, u32[]{:S(2)}, u32[]{:S(2)}) collective-permute-start(bf16[256,640]{1,0:T(8,128)(2,1)} %get-tuple-element.32), channel_id=1, source_target_pairs={{0,1},{1,0},{2,3},{3,2},{4,5},{5,4},{6,7},{7,6},{8,9},{9,8},{10,11... | collective-permute-start | bytes 983048 | tf_op jit(solution)/shard_map/ppermute | solution.py:580
  79.3 1.5 %collective-permute-done.2.rest_0_ = bf16[256,640]{1,0:T(8,128)(2,1)S(1)} collective-permute-done((bf16[256,640]{1,0:T(8,128)(2,1)}, bf16[256,640]{1,0:T(8,128)(2,1)S(1)}, u32[]{:S(2)}, u32[]{:S(2)}) %collective-permute-start.2) | collective-permute-done | bytes 327712 | tf_op jit(solution)/shard_map/ppermute | solution.py:580
  80.7 3.4 %project.3 = bf16[256,640]{1,0:T(8,128)(2,1)S(1)} custom-call(s32[1]{0:T(128)} %bitcast.1.q_ref, bf16[256,2560]{1,0:T(8,128)(2,1)S(1)} %get-tuple-element.33.g_ref, bf16[1280,2560]{1,0:T(8,128)(2,1)} %w_ref.7, bf16[256,640]{1,0:T(8,128)(2,1)S(1)} %collective-permute-done.2.rest_0_), custom_call_target="tpu_custom_call" | custom-call | flops 838860800 | bytes 5242880 | tf_op jit(solution)/shard_map/project/pallas_call | solution.py:538
  84.1 3.4 %project.4 = bf16[256,640]{1,0:T(8,128)(2,1)S(1)} custom-call(s32[1]{0:T(128)} %bitcast.10.q_ref, bf16[256,2560]{1,0:T(8,128)(2,1)S(1)} %get-tuple-element.33.g_ref, bf16[1280,2560]{1,0:T(8,128)(2,1)} %w_ref.7), custom_call_target="tpu_custom_call" | custom-call | flops 838860800 | bytes 5242880 | tf_op jit(solution)/shard_map/project/pallas_call | solution.py:538
  87.5 0.5 collective-permute-start.3
  88.0 2.5 %collective-permute-start.4 = (bf16[256,640]{1,0:T(8,128)(2,1)S(1)}, bf16[256,640]{1,0:T(8,128)(2,1)S(1)}, u32[]{:S(2)}, u32[]{:S(2)}) collective-permute-start(bf16[256,640]{1,0:T(8,128)(2,1)S(1)} %project.3), channel_id=1, source_target_pairs={{0,2},{2,0},{1,3},{3,1},{4,6},{6,4},{5,7},{7,5},{8,10},{10,8},{9,1... | collective-permute-start | bytes 983048 | tf_op jit(solution)/shard_map/ppermute | solution.py:583
  90.4 1.0 %constant_dynamic-slice_fusion.rest_1_ = bf16[256,640]{1,0:T(8,128)(2,1)S(1)} fusion(bf16[256,2560]{1,0:T(8,128)(2,1)} %h_ref.1, s32[]{:T(128)S(6)} %select_n.21), kind=kLoop, calls=%fused_computation.1 | loop fusion | bytes 655364 | tf_op jit(solution)/shard_map/dynamic_slice | solution.py:587
  91.4 3.4 %project.5 = f32[256,640]{1,0:T(8,128)S(1)} custom-call(s32[1]{0:T(128)} %bitcast.q_ref, bf16[256,2560]{1,0:T(8,128)(2,1)S(1)} %get-tuple-element.33.g_ref, bf16[1280,2560]{1,0:T(8,128)(2,1)} %w_ref.7, bf16[256,640]{1,0:T(8,128)(2,1)S(1)} %collective-permute-done.3.rest_0_, bf16[256,640]{1,0:T(8,128)(2,1)S(1)} %constant_dynamic-slice_fusion.rest_1_), custom_call_target="tpu_custom_call" | custom-call | flops 838860800 | bytes 5242880 | tf_op jit(solution)/shard_map/project/pallas_call | solution.py:538
  94.8 3.8 %collective-permute-done.4 = bf16[256,640]{1,0:T(8,128)(2,1)S(1)} collective-permute-done((bf16[256,640]{1,0:T(8,128)(2,1)S(1)}, bf16[256,640]{1,0:T(8,128)(2,1)S(1)}, u32[]{:S(2)}, u32[]{:S(2)}) %collective-permute-start.4) | collective-permute-done | bytes 327712 | tf_op jit(solution)/shard_map/ppermute | solution.py:583
  98.6 0.8 add_convert_fusion
  (4 shorter events, 0.0 us)
Async XLA Ops:
  0.9 10.1 %collective-permute-start.1 = (bf16[16,2560]{1,0:T(8,128)(2,1)S(1)}, bf16[16,2560]{1,0:T(8,128)(2,1)S(1)}, u32[]{:S(2)}, u32[]{:S(2)}) collective-permute-start(bf16[16,2560]{1,0:T(8,128)(2,1)S(1)} %get-tuple-element.35), channel_id=1, source_target_pairs={{4,0},{8,4},{12,8},{16,12},{20,16},{24,20},{28,24},{32,28},{36,32}... | collective-permute-start | bytes 245768 | tf_op jit(solution)/shard_map/ppermute | solution.py:561
  2.2 8.8 %collective-permute-start = (bf16[16,2560]{1,0:T(8,128)(2,1)S(1)}, bf16[16,2560]{1,0:T(8,128)(2,1)S(1)}, u32[]{:S(2)}, u32[]{:S(2)}) collective-permute-start(bf16[16,2560]{1,0:T(8,128)(2,1)S(1)} %get-tuple-element.36), channel_id=1, source_target_pairs={{0,4},{4,8},{8,12},{12,16},{16,20},{20,24},{24,28},{28,32},{32,36}... | collective-permute-start | bytes 245768 | tf_op jit(solution)/shard_map/ppermute | solution.py:560
  11.1 13.4 %copy-start = (bf16[512,2560]{1,0:T(8,128)(2,1)}, bf16[512,2560]{1,0:T(8,128)(2,1)S(1)}, u32[]{:S(2)}) copy-start(bf16[512,2560]{1,0:T(8,128)(2,1)S(1)} %get-tuple-element.20.x_ref) | copy-start | bytes 7864324
  24.4 25.0 %all-to-all-start = ((bf16[32,88,128]{2,1,0:T(8,128)(2,1)}), bf16[32,88,128]{2,1,0:T(8,128)(2,1)S(1)}, u32[]{:S(2)}, u32[]{:S(2)}) async-start(bf16[32,88,128]{2,1,0:T(8,128)(2,1)} %get-tuple-element.23), calls=%async_computation | async-start | bytes 1441792 | tf_op jit(solution)/shard_map/all_to_all | solution.py:567
  51.7 16.4 %all-to-all-start.1 = ((bf16[32,80,128]{2,1,0:T(8,128)(2,1)}), bf16[32,80,128]{2,1,0:T(8,128)(2,1)S(1)}, u32[]{:S(2)}, u32[]{:S(2)}) async-start(bf16[32,80,128]{2,1,0:T(8,128)(2,1)} %scan.1), calls=%async_computation.1 | async-start | bytes 1310720 | tf_op jit(solution)/shard_map/all_to_all | solution.py:571
  76.2 4.5 %collective-permute-start.2 = (bf16[256,640]{1,0:T(8,128)(2,1)}, bf16[256,640]{1,0:T(8,128)(2,1)S(1)}, u32[]{:S(2)}, u32[]{:S(2)}) collective-permute-start(bf16[256,640]{1,0:T(8,128)(2,1)} %get-tuple-element.32), channel_id=1, source_target_pairs={{0,1},{1,0},{2,3},{3,2},{4,5},{5,4},{6,7},{7,6},{8,9},{9,8},{10,11... | collective-permute-start | bytes 983048 | tf_op jit(solution)/shard_map/ppermute | solution.py:580
  87.5 3.9 %collective-permute-start.3 = (bf16[256,640]{1,0:T(8,128)(2,1)S(1)}, bf16[256,640]{1,0:T(8,128)(2,1)S(1)}, u32[]{:S(2)}, u32[]{:S(2)}) collective-permute-start(bf16[256,640]{1,0:T(8,128)(2,1)S(1)} %project.4), channel_id=1, source_target_pairs={{0,1},{1,0},{2,3},{3,2},{4,5},{5,4},{6,7},{7,6},{8,9},{9,8},{10,11... | collective-permute-start | bytes 983048 | tf_op jit(solution)/shard_map/ppermute | solution.py:585
  88.0 10.6 %collective-permute-start.4 = (bf16[256,640]{1,0:T(8,128)(2,1)S(1)}, bf16[256,640]{1,0:T(8,128)(2,1)S(1)}, u32[]{:S(2)}, u32[]{:S(2)}) collective-permute-start(bf16[256,640]{1,0:T(8,128)(2,1)S(1)} %project.3), channel_id=1, source_target_pairs={{0,2},{2,0},{1,3},{3,1},{4,6},{6,4},{5,7},{7,5},{8,10},{10,8},{9,1... | collective-permute-start | bytes 983048 | tf_op jit(solution)/shard_map/ppermute | solution.py:583

commit v4 on v3

--- a/solution.py
+++ b/solution.py
@@ -10,10 +10,11 @@
 HEAD_DIM = 64
 STATE = 128
 HALO = 16
+EXTRA = 32
+CHUNK = 64
 TILE = 256
 LANES = 128
 epsilon = 1e-05
-highest = lax.Precision.HIGHEST
 f32 = jnp.float32
 bf16 = jnp.bfloat16
 
@@ -44,16 +45,18 @@
     return (rows == first + iota((2 * LANES, width), 1) // HEAD_DIM).astype(bf16)
 
 
-def conv_pair(ext_ref, taps, rows):
-    first, second = HALO - 3, HALO + rows
-    fwd = bwd = None
+def time_of(index, rows):
+    return (index % 8) * (rows // 8) + index // 8
+
+
+def conv_rows(ext_ref, taps, direction, rows, first, count):
+    base = (EXTRA - 24 if direction == 0 else EXTRA + rows) + first
+    total = None
     for k in range(4):
-        tap = taps[k : k + 1]
-        ahead = tap * ext_ref[first + k : first + k + rows]
-        behind = tap * ext_ref[second + 3 - k : second + 3 - k + rows]
-        fwd = ahead if fwd is None else fwd + ahead
-        bwd = behind if bwd is None else bwd + behind
-    return silu(fwd).astype(bf16), silu(bwd).astype(bf16)
+        at = base + 8 * (k if direction == 0 else 3 - k)
+        term = taps[k : k + 1] * ext_ref[at : at + count]
+        total = term if total is None else total + term
+    return silu(total).astype(bf16)
 
 
 def cumulate(matrix, v, lanes):
@@ -89,27 +92,28 @@
 def norm_kernel(
     h_ref, gain_ref, dtw_ref, dtb_ref, lr_ref,
     x_ref, delta_ref, cum_ref, cumt_ref, wend_ref, dec_ref,
-    rs_ref, dtp_ref,
+    raw_ref, dtp_ref,
 ):
     rows, width = h_ref.shape
     heads = dtb_ref.shape[1]
 
-    def forward(i, _):
-        at = pl.ds(pl.multiple_of(i * 32, 32), 32)
-        v = h_ref[at].astype(f32)
-        scale = scale_of(v)
-        rs_ref[at] = jnp.broadcast_to(scale, (32, LANES))
-        x_ref[at] = scaled(v, scale, gain_ref, 0)
-        return 0
-
-    lax.fori_loop(0, rows // 32, forward, 0)
+    order = (iota((rows, rows), 1) == time_of(iota((rows, rows), 0), rows)).astype(bf16)
     flip = flip_matrix(TILE)
     blocks = width // TILE
-    scale = rs_ref[...]
+    squares = jnp.zeros((rows, LANES), f32)
     for b in range(blocks):
+        cols = slice(b * TILE, (b + 1) * TILE)
+        v = mm(order, h_ref[:, cols])
+        raw_ref[:, cols] = v.astype(bf16)
+        squares = squares + v[:, :LANES] * v[:, :LANES] + v[:, LANES:] * v[:, LANES:]
+    mean_sq = jnp.sum(squares, axis=-1, keepdims=True) * (1.0 / width)
+    scale = jnp.broadcast_to(lax.rsqrt(mean_sq + epsilon), (rows, LANES))
+    for b in range(blocks):
+        cols = slice(b * TILE, (b + 1) * TILE)
         mirror = blocks - 1 - b
-        turned = mm(h_ref[:, mirror * TILE : (mirror + 1) * TILE], flip)
-        x_ref[rows:, b * TILE : (b + 1) * TILE] = scaled(turned, scale, gain_ref, b * 2)
+        x_ref[:rows, cols] = scaled(raw_ref[:, cols].astype(f32), scale, gain_ref, b * 2)
+        turned = mm(raw_ref[:, mirror * TILE : (mirror + 1) * TILE], flip)
+        x_ref[rows:, cols] = scaled(turned, scale, gain_ref, b * 2)
     dtp_ref[...] = jnp.zeros_like(dtp_ref)
     dtp_ref[0:heads] = dtw_ref[...]
     bias = jnp.concatenate([dtb_ref[...], jnp.zeros((1, LANES - heads), f32)], axis=1)
@@ -121,8 +125,9 @@
     delta = jnp.maximum(dt, 0.0) + jnp.log1p(jnp.exp(-jnp.abs(dt)))
     delta_ref[...] = delta
     log_decay = -delta * jnp.exp(rate)
-    lower = (iota((rows, rows), 0) >= iota((rows, rows), 1)).astype(bf16)
-    upper = (iota((rows, rows), 0) <= iota((rows, rows), 1)).astype(bf16)
+    later, sooner = time_of(iota((rows, rows), 0), rows), time_of(iota((rows, rows), 1), rows)
+    lower = (later >= sooner).astype(bf16)
+    upper = (later <= sooner).astype(bf16)
     for d in range(2):
         at = slice(d * rows, (d + 1) * rows)
         cum = cumulate(upper if d else lower, log_decay[at], heads)
@@ -156,7 +161,7 @@
             jax.ShapeDtypeStruct((2 * rows, 2 * LANES), bf16),
             jax.ShapeDtypeStruct((8, LANES), f32),
         ],
-        scratch_shapes=[pltpu.VMEM((rows, LANES), f32), pltpu.VMEM((LANES, width), bf16)],
+        scratch_shapes=[pltpu.VMEM((rows, width), bf16), pltpu.VMEM((LANES, width), bf16)],
         compiler_params=pltpu.CompilerParams(vmem_limit_bytes=16 << 20),
         cost_estimate=pl.CostEstimate(flops=4 << 30, bytes_accessed=5 << 20, transcendentals=0),
         name="norm",
@@ -166,7 +171,7 @@
 def entry_kernel(
     x_ref, prev_ref, next_ref, gain_ref, xw_ref, bcw_ref, xk_ref, bck_ref, wend_ref, dec_ref,
     xconv_ref, bc_ref, pay_ref,
-    ext_ref, xin_ref, bcin_ref, st_ref, bt_ref,
+    ext_ref, xin_ref, bcin_ref, st_ref, bt_ref, rim_ref, weighted_ref,
 ):
     width = x_ref.shape[1]
     rows = x_ref.shape[0] // 2
@@ -174,40 +179,57 @@
     steps = pl.num_programs(0) - 1
 
     def prelude():
-        ext_ref[HALO : HALO + 2 * rows] = x_ref[...]
+        ext_ref[EXTRA : EXTRA + 2 * rows] = x_ref[...]
         prev = prev_ref[...].astype(f32)
-        ext_ref[0:HALO] = scaled(prev, scale_of(prev), gain_ref, 0)
+        rim_ref[0, :EXTRA] = x_ref[rows - EXTRA : rows]
+        rim_ref[0, EXTRA:] = scaled(prev, scale_of(prev), gain_ref, 0)
         flip = flip_matrix(TILE)
         blocks = width // TILE
         after = next_ref[...]
         after_scale = scale_of(after.astype(f32))
         stacked = jnp.concatenate([after[:, b * TILE : (b + 1) * TILE] for b in range(blocks)], axis=0)
         stacked = mm(stacked, flip)
+        rim_ref[1, :EXTRA] = x_ref[rows : rows + EXTRA]
         for b in range(blocks):
             mirror = blocks - 1 - b
-            ext_ref[HALO + 2 * rows :, b * TILE : (b + 1) * TILE] = scaled(
+            rim_ref[1, EXTRA:, b * TILE : (b + 1) * TILE] = scaled(
                 stacked[mirror * HALO : (mirror + 1) * HALO], after_scale, gain_ref, b * 2
             )
+        shape = (EXTRA, EXTRA + HALO)
+        r, c = iota(shape, 0), iota(shape, 1)
+        s = r % 8
+        v = r // 8 - 4
+        ahead = jnp.where(s == 0, EXTRA + HALO + v, EXTRA + 8 * v + s - 1)
+        ahead = ((c == ahead) & (r >= 8)).astype(bf16)
+        j = r // 8
+        behind = jnp.where(s == 7, EXTRA + j, 8 * j + s + 1)
+        behind = ((c == behind) & (r < 24)).astype(bf16)
+        ext_ref[:EXTRA] = mm(ahead, rim_ref[0]).astype(bf16)
+        ext_ref[EXTRA + 2 * rows :] = mm(behind, rim_ref[1]).astype(bf16)
         bcin_ref[...] = mm(ext_ref[...], bcw_ref[...]).astype(bf16).astype(f32)
-        bc_pair = conv_pair(bcin_ref, bck_ref[...], rows)
         for d in range(2):
+            for first in range(0, rows, CHUNK):
+                at = slice(d * rows + first, d * rows + first + CHUNK)
+                bc_ref[at] = conv_rows(bcin_ref, bck_ref[...], d, rows, first, CHUNK)
             at = slice(d * rows, (d + 1) * rows)
-            bc_ref[at] = bc_pair[d]
-            bt_ref[d] = jnp.transpose(bc_pair[d][:, :STATE].astype(f32)).astype(bf16)
+            bt_ref[d] = jnp.transpose(bc_ref[at, :STATE].astype(f32)).astype(bf16)
 
     def product():
         return mm(ext_ref[...], xw_ref[...]).astype(bf16).astype(f32)
 
     def finish():
         tile = n - 1
-        pair = conv_pair(xin_ref, xk_ref[...], rows)
         spread_n = spread(tile * (TILE // HEAD_DIM), TILE)
         for d in range(2):
-            at = slice(d * rows, (d + 1) * rows)
-            xconv_ref[at] = pair[d]
-            weighted = (pair[d].astype(f32) * mm(wend_ref[at], spread_n)).astype(bf16)
+            for first in range(0, rows, CHUNK):
+                at = slice(d * rows + first, d * rows + first + CHUNK)
+                conv = conv_rows(xin_ref, xk_ref[...], d, rows, first, CHUNK)
+                xconv_ref[at] = conv
+                weighted_ref[at] = (conv.astype(f32) * mm(wend_ref[at], spread_n)).astype(bf16)
             column = pl.multiple_of(d * steps * TILE + tile * TILE, TILE)
-            st_ref[:, pl.ds(column, TILE)] = mm(bt_ref[d], weighted).astype(bf16)
+            st_ref[:, pl.ds(column, TILE)] = mm(
+                bt_ref[d], weighted_ref[d * rows : (d + 1) * rows]
+            ).astype(bf16)
 
     @pl.when(n == 0)
     def _():
@@ -269,11 +291,13 @@
             pltpu.HBM((slots, 88, LANES), bf16),
         ],
         scratch_shapes=[
-            pltpu.VMEM((2 * rows + 2 * HALO, width), bf16),
-            pltpu.VMEM((2 * rows + 2 * HALO, TILE), f32),
-            pltpu.VMEM((2 * rows + 2 * HALO, TILE), f32),
+            pltpu.VMEM((2 * rows + 2 * EXTRA, width), bf16),
+            pltpu.VMEM((2 * rows + 2 * EXTRA, TILE), f32),
+            pltpu.VMEM((2 * rows + 2 * EXTRA, TILE), f32),
             pltpu.VMEM((STATE, 2 * inner), bf16),
             pltpu.VMEM((2, STATE, rows), bf16),
+            pltpu.VMEM((2, EXTRA + HALO, width), bf16),
+            pltpu.VMEM((2 * rows, TILE), bf16),
         ],
         compiler_params=pltpu.CompilerParams(
             dimension_semantics=("arbitrary",), vmem_limit_bytes=26 << 20
@@ -319,7 +343,7 @@
         gram = lax.dot_general(
             bc_ref[:, STATE:], bc_ref[:, :STATE], (((1,), (1,)), ((), ())), preferred_element_type=f32
         )
-        t, s = iota((rows, rows), 0), iota((rows, rows), 1)
+        t, s = time_of(iota((rows, rows), 0), rows), time_of(iota((rows, rows), 1), rows)
         seen = jnp.where(d == 0, t - s, s - t) >= 0
         gram_ref[...] = jnp.where(seen, gram, 0.0)
 
@@ -406,56 +430,48 @@
 
 
 def weight_fetches(q, w_ref, near_ref, far_ref, sems):
-    chunks, depth, lanes = near_ref.shape
+    lanes = near_ref.shape[1]
     near = pl.ds(pl.multiple_of(q * lanes, LANES), lanes)
     far = pl.ds(pl.multiple_of((3 - q) * lanes, LANES), lanes)
-    copies = []
-    for k in range(chunks):
-        rows = slice(k * depth, (k + 1) * depth)
-        copies.append(
-            (
-                pltpu.make_async_copy(w_ref.at[rows, near], near_ref.at[k], sems.at[0, k]),
-                pltpu.make_async_copy(w_ref.at[rows, far], far_ref.at[k], sems.at[1, k]),
-            )
-        )
-    return copies
+    near_copies, far_copies = [], []
+    for k in range(near_ref.shape[0] // TILE):
+        rows = slice(k * TILE, (k + 1) * TILE)
+        near_copies.append(pltpu.make_async_copy(w_ref.at[rows, near], near_ref.at[rows], sems.at[0, k]))
+        far_copies.append(pltpu.make_async_copy(w_ref.at[rows, far], far_ref.at[rows], sems.at[1, k]))
+    return near_copies, far_copies
 
 
 def project_into(out_ref, g_ref, copies, near_ref, far_ref, adds):
-    chunks, depth, lanes = near_ref.shape
-    ahead = behind = None
-    for k in range(chunks):
-        for copy in copies[k]:
-            copy.wait()
-        one = mm(g_ref[:, k * depth : (k + 1) * depth], near_ref[k])
-        two = mm(g_ref[:, (chunks + k) * depth : (chunks + k + 1) * depth], far_ref[k])
-        ahead = one if ahead is None else ahead + one
-        behind = two if behind is None else behind + two
+    inner, lanes = near_ref.shape
+    for copy in copies[1]:
+        copy.wait()
+    behind = mm(g_ref[:, inner:], far_ref[...]).astype(bf16)
+    for copy in copies[0]:
+        copy.wait()
+    ahead = mm(g_ref[:, :inner], near_ref[...])
     flip = flip_matrix(LANES)
-    flip = jnp.concatenate([flip, flip], axis=0)
     blocks = lanes // LANES
     for b in range(blocks):
         at = slice(b * LANES, (b + 1) * LANES)
         source = slice((blocks - 1 - b) * LANES, (blocks - b) * LANES)
-        total = ahead[:, at] + mm(hi_lo(behind[:, source]), flip)
+        total = ahead[:, at] + mm(behind[:, source], flip)
         for add in adds:
             total = total + add[:, at].astype(f32)
         out_ref[:, at] = total.astype(out_ref.dtype)
 
 
 def weight_scratch(inner, lanes):
-    chunks = inner // TILE
     return [
-        pltpu.VMEM((chunks, TILE, lanes), bf16),
-        pltpu.VMEM((chunks, TILE, lanes), bf16),
-        pltpu.SemaphoreType.DMA((2, chunks)),
+        pltpu.VMEM((inner, lanes), bf16),
+        pltpu.VMEM((inner, lanes), bf16),
+        pltpu.SemaphoreType.DMA((2, inner // TILE)),
     ]
 
 
 def gate_kernel(
     target_ref, y_ref, z_ref, bc_ref, cum_ref, st_ref, gain_ref, w_ref,
     g_ref, out_ref,
-    near_ref, far_ref, sems,
+    near_ref, far_ref, sems, held_ref,
 ):
     q = pl.program_id(0)
     rows, lanes = y_ref.shape
@@ -464,9 +480,8 @@
 
     @pl.when(q == 0)
     def _():
-        for pair in copies:
-            for copy in pair:
-                copy.start()
+        for copy in copies[1] + copies[0]:
+            copy.start()
 
     state = jnp.concatenate([st_ref[:, 0, j].reshape(STATE, LANES) for j in range(groups)], axis=1)
     carried = mm(bc_ref[:, STATE:], state)
@@ -479,8 +494,9 @@
         part = y * z_ref[:, at].astype(f32)
         mean_sq = mm(hi_lo(part * part), same) * (1.0 / HEAD_DIM)
         gain = gain_ref[pl.ds((q % 2) * groups + b, 1), :]
-        column = pl.multiple_of((q * groups + b) * LANES, LANES)
-        g_ref[:, pl.ds(column, LANES)] = (part * lax.rsqrt(mean_sq + epsilon) * gain).astype(bf16)
+        held_ref[:, at] = (part * lax.rsqrt(mean_sq + epsilon) * gain).astype(bf16)
+    order = (iota((rows, rows), 0) == time_of(iota((rows, rows), 1), rows)).astype(bf16)
+    g_ref[:, pl.ds(pl.multiple_of(q * lanes, LANES), lanes)] = mm(order, held_ref[...]).astype(bf16)
 
     @pl.when(q == pl.num_programs(0) - 1)
     def _():
@@ -508,7 +524,7 @@
                 pl.BlockSpec(memory_space=pltpu.HBM),
             ],
             out_specs=[fixed(rows, 2 * inner), fixed(rows, columns)],
-            scratch_shapes=weight_scratch(inner, columns),
+            scratch_shapes=weight_scratch(inner, columns) + [pltpu.VMEM((rows, lanes), bf16)],
         ),
         out_shape=[
             jax.ShapeDtypeStruct((rows, 2 * inner), bf16),
@@ -524,9 +540,8 @@
 def project_kernel(has_add, q_ref, g_ref, w_ref, *rest):
     adds, (out_ref, near_ref, far_ref, sems) = rest[:has_add], rest[has_add:]
     copies = weight_fetches(q_ref[0], w_ref, near_ref, far_ref, sems)
-    for pair in copies:
-        for copy in pair:
-            copy.start()
+    for copy in copies[1] + copies[0]:
+        copy.start()
     project_into(out_ref, g_ref, copies, near_ref, far_ref, adds)
 
 

time: 100 us -> 98.1 us (0.981)
  Pallas kernels: 55.2 us -> 52.6 us
    pallas_call x3, Pallas kernels: 10.1 us -> 8.84 us  [project(): pl.pallas_call(functools.partial(project_kernel, len(adds)), in_specs=[pl...]
where the time goes in v4:
time: 98.1 us; the launch traced here: 97.3 us
  Pallas kernels  52.6 us (54%)
  starting transfers between devices  28.7 us (29%)
  waiting for transfers between devices  13.1 us (13%)
  local copies, waits for them, and re-layouts  1.94 us (2%)
    pallas_call x1, Pallas kernels, entry(): pl.pallas_call(entry_kernel, grid=(steps + 1,), in_specs=[vmem, vmem, vme...  12.4 us
    all_to_all x1, starting transfers between devices, per_device(): pay = lax.all_to_all(pay, 'ctx', 0, 0, tiled=True)  12.3 us
    pallas_call x1, Pallas kernels, within(): pl.pallas_call(within_kernel, grid=(2, inner // TILE), in_specs=[pl.Block...  9.59 us
    pallas_call x3, Pallas kernels, project(): pl.pallas_call(functools.partial(project_kernel, len(adds)), in_specs=[pl...  8.84 us
    pallas_call x1, Pallas kernels, gate(): pl.pallas_call(gate_kernel, grid_spec=pltpu.PrefetchScalarGridSpec(num_sc...  8.04 us
    pallas_call x1, Pallas kernels, open_gate(): pl.pallas_call(open_gate_kernel, grid=(inner // TILE,), in_specs=[fixed(h...  7.45 us
    all_to_all x1, starting transfers between devices, per_device(): state = lax.all_to_all(state, 'ctx', 0, 0, tiled=True)  4.62 us
    ppermute x1, starting transfers between devices, per_device(): lax.ppermute(hidden[-HALO:], 'ctx', [(i, i + 1) for i in range(blocks - 1)])  4.57 us
  transfers between devices with their start and end apart: 7, of which 4 were waited for; matrix products, arithmetic and copies ran while one was open for 1% of the time, Pallas kernels for 25%

profile of v4, /device:TPU:1, one launch (start us, length us, event | category | flops | bytes accessed | tf_op | source)
XLA Modules:
  0.0 97.3 jit_solution(11212123513610353801)
XLA Ops:
  0.0 0.9 fusion
  0.9 1.3 %collective-permute-start.1 = (bf16[16,2560]{1,0:T(8,128)(2,1)S(1)}, bf16[16,2560]{1,0:T(8,128)(2,1)S(1)}, u32[]{:S(2)}, u32[]{:S(2)}) collective-permute-start(bf16[16,2560]{1,0:T(8,128)(2,1)S(1)} %get-tuple-element.35), channel_id=1, source_target_pairs={{4,0},{8,4},{12,8},{16,12},{20,16},{24,20},{28,24},{32,28},{36,32}... | collective-permute-start | bytes 245768 | tf_op jit(solution)/shard_map/ppermute | solution.py:576
  2.2 4.6 %collective-permute-start = (bf16[16,2560]{1,0:T(8,128)(2,1)S(1)}, bf16[16,2560]{1,0:T(8,128)(2,1)S(1)}, u32[]{:S(2)}, u32[]{:S(2)}) collective-permute-start(bf16[16,2560]{1,0:T(8,128)(2,1)S(1)} %get-tuple-element.36), channel_id=1, source_target_pairs={{0,4},{4,8},{8,12},{12,16},{16,20},{20,24},{24,28},{28,32},{32,36}... | collective-permute-start | bytes 245768 | tf_op jit(solution)/shard_map/ppermute | solution.py:575
  6.8 4.0 %norm.1 = (bf16[512,2560]{1,0:T(8,128)(2,1)S(1)}, f32[512,128]{1,0:T(8,128)S(1)}, f32[512,128]{1,0:T(8,128)S(1)}, f32[2,24,256]{2,1,0:T(8,128)S(1)}, bf16[512,256]{1,0:T(8,128)(2,1)S(1)}, /*index=5*/f32[8,128]{1,0:T(8,128)S(1)}) custom-call(bf16[256,2560]{1,0:T(8,128)(2,1)} %h_ref.1, f32[20,128]{1,0:T(8,128)} %bitcast.14, bf16[20,2560]{1,0:T(8,128)(2,1)} %bitcast.13, ...), custom_call_target="tpu_custom_call" | custom-call | flops 4294967296 | bytes 5242880 | tf_op jit(solution)/shard_map/norm/pallas_call | solution.py:145
  10.8 0.0 collective-permute-done.prev_ref
  10.9 12.4 %entry.1 = (bf16[512,1280]{1,0:T(8,128)(2,1)}, bf16[512,256]{1,0:T(8,128)(2,1)}, bf16[32,88,128]{2,1,0:T(8,128)(2,1)}) custom-call(bf16[512,2560]{1,0:T(8,128)(2,1)S(1)} %get-tuple-element.20.x_ref, bf16[16,2560]{1,0:T(8,128)(2,1)S(1)} %collective-permute-done.prev_ref, bf16[16,2560]{1,0:T(8,128)(2,1)S(1)} %collective-permute-done.1.next_ref, ...), custom_call_target="tpu_custom_call" | custom-call | flops 4278190080 | bytes 12582912 | tf_op jit(solution)/shard_map/entry/pallas_call | solution.py:274
  23.2 12.3 %all-to-all-start = ((bf16[32,88,128]{2,1,0:T(8,128)(2,1)}), bf16[32,88,128]{2,1,0:T(8,128)(2,1)S(1)}, u32[]{:S(2)}, u32[]{:S(2)}) async-start(bf16[32,88,128]{2,1,0:T(8,128)(2,1)} %get-tuple-element.23), calls=%async_computation | async-start | bytes 1441792 | tf_op jit(solution)/shard_map/all_to_all | solution.py:582
  35.5 9.6 %within.1.y_ref = f32[512,1280]{1,0:T(8,128)} custom-call(bf16[512,1280]{1,0:T(8,128)(2,1)} %get-tuple-element.24.x_ref, bf16[512,256]{1,0:T(8,128)(2,1)} %get-tuple-element.25.bc_ref, f32[512,128]{1,0:T(8,128)S(1)} %get-tuple-element.26.cum_ref, f32[2,24,256]{2,1,0:T(8,128)S(1)} %get-tuple-element.27.cumt_ref, f32[512,128]{1,0:T(8,128)S(1)} %get-tuple-element.28.delta_ref), custom_call_target="tpu_custom_call" | custom-call | flops 3221225472 | bytes 5242880 | tf_op jit(solution)/shard_map/within/pallas_call | solution.py:364
  45.1 3.1 %all-to-all-done.pay_ref = bf16[32,88,128]{2,1,0:T(8,128)(2,1)S(1)} async-done(((bf16[32,88,128]{2,1,0:T(8,128)(2,1)}), bf16[32,88,128]{2,1,0:T(8,128)(2,1)S(1)}, u32[]{:S(2)}, u32[]{:S(2)}) %all-to-all-start) | async-done | bytes 720928 | tf_op jit(solution)/shard_map/all_to_all | solution.py:582
  48.2 2.3 %scan.1 = bf16[32,80,128]{2,1,0:T(8,128)(2,1)} custom-call(s32[1]{0:T(128)} %bitcast.7.q_ref, bf16[32,88,128]{2,1,0:T(8,128)(2,1)S(1)} %all-to-all-done.pay_ref), custom_call_target="tpu_custom_call" | custom-call | tf_op jit(solution)/shard_map/scan/pallas_call | solution.py:415
  50.5 4.6 %all-to-all-start.1 = ((bf16[32,80,128]{2,1,0:T(8,128)(2,1)}), bf16[32,80,128]{2,1,0:T(8,128)(2,1)S(1)}, u32[]{:S(2)}, u32[]{:S(2)}) async-start(bf16[32,80,128]{2,1,0:T(8,128)(2,1)} %scan.1), calls=%async_computation.1 | async-start | bytes 1310720 | tf_op jit(solution)/shard_map/all_to_all | solution.py:586
  55.2 7.5 %open_gate.1.z_ref = bf16[512,1280]{1,0:T(8,128)(2,1)S(1)} custom-call(bf16[512,2560]{1,0:T(8,128)(2,1)} %copy-done, bf16[2560,1280]{1,0:T(8,128)(2,1)} %zw_ref.1), custom_call_target="tpu_custom_call" | custom-call | flops 3355443200 | bytes 16777216 | tf_op jit(solution)/shard_map/open_gate/pallas_call | solution.py:320
  62.6 4.3 %all-to-all-done.1 = bf16[32,80,128]{2,1,0:T(8,128)(2,1)S(1)} async-done(((bf16[32,80,128]{2,1,0:T(8,128)(2,1)}), bf16[32,80,128]{2,1,0:T(8,128)(2,1)S(1)}, u32[]{:S(2)}, u32[]{:S(2)}) %all-to-all-start.1) | async-done | bytes 655392 | tf_op jit(solution)/shard_map/all_to_all | solution.py:586
  67.0 8.0 %gate.1 = (bf16[256,2560]{1,0:T(8,128)(2,1)S(1)}, bf16[256,640]{1,0:T(8,128)(2,1)}) custom-call(s32[1]{0:T(128)} %bitcast.2.target_ref, f32[512,1280]{1,0:T(8,128)} %within.1.y_ref, bf16[512,1280]{1,0:T(8,128)(2,1)S(1)} %open_gate.1.z_ref, bf16[512,256]{1,0:T(8,128)(2,1)} %get-tuple-element.25.bc_ref, f32[512,128]{1,0:T(8,128)S(1)} %get-tuple-element.26.cum_ref, ...), custom_call_target="tpu_custom_call" | custom-call | tf_op jit(solution)/shard_map/gate/pallas_call | solution.py:512
  75.0 3.0 %collective-permute-start.2 = (bf16[256,640]{1,0:T(8,128)(2,1)}, bf16[256,640]{1,0:T(8,128)(2,1)S(1)}, u32[]{:S(2)}, u32[]{:S(2)}) collective-permute-start(bf16[256,640]{1,0:T(8,128)(2,1)} %get-tuple-element.32), channel_id=1, source_target_pairs={{0,1},{1,0},{2,3},{3,2},{4,5},{5,4},{6,7},{7,6},{8,9},{9,8},{10,11... | collective-permute-start | bytes 983048 | tf_op jit(solution)/shard_map/ppermute | solution.py:595
  78.1 1.5 %collective-permute-done.2.rest_0_ = bf16[256,640]{1,0:T(8,128)(2,1)S(1)} collective-permute-done((bf16[256,640]{1,0:T(8,128)(2,1)}, bf16[256,640]{1,0:T(8,128)(2,1)S(1)}, u32[]{:S(2)}, u32[]{:S(2)}) %collective-permute-start.2) | collective-permute-done | bytes 327712 | tf_op jit(solution)/shard_map/ppermute | solution.py:595
  79.5 2.9 %project.3 = bf16[256,640]{1,0:T(8,128)(2,1)S(1)} custom-call(s32[1]{0:T(128)} %bitcast.1.q_ref, bf16[256,2560]{1,0:T(8,128)(2,1)S(1)} %get-tuple-element.33.g_ref, bf16[1280,2560]{1,0:T(8,128)(2,1)} %w_ref.7, bf16[256,640]{1,0:T(8,128)(2,1)S(1)} %collective-permute-done.2.rest_0_), custom_call_target="tpu_custom_call" | custom-call | flops 838860800 | bytes 5242880 | tf_op jit(solution)/shard_map/project/pallas_call | solution.py:553
  82.5 2.9 %project.4 = bf16[256,640]{1,0:T(8,128)(2,1)S(1)} custom-call(s32[1]{0:T(128)} %bitcast.10.q_ref, bf16[256,2560]{1,0:T(8,128)(2,1)S(1)} %get-tuple-element.33.g_ref, bf16[1280,2560]{1,0:T(8,128)(2,1)} %w_ref.7), custom_call_target="tpu_custom_call" | custom-call | flops 838860800 | bytes 5242880 | tf_op jit(solution)/shard_map/project/pallas_call | solution.py:553
  85.4 0.5 collective-permute-start.3
  85.9 2.4 %collective-permute-start.4 = (bf16[256,640]{1,0:T(8,128)(2,1)S(1)}, bf16[256,640]{1,0:T(8,128)(2,1)S(1)}, u32[]{:S(2)}, u32[]{:S(2)}) collective-permute-start(bf16[256,640]{1,0:T(8,128)(2,1)S(1)} %project.3), channel_id=1, source_target_pairs={{0,2},{2,0},{1,3},{3,1},{4,6},{6,4},{5,7},{7,5},{8,10},{10,8},{9,1... | collective-permute-start | bytes 983048 | tf_op jit(solution)/shard_map/ppermute | solution.py:598
  88.3 1.0 %constant_dynamic-slice_fusion.rest_1_ = bf16[256,640]{1,0:T(8,128)(2,1)S(1)} fusion(bf16[256,2560]{1,0:T(8,128)(2,1)} %h_ref.1, s32[]{:T(128)S(6)} %select_n.21), kind=kLoop, calls=%fused_computation.1 | loop fusion | bytes 655364 | tf_op jit(solution)/shard_map/dynamic_slice | solution.py:602
  89.4 3.0 %project.5 = f32[256,640]{1,0:T(8,128)S(1)} custom-call(s32[1]{0:T(128)} %bitcast.q_ref, bf16[256,2560]{1,0:T(8,128)(2,1)S(1)} %get-tuple-element.33.g_ref, bf16[1280,2560]{1,0:T(8,128)(2,1)} %w_ref.7, bf16[256,640]{1,0:T(8,128)(2,1)S(1)} %collective-permute-done.3.rest_0_, bf16[256,640]{1,0:T(8,128)(2,1)S(1)} %constant_dynamic-slice_fusion.rest_1_), custom_call_target="tpu_custom_call" | custom-call | flops 838860800 | bytes 5242880 | tf_op jit(solution)/shard_map/project/pallas_call | solution.py:553
  92.3 4.2 %collective-permute-done.4 = bf16[256,640]{1,0:T(8,128)(2,1)S(1)} collective-permute-done((bf16[256,640]{1,0:T(8,128)(2,1)S(1)}, bf16[256,640]{1,0:T(8,128)(2,1)S(1)}, u32[]{:S(2)}, u32[]{:S(2)}) %collective-permute-start.4) | collective-permute-done | bytes 327712 | tf_op jit(solution)/shard_map/ppermute | solution.py:598
  96.5 0.8 add_convert_fusion
  (4 shorter events, 0.0 us)
Async XLA Ops:
  0.9 9.9 %collective-permute-start.1 = (bf16[16,2560]{1,0:T(8,128)(2,1)S(1)}, bf16[16,2560]{1,0:T(8,128)(2,1)S(1)}, u32[]{:S(2)}, u32[]{:S(2)}) collective-permute-start(bf16[16,2560]{1,0:T(8,128)(2,1)S(1)} %get-tuple-element.35), channel_id=1, source_target_pairs={{4,0},{8,4},{12,8},{16,12},{20,16},{24,20},{28,24},{32,28},{36,32}... | collective-permute-start | bytes 245768 | tf_op jit(solution)/shard_map/ppermute | solution.py:576
  2.2 8.6 %collective-permute-start = (bf16[16,2560]{1,0:T(8,128)(2,1)S(1)}, bf16[16,2560]{1,0:T(8,128)(2,1)S(1)}, u32[]{:S(2)}, u32[]{:S(2)}) collective-permute-start(bf16[16,2560]{1,0:T(8,128)(2,1)S(1)} %get-tuple-element.36), channel_id=1, source_target_pairs={{0,4},{4,8},{8,12},{12,16},{16,20},{20,24},{24,28},{28,32},{32,36}... | collective-permute-start | bytes 245768 | tf_op jit(solution)/shard_map/ppermute | solution.py:575
  10.8 12.4 %copy-start = (bf16[512,2560]{1,0:T(8,128)(2,1)}, bf16[512,2560]{1,0:T(8,128)(2,1)S(1)}, u32[]{:S(2)}) copy-start(bf16[512,2560]{1,0:T(8,128)(2,1)S(1)} %get-tuple-element.20.x_ref) | copy-start | bytes 7864324
  23.2 25.0 %all-to-all-start = ((bf16[32,88,128]{2,1,0:T(8,128)(2,1)}), bf16[32,88,128]{2,1,0:T(8,128)(2,1)S(1)}, u32[]{:S(2)}, u32[]{:S(2)}) async-start(bf16[32,88,128]{2,1,0:T(8,128)(2,1)} %get-tuple-element.23), calls=%async_computation | async-start | bytes 1441792 | tf_op jit(solution)/shard_map/all_to_all | solution.py:582
  50.5 16.5 %all-to-all-start.1 = ((bf16[32,80,128]{2,1,0:T(8,128)(2,1)}), bf16[32,80,128]{2,1,0:T(8,128)(2,1)S(1)}, u32[]{:S(2)}, u32[]{:S(2)}) async-start(bf16[32,80,128]{2,1,0:T(8,128)(2,1)} %scan.1), calls=%async_computation.1 | async-start | bytes 1310720 | tf_op jit(solution)/shard_map/all_to_all | solution.py:586
  75.0 4.5 %collective-permute-start.2 = (bf16[256,640]{1,0:T(8,128)(2,1)}, bf16[256,640]{1,0:T(8,128)(2,1)S(1)}, u32[]{:S(2)}, u32[]{:S(2)}) collective-permute-start(bf16[256,640]{1,0:T(8,128)(2,1)} %get-tuple-element.32), channel_id=1, source_target_pairs={{0,1},{1,0},{2,3},{3,2},{4,5},{5,4},{6,7},{7,6},{8,9},{9,8},{10,11... | collective-permute-start | bytes 983048 | tf_op jit(solution)/shard_map/ppermute | solution.py:595
  85.4 3.9 %collective-permute-start.3 = (bf16[256,640]{1,0:T(8,128)(2,1)S(1)}, bf16[256,640]{1,0:T(8,128)(2,1)S(1)}, u32[]{:S(2)}, u32[]{:S(2)}) collective-permute-start(bf16[256,640]{1,0:T(8,128)(2,1)S(1)} %project.4), channel_id=1, source_target_pairs={{0,1},{1,0},{2,3},{3,2},{4,5},{5,4},{6,7},{7,6},{8,9},{9,8},{10,11... | collective-permute-start | bytes 983048 | tf_op jit(solution)/shard_map/ppermute | solution.py:600
  85.9 10.6 %collective-permute-start.4 = (bf16[256,640]{1,0:T(8,128)(2,1)S(1)}, bf16[256,640]{1,0:T(8,128)(2,1)S(1)}, u32[]{:S(2)}, u32[]{:S(2)}) collective-permute-start(bf16[256,640]{1,0:T(8,128)(2,1)S(1)} %project.3), channel_id=1, source_target_pairs={{0,2},{2,0},{1,3},{3,1},{4,6},{6,4},{5,7},{7,5},{8,10},{10,8},{9,1... | collective-permute-start | bytes 983048 | tf_op jit(solution)/shard_map/ppermute | solution.py:598

commit v5 on v4

--- a/solution.py
+++ b/solution.py
@@ -12,6 +12,7 @@
 HALO = 16
 EXTRA = 32
 CHUNK = 64
+FETCHES = 5
 TILE = 256
 LANES = 128
 epsilon = 1e-05
@@ -90,12 +91,18 @@
 
 
 def norm_kernel(
-    h_ref, gain_ref, dtw_ref, dtb_ref, lr_ref,
-    x_ref, delta_ref, cum_ref, cumt_ref, wend_ref, dec_ref,
-    raw_ref, dtp_ref,
+    h_ref, gain_ref, dtw_ref, dtb_ref, lr_ref, xw_ref, bcw_ref,
+    x_ref, delta_ref, cum_ref, cumt_ref, wend_ref, dec_ref, xw_kept, bcw_kept,
+    raw_ref, dtp_ref, sems,
 ):
     rows, width = h_ref.shape
     heads = dtb_ref.shape[1]
+    copies = [pltpu.make_async_copy(bcw_ref, bcw_kept, sems.at[0])]
+    for k in range(FETCHES):
+        part = slice(k * width // FETCHES, (k + 1) * width // FETCHES)
+        copies.append(pltpu.make_async_copy(xw_ref.at[part], xw_kept.at[part], sems.at[1 + k]))
+    for copy in copies:
+        copy.start()
 
     order = (iota((rows, rows), 1) == time_of(iota((rows, rows), 0), rows)).astype(bf16)
     flip = flip_matrix(TILE)
@@ -137,9 +144,11 @@
         wend_ref[at] = hi_lo(jnp.exp(jnp.minimum(last - cum, 0.0)) * delta[at])
         dec = jnp.where(iota((1, LANES), 1) < heads, jnp.exp(last), 0.0)
         dec_ref[d : d + 1] = dec
-
-
-def norm(hidden, gain, dtw, dtb, lr):
+    for copy in copies:
+        copy.wait()
+
+
+def norm(hidden, gain, dtw, dtb, lr, xw, bcw):
     rows, width = hidden.shape
     heads = dtb.shape[1]
     return pl.pallas_call(
@@ -148,10 +157,12 @@
         in_specs=[
             fixed(rows, width), fixed(width // LANES, LANES), fixed(heads, width),
             fixed(1, heads), fixed(1, heads),
+            pl.BlockSpec(memory_space=pltpu.HBM), pl.BlockSpec(memory_space=pltpu.HBM),
         ],
         out_specs=[
             fixed(2 * rows, width), fixed(2 * rows, LANES), fixed(2 * rows, LANES),
             fixed(2, 24, rows), fixed(2 * rows, 2 * LANES), fixed(8, LANES),
+            pl.BlockSpec(memory_space=pltpu.VMEM), pl.BlockSpec(memory_space=pltpu.VMEM),
         ],
         out_shape=[
             jax.ShapeDtypeStruct((2 * rows, width), bf16),
@@ -160,12 +171,20 @@
             jax.ShapeDtypeStruct((2, 24, rows), f32),
             jax.ShapeDtypeStruct((2 * rows, 2 * LANES), bf16),
             jax.ShapeDtypeStruct((8, LANES), f32),
-        ],
-        scratch_shapes=[pltpu.VMEM((rows, width), bf16), pltpu.VMEM((LANES, width), bf16)],
-        compiler_params=pltpu.CompilerParams(vmem_limit_bytes=16 << 20),
+            jax.ShapeDtypeStruct(xw.shape, bf16),
+            jax.ShapeDtypeStruct(bcw.shape, bf16),
+        ],
+        scratch_shapes=[
+            pltpu.VMEM((rows, width), bf16),
+            pltpu.VMEM((LANES, width), bf16),
+            pltpu.SemaphoreType.DMA((1 + FETCHES,)),
+        ],
+        compiler_params=pltpu.CompilerParams(vmem_limit_bytes=28 << 20),
         cost_estimate=pl.CostEstimate(flops=4 << 30, bytes_accessed=5 << 20, transcendentals=0),
         name="norm",
-    )(off_chip(hidden), off_chip(gain), off_chip(dtw), off_chip(dtb), off_chip(lr))
+    )(
+        off_chip(hidden), off_chip(gain), off_chip(dtw), off_chip(dtb), off_chip(lr), off_chip(xw), off_chip(bcw)
+    )
 
 
 def entry_kernel(
@@ -215,7 +234,8 @@
             bt_ref[d] = jnp.transpose(bc_ref[at, :STATE].astype(f32)).astype(bf16)
 
     def product():
-        return mm(ext_ref[...], xw_ref[...]).astype(bf16).astype(f32)
+        column = pl.multiple_of(jnp.minimum(n, steps - 1) * TILE, TILE)
+        return mm(ext_ref[...], xw_ref[:, pl.ds(column, TILE)]).astype(bf16).astype(f32)
 
     def finish():
         tile = n - 1
@@ -264,7 +284,6 @@
     rows = x.shape[0] // 2
     inner = xw.shape[1]
     steps = inner // TILE
-    ahead = lambda n: jnp.minimum(n, steps - 1)
     behind = lambda n: jnp.maximum(n - 1, 0)
     whole = lambda *shape: pl.BlockSpec(shape, lambda n: (0,) * len(shape))
     once = lambda *shape: pl.BlockSpec(
@@ -276,8 +295,7 @@
         grid=(steps + 1,),
         in_specs=[
             vmem, vmem, vmem, once(width // LANES, LANES),
-            pl.BlockSpec((width, TILE), lambda n: (0, ahead(n))),
-            once(width, 2 * STATE),
+            vmem, vmem,
             pl.BlockSpec((4, TILE), lambda n: (0, behind(n))),
             once(4, 2 * STATE), vmem, vmem,
         ],
@@ -306,7 +324,7 @@
             flops=2 * 544 * width * (inner + 256), bytes_accessed=12 << 20, transcendentals=0
         ),
         name="entry",
-    )(x, prev_rows, next_rows, off_chip(gain), off_chip(xw), off_chip(bcw), off_chip(xk), off_chip(bck), wend, dec)
+    )(x, prev_rows, next_rows, off_chip(gain), xw, bcw, off_chip(xk), off_chip(bck), wend, dec)
 
 
 def open_gate_kernel(x_ref, zw_ref, z_ref):
@@ -355,7 +373,7 @@
         behind = cumt_ref[0, pl.ds(n * heads + k, 1), :]
         decay = jnp.exp(jnp.minimum(cum[:, k : k + 1] - behind, 0.0)) * gram_ref[...]
         total = total + mm(decay.astype(bf16), jnp.where(owner == k, weighted, 0.0).astype(bf16))
-    y_ref[...] = total
+    y_ref[...] = total.astype(bf16)
 
 
 def within(xconv, bc, cum, cumt, delta):
@@ -372,7 +390,7 @@
             pl.BlockSpec((rows, LANES), lambda d, n: (d, 0)),
         ],
         out_specs=pl.BlockSpec((rows, TILE), lambda d, n: (d, n)),
-        out_shape=pltpu.HBM((2 * rows, inner), f32),
+        out_shape=pltpu.HBM((2 * rows, inner), bf16),
         scratch_shapes=[pltpu.VMEM((rows, rows), f32)],
         compiler_params=pltpu.CompilerParams(
             dimension_semantics=("arbitrary", "arbitrary"), vmem_limit_bytes=12 << 20
@@ -382,7 +400,7 @@
     )(off_chip(xconv), off_chip(bc), cum, cumt, delta)
 
 
-def scan_kernel(q_ref, pay_ref, out_ref, carry_ref):
+def scan_kernel(q_ref, pay_ref, out_ref, carry_ref, dec_ref):
     q = q_ref[0]
     half, turned = q % 2, q // 2
     depth = pay_ref.shape[0]
@@ -394,10 +412,12 @@
     first = half * (5 * LANES // HEAD_DIM)
     place = iota((LANES, 5 * LANES), 0) == first + iota((LANES, 5 * LANES), 1) // HEAD_DIM
     place = place.astype(bf16)
+    tails = pay_ref[:, 80:88].astype(f32).reshape(8 * depth, LANES).astype(bf16)
+    dec_ref[...] = mm(tails, place)
     carry = [carry_ref[16 * j : 16 * j + 16] for j in range(5)]
     for i in range(depth):
         at = jnp.where(turned == 1, depth - 1 - i, i)
-        decays = mm(pay_ref[at, 80:88], place)
+        decays = dec_ref[pl.ds(pl.multiple_of(8 * at, 8), 8)]
         decay = decays[0:1] + decays[1:2]
         for j in range(5):
             rows = slice(16 * j, 16 * j + 16)
@@ -419,7 +439,7 @@
             grid=(steps,),
             in_specs=[pl.BlockSpec((depth, 88, LANES), chunk)],
             out_specs=pl.BlockSpec((depth, 80, LANES), chunk),
-            scratch_shapes=[pltpu.VMEM((80, LANES), f32)],
+            scratch_shapes=[pltpu.VMEM((80, LANES), f32), pltpu.VMEM((8 * depth, 5 * LANES), f32)],
         ),
         out_shape=jax.ShapeDtypeStruct((slots, 80, LANES), bf16),
         compiler_params=pltpu.CompilerParams(
@@ -486,13 +506,13 @@
     state = jnp.concatenate([st_ref[:, 0, j].reshape(STATE, LANES) for j in range(groups)], axis=1)
     carried = mm(bc_ref[:, STATE:], state)
     reach = mm(hi_lo(jnp.exp(cum_ref[...])), spread((q % 2) * (lanes // HEAD_DIM), lanes))
-    same = (iota((2 * LANES, LANES), 0) % LANES) // HEAD_DIM == iota((2 * LANES, LANES), 1) // HEAD_DIM
+    same = iota((LANES, LANES), 0) // HEAD_DIM == iota((LANES, LANES), 1) // HEAD_DIM
     same = same.astype(bf16)
     for b in range(groups):
         at = slice(b * LANES, (b + 1) * LANES)
-        y = y_ref[:, at] + carried[:, at] * reach[:, at]
+        y = y_ref[:, at].astype(f32) + carried[:, at] * reach[:, at]
         part = y * z_ref[:, at].astype(f32)
-        mean_sq = mm(hi_lo(part * part), same) * (1.0 / HEAD_DIM)
+        mean_sq = mm((part * part).astype(bf16), same) * (1.0 / HEAD_DIM)
         gain = gain_ref[pl.ds((q % 2) * groups + b, 1), :]
         held_ref[:, at] = (part * lax.rsqrt(mean_sq + epsilon) * gain).astype(bf16)
     order = (iota((rows, rows), 0) == time_of(iota((rows, rows), 1), rows)).astype(bf16)
@@ -575,9 +595,11 @@
     prev_rows = lax.ppermute(hidden[-HALO:], "ctx", [(i, i + 1) for i in range(blocks - 1)])
     next_rows = lax.ppermute(hidden[:HALO], "ctx", [(i + 1, i) for i in range(blocks - 1)])
     gain = norm_gain.reshape(-1, LANES)
-    normed, delta, cum, cumt, wend, dec = norm(hidden, gain, dt_weight.T, dt_bias[None], log_rate[None])
+    normed, delta, cum, cumt, wend, dec, x_kept, bc_kept = norm(
+        hidden, gain, dt_weight.T, dt_bias[None], log_rate[None], x_weight, bc_weight
+    )
     xconv, bc, pay = entry(
-        normed, prev_rows, next_rows, gain, x_weight, bc_weight, x_kernel, bc_kernel, wend, dec, blocks
+        normed, prev_rows, next_rows, gain, x_kept, bc_kept, x_kernel, bc_kernel, wend, dec, blocks
     )
     pay = lax.all_to_all(pay, "ctx", 0, 0, tiled=True)
     y = within(xconv, bc, cum, cumt, delta)
@@ -593,7 +615,8 @@
         quarter(1 - far, 1 - core), y, open_z, bc, cum, state, out_gain.reshape(-1, LANES), out_weight
     )
     first = lax.ppermute(first, "head", core_swap)
-    second = project(quarter(1 - far, core), gated, out_weight, bf16, first)
+    second = project(quarter(1 - far, core), gated, out_weight, f32)
+    second = (second + first.astype(f32)).astype(bf16)
     second, gated = lax.optimization_barrier((second, gated))
     second = lax.ppermute(second, "head", far_swap)
     third = project(quarter(far, 1 - core), gated, out_weight, bf16)

time: 98.1 us -> 92.5 us (0.943)
  starting transfers between devices: 28.7 us -> 25.4 us
  waiting for transfers between devices: 13.1 us -> 11.4 us
    all_to_all x1, starting transfers between devices: 12.3 us -> 9.87 us  [per_device(): pay = lax.all_to_all(pay, 'ctx', 0, 0, tiled=True)]
    pallas_call x1, Pallas kernels: 4.01 us -> 6.04 us  [norm(): pl.pallas_call(norm_kernel, grid=(1,), in_specs=[fixed(rows, width), fixe...]
    pallas_call x1, Pallas kernels: 12.4 us -> 10.5 us  [entry(): pl.pallas_call(entry_kernel, grid=(steps + 1,), in_specs=[vmem, vmem, vme...]
    ppermute x1, waiting for transfers between devices: 1.47 us -> 0.01 us  [per_device(): first = lax.ppermute(first, 'head', core_swap)]
  transfers between devices with their start and end apart: 7 -> 7, of which waited for: 4 -> 3; matrix products, arithmetic and copies ran while one was open for 1% -> 1% of each run, Pallas kernels for 25% -> 31%
where the time goes in v5:
time: 92.5 us; the launch traced here: 91.7 us
  Pallas kernels  52 us (56%)
  starting transfers between devices  25.4 us (27%)
  waiting for transfers between devices  11.4 us (12%)
  local copies, waits for them, and re-layouts  1.94 us (2%)
    pallas_call x1, Pallas kernels, entry(): pl.pallas_call(entry_kernel, grid=(steps + 1,), in_specs=[vmem, vmem, vme...  10.5 us
    all_to_all x1, starting transfers between devices, per_device(): pay = lax.all_to_all(pay, 'ctx', 0, 0, tiled=True)  9.87 us
    pallas_call x1, Pallas kernels, within(): pl.pallas_call(within_kernel, grid=(2, inner // TILE), in_specs=[pl.Block...  9.36 us
    pallas_call x3, Pallas kernels, project(): pl.pallas_call(functools.partial(project_kernel, len(adds)), in_specs=[pl...  8.84 us
    pallas_call x1, Pallas kernels, gate(): pl.pallas_call(gate_kernel, grid_spec=pltpu.PrefetchScalarGridSpec(num_sc...  7.68 us
    pallas_call x1, Pallas kernels, open_gate(): pl.pallas_call(open_gate_kernel, grid=(inner // TILE,), in_specs=[fixed(h...  7.45 us
    pallas_call x1, Pallas kernels, norm(): pl.pallas_call(norm_kernel, grid=(1,), in_specs=[fixed(rows, width), fixe...  6.04 us
    all_to_all x1, starting transfers between devices, per_device(): state = lax.all_to_all(state, 'ctx', 0, 0, tiled=True)  4.39 us
  transfers between devices with their start and end apart: 7, of which 3 were waited for; matrix products, arithmetic and copies ran while one was open for 1% of the time, Pallas kernels for 31%

profile of v5, /device:TPU:1, one launch (start us, length us, event | category | flops | bytes accessed | tf_op | source)
XLA Modules:
  0.0 91.7 jit_solution(17599747181616017559)
XLA Ops:
  0.0 0.9 %fusion = (bf16[16,2560]{1,0:T(8,128)(2,1)S(1)}, bf16[16,2560]{1,0:T(8,128)(2,1)S(1)}) fusion(bf16[256,2560]{1,0:T(8,128)(2,1)} %h_ref.1), kind=kLoop, calls=%fused_computation.3 | loop fusion | bytes 327680 | tf_op jit(solution)/shard_map/slice | solution.py:596
  0.9 3.9 %collective-permute-start = (bf16[16,2560]{1,0:T(8,128)(2,1)S(1)}, bf16[16,2560]{1,0:T(8,128)(2,1)S(1)}, u32[]{:S(2)}, u32[]{:S(2)}) collective-permute-start(bf16[16,2560]{1,0:T(8,128)(2,1)S(1)} %get-tuple-element.40), channel_id=1, source_target_pairs={{0,4},{4,8},{8,12},{12,16},{16,20},{20,24},{24,28},{28,32},{32,36}... | collective-permute-start | bytes 245768 | tf_op jit(solution)/shard_map/ppermute | solution.py:595
  4.9 1.3 %collective-permute-start.1 = (bf16[16,2560]{1,0:T(8,128)(2,1)S(1)}, bf16[16,2560]{1,0:T(8,128)(2,1)S(1)}, u32[]{:S(2)}, u32[]{:S(2)}) collective-permute-start(bf16[16,2560]{1,0:T(8,128)(2,1)S(1)} %get-tuple-element.39), channel_id=1, source_target_pairs={{4,0},{8,4},{12,8},{16,12},{20,16},{24,20},{28,24},{32,28},{36,32}... | collective-permute-start | bytes 245768 | tf_op jit(solution)/shard_map/ppermute | solution.py:596
  6.2 6.0 %norm.1 = (bf16[512,2560]{1,0:T(8,128)(2,1)S(1)}, f32[512,128]{1,0:T(8,128)S(1)}, f32[512,128]{1,0:T(8,128)S(1)}, f32[2,24,256]{2,1,0:T(8,128)S(1)}, bf16[512,25...) custom-call(bf16[256,2560]{1,0:T(8,128)(2,1)} %h_ref.1, ...), custom_call_target="tpu_custom_call" | custom-call | flops 4294967296 | bytes 5242880 | tf_op jit(solution)/shard_map/norm/pallas_call | solution.py:154
  12.2 0.0 collective-permute-done.prev_ref
  12.3 10.5 %entry.1 = (bf16[512,1280]{1,0:T(8,128)(2,1)}, bf16[512,256]{1,0:T(8,128)(2,1)}, bf16[32,88,128]{2,1,0:T(8,128)(2,1)}) custom-call(bf16[512,2560]{1,0:T(8,128)(2,1)S(1)} %get-tuple-element.22.x_ref, bf16[16,2560]{1,0:T(8,128)(2,1)S(1)} %collective-permute-done.prev_ref, bf16[16,2560]{1,0:T(8,128)(2,1)S(1)} %collective-permute-done.1.next_ref, ...), custom_call_target="tpu_custom_call" | custom-call | flops 4278190080 | bytes 12582912 | tf_op jit(solution)/shard_map/entry/pallas_call | solution.py:293
  22.8 9.9 %all-to-all-start = ((bf16[32,88,128]{2,1,0:T(8,128)(2,1)}), bf16[32,88,128]{2,1,0:T(8,128)(2,1)S(1)}, u32[]{:S(2)}, u32[]{:S(2)}) async-start(bf16[32,88,128]{2,1,0:T(8,128)(2,1)} %get-tuple-element.27), calls=%async_computation | async-start | bytes 1441792 | tf_op jit(solution)/shard_map/all_to_all | solution.py:604
  32.6 9.4 %within.1.y_ref = bf16[512,1280]{1,0:T(8,128)(2,1)} custom-call(bf16[512,1280]{1,0:T(8,128)(2,1)} %get-tuple-element.28.x_ref, bf16[512,256]{1,0:T(8,128)(2,1)} %get-tuple-element.29.bc_ref, f32[512,128]{1,0:T(8,128)S(1)} %get-tuple-element.30.cum_ref, f32[2,24,256]{2,1,0:T(8,128)S(1)} %get-tuple-element.31.cumt_ref, f32[512,128]{1,0:T(8,128)S(1)} %get-tuple-element.32.delta_ref), custom_call_target="tpu_custom_call" | custom-call | flops 3221225472 | bytes 5242880 | tf_op jit(solution)/shard_map/within/pallas_call | solution.py:382
  42.0 3.3 %all-to-all-done.pay_ref = bf16[32,88,128]{2,1,0:T(8,128)(2,1)S(1)} async-done(((bf16[32,88,128]{2,1,0:T(8,128)(2,1)}), bf16[32,88,128]{2,1,0:T(8,128)(2,1)S(1)}, u32[]{:S(2)}, u32[]{:S(2)}) %all-to-all-start) | async-done | bytes 720928 | tf_op jit(solution)/shard_map/all_to_all | solution.py:604
  45.4 2.1 %scan.1 = bf16[32,80,128]{2,1,0:T(8,128)(2,1)} custom-call(s32[1]{0:T(128)} %bitcast.7.q_ref, bf16[32,88,128]{2,1,0:T(8,128)(2,1)S(1)} %all-to-all-done.pay_ref), custom_call_target="tpu_custom_call" | custom-call | tf_op jit(solution)/shard_map/scan/pallas_call | solution.py:435
  47.5 4.4 %all-to-all-start.1 = ((bf16[32,80,128]{2,1,0:T(8,128)(2,1)}), bf16[32,80,128]{2,1,0:T(8,128)(2,1)S(1)}, u32[]{:S(2)}, u32[]{:S(2)}) async-start(bf16[32,80,128]{2,1,0:T(8,128)(2,1)} %scan.1), calls=%async_computation.1 | async-start | bytes 1310720 | tf_op jit(solution)/shard_map/all_to_all | solution.py:608
  51.9 7.5 %open_gate.1.z_ref = bf16[512,1280]{1,0:T(8,128)(2,1)S(1)} custom-call(bf16[512,2560]{1,0:T(8,128)(2,1)} %copy-done, bf16[2560,1280]{1,0:T(8,128)(2,1)} %zw_ref.1), custom_call_target="tpu_custom_call" | custom-call | flops 3355443200 | bytes 16777216 | tf_op jit(solution)/shard_map/open_gate/pallas_call | solution.py:338
  59.4 4.3 %all-to-all-done.1 = bf16[32,80,128]{2,1,0:T(8,128)(2,1)S(1)} async-done(((bf16[32,80,128]{2,1,0:T(8,128)(2,1)}), bf16[32,80,128]{2,1,0:T(8,128)(2,1)S(1)}, u32[]{:S(2)}, u32[]{:S(2)}) %all-to-all-start.1) | async-done | bytes 655392 | tf_op jit(solution)/shard_map/all_to_all | solution.py:608
  63.7 7.7 %gate.1 = (bf16[256,2560]{1,0:T(8,128)(2,1)S(1)}, bf16[256,640]{1,0:T(8,128)(2,1)}) custom-call(s32[1]{0:T(128)} %bitcast.2.target_ref, bf16[512,1280]{1,0:T(8,128)(2,1)} %within.1.y_ref, bf16[512,1280]{1,0:T(8,128)(2,1)S(1)} %open_gate.1.z_ref, bf16[512,256]{1,0:T(8,128)(2,1)} %get-tuple-element.29.bc_ref, f32[512,128]{1,0:T(8,128)S(1)} %get-tuple-element.30.cum_ref, ...), custom_call_target="tpu_custom_call" | custom-call | tf_op jit(solution)/shard_map/gate/pallas_call | solution.py:532
  71.4 3.0 %collective-permute-start.2 = (bf16[256,640]{1,0:T(8,128)(2,1)}, bf16[256,640]{1,0:T(8,128)(2,1)S(1)}, u32[]{:S(2)}, u32[]{:S(2)}) collective-permute-start(bf16[256,640]{1,0:T(8,128)(2,1)} %get-tuple-element.36), channel_id=1, source_target_pairs={{0,1},{1,0},{2,3},{3,2},{4,5},{5,4},{6,7},{7,6},{8,9},{9,8},{10,11... | collective-permute-start | bytes 983048 | tf_op jit(solution)/shard_map/ppermute | solution.py:617
  74.4 2.9 %project.3 = f32[256,640]{1,0:T(8,128)S(1)} custom-call(s32[1]{0:T(128)} %bitcast.1.q_ref, bf16[256,2560]{1,0:T(8,128)(2,1)S(1)} %get-tuple-element.37.g_ref, bf16[1280,2560]{1,0:T(8,128)(2,1)} %w_ref.7), custom_call_target="tpu_custom_call" | custom-call | flops 838860800 | bytes 5242880 | tf_op jit(solution)/shard_map/project/pallas_call | solution.py:573
  77.4 0.1 add_convert_fusion.1
  77.4 2.9 %project.4 = bf16[256,640]{1,0:T(8,128)(2,1)S(1)} custom-call(s32[1]{0:T(128)} %bitcast.10.q_ref, bf16[256,2560]{1,0:T(8,128)(2,1)S(1)} %get-tuple-element.37.g_ref, bf16[1280,2560]{1,0:T(8,128)(2,1)} %w_ref.7), custom_call_target="tpu_custom_call" | custom-call | flops 838860800 | bytes 5242880 | tf_op jit(solution)/shard_map/project/pallas_call | solution.py:573
  80.4 0.1 collective-permute-start.3
  80.5 2.8 %collective-permute-start.4 = (bf16[256,640]{1,0:T(8,128)(2,1)S(1)}, bf16[256,640]{1,0:T(8,128)(2,1)S(1)}, u32[]{:S(2)}, u32[]{:S(2)}) collective-permute-start(bf16[256,640]{1,0:T(8,128)(2,1)S(1)} %add_convert_fusion.1), channel_id=1, source_target_pairs={{0,2},{2,0},{1,3},{3,1},{4,6},{6,4},{5,7},{7,5},{8,10},{10,8},{9,1... | collective-permute-start | bytes 983048 | tf_op jit(solution)/shard_map/ppermute | solution.py:621
  83.3 1.0 %constant_dynamic-slice_fusion.rest_1_ = bf16[256,640]{1,0:T(8,128)(2,1)S(1)} fusion(bf16[256,2560]{1,0:T(8,128)(2,1)} %h_ref.1, s32[]{:T(128)S(6)} %select_n.21), kind=kLoop, calls=%fused_computation.2 | loop fusion | bytes 655364 | tf_op jit(solution)/shard_map/dynamic_slice | solution.py:625
  84.3 3.0 %project.5 = f32[256,640]{1,0:T(8,128)S(1)} custom-call(s32[1]{0:T(128)} %bitcast.q_ref, bf16[256,2560]{1,0:T(8,128)(2,1)S(1)} %get-tuple-element.37.g_ref, bf16[1280,2560]{1,0:T(8,128)(2,1)} %w_ref.7, bf16[256,640]{1,0:T(8,128)(2,1)S(1)} %collective-permute-done.3.rest_0_, bf16[256,640]{1,0:T(8,128)(2,1)S(1)} %constant_dynamic-slice_fusion.rest_1_), custom_call_target="tpu_custom_call" | custom-call | flops 838860800 | bytes 5242880 | tf_op jit(solution)/shard_map/project/pallas_call | solution.py:573
  87.3 3.7 %collective-permute-done.4 = bf16[256,640]{1,0:T(8,128)(2,1)S(1)} collective-permute-done((bf16[256,640]{1,0:T(8,128)(2,1)S(1)}, bf16[256,640]{1,0:T(8,128)(2,1)S(1)}, u32[]{:S(2)}, u32[]{:S(2)}) %collective-permute-start.4) | collective-permute-done | bytes 327712 | tf_op jit(solution)/shard_map/ppermute | solution.py:621
  90.9 0.8 add_convert_fusion
  (5 shorter events, 0.0 us)
Async XLA Ops:
  0.9 11.3 %collective-permute-start = (bf16[16,2560]{1,0:T(8,128)(2,1)S(1)}, bf16[16,2560]{1,0:T(8,128)(2,1)S(1)}, u32[]{:S(2)}, u32[]{:S(2)}) collective-permute-start(bf16[16,2560]{1,0:T(8,128)(2,1)S(1)} %get-tuple-element.40), channel_id=1, source_target_pairs={{0,4},{4,8},{8,12},{12,16},{16,20},{20,24},{24,28},{28,32},{32,36}... | collective-permute-start | bytes 245768 | tf_op jit(solution)/shard_map/ppermute | solution.py:595
  4.9 7.4 %collective-permute-start.1 = (bf16[16,2560]{1,0:T(8,128)(2,1)S(1)}, bf16[16,2560]{1,0:T(8,128)(2,1)S(1)}, u32[]{:S(2)}, u32[]{:S(2)}) collective-permute-start(bf16[16,2560]{1,0:T(8,128)(2,1)S(1)} %get-tuple-element.39), channel_id=1, source_target_pairs={{4,0},{8,4},{12,8},{16,12},{20,16},{24,20},{28,24},{32,28},{36,32}... | collective-permute-start | bytes 245768 | tf_op jit(solution)/shard_map/ppermute | solution.py:596
  12.2 10.5 %copy-start = (bf16[512,2560]{1,0:T(8,128)(2,1)}, bf16[512,2560]{1,0:T(8,128)(2,1)S(1)}, u32[]{:S(2)}) copy-start(bf16[512,2560]{1,0:T(8,128)(2,1)S(1)} %get-tuple-element.22.x_ref) | copy-start | bytes 7864324
  22.8 22.6 %all-to-all-start = ((bf16[32,88,128]{2,1,0:T(8,128)(2,1)}), bf16[32,88,128]{2,1,0:T(8,128)(2,1)S(1)}, u32[]{:S(2)}, u32[]{:S(2)}) async-start(bf16[32,88,128]{2,1,0:T(8,128)(2,1)} %get-tuple-element.27), calls=%async_computation | async-start | bytes 1441792 | tf_op jit(solution)/shard_map/all_to_all | solution.py:604
  47.5 16.2 %all-to-all-start.1 = ((bf16[32,80,128]{2,1,0:T(8,128)(2,1)}), bf16[32,80,128]{2,1,0:T(8,128)(2,1)S(1)}, u32[]{:S(2)}, u32[]{:S(2)}) async-start(bf16[32,80,128]{2,1,0:T(8,128)(2,1)} %scan.1), calls=%async_computation.1 | async-start | bytes 1310720 | tf_op jit(solution)/shard_map/all_to_all | solution.py:608
  71.4 6.0 %collective-permute-start.2 = (bf16[256,640]{1,0:T(8,128)(2,1)}, bf16[256,640]{1,0:T(8,128)(2,1)S(1)}, u32[]{:S(2)}, u32[]{:S(2)}) collective-permute-start(bf16[256,640]{1,0:T(8,128)(2,1)} %get-tuple-element.36), channel_id=1, source_target_pairs={{0,1},{1,0},{2,3},{3,2},{4,5},{5,4},{6,7},{7,6},{8,9},{9,8},{10,11... | collective-permute-start | bytes 983048 | tf_op jit(solution)/shard_map/ppermute | solution.py:617
  80.4 3.9 %collective-permute-start.3 = (bf16[256,640]{1,0:T(8,128)(2,1)S(1)}, bf16[256,640]{1,0:T(8,128)(2,1)S(1)}, u32[]{:S(2)}, u32[]{:S(2)}) collective-permute-start(bf16[256,640]{1,0:T(8,128)(2,1)S(1)} %project.4), channel_id=1, source_target_pairs={{0,1},{1,0},{2,3},{3,2},{4,5},{5,4},{6,7},{7,6},{8,9},{9,8},{10,11... | collective-permute-start | bytes 983048 | tf_op jit(solution)/shard_map/ppermute | solution.py:623
  80.5 10.4 %collective-permute-start.4 = (bf16[256,640]{1,0:T(8,128)(2,1)S(1)}, bf16[256,640]{1,0:T(8,128)(2,1)S(1)}, u32[]{:S(2)}, u32[]{:S(2)}) collective-permute-start(bf16[256,640]{1,0:T(8,128)(2,1)S(1)} %add_convert_fusion.1), channel_id=1, source_target_pairs={{0,2},{2,0},{1,3},{3,1},{4,6},{6,4},{5,7},{7,5},{8,10},{10,8},{9,1... | collective-permute-start | bytes 983048 | tf_op jit(solution)/shard_map/ppermute | solution.py:621

commit v6 on v5

--- a/solution.py
+++ b/solution.py
@@ -12,7 +12,7 @@
 HALO = 16
 EXTRA = 32
 CHUNK = 64
-FETCHES = 5
+DEPTHS = 5
 TILE = 256
 LANES = 128
 epsilon = 1e-05
@@ -98,9 +98,7 @@
     rows, width = h_ref.shape
     heads = dtb_ref.shape[1]
     copies = [pltpu.make_async_copy(bcw_ref, bcw_kept, sems.at[0])]
-    for k in range(FETCHES):
-        part = slice(k * width // FETCHES, (k + 1) * width // FETCHES)
-        copies.append(pltpu.make_async_copy(xw_ref.at[part], xw_kept.at[part], sems.at[1 + k]))
+    copies.append(pltpu.make_async_copy(xw_ref.at[:, :TILE], xw_kept, sems.at[1]))
     for copy in copies:
         copy.start()
 
@@ -171,15 +169,15 @@
             jax.ShapeDtypeStruct((2, 24, rows), f32),
             jax.ShapeDtypeStruct((2 * rows, 2 * LANES), bf16),
             jax.ShapeDtypeStruct((8, LANES), f32),
-            jax.ShapeDtypeStruct(xw.shape, bf16),
+            jax.ShapeDtypeStruct((width, TILE), bf16),
             jax.ShapeDtypeStruct(bcw.shape, bf16),
         ],
         scratch_shapes=[
             pltpu.VMEM((rows, width), bf16),
             pltpu.VMEM((LANES, width), bf16),
-            pltpu.SemaphoreType.DMA((1 + FETCHES,)),
-        ],
-        compiler_params=pltpu.CompilerParams(vmem_limit_bytes=28 << 20),
+            pltpu.SemaphoreType.DMA((2,)),
+        ],
+        compiler_params=pltpu.CompilerParams(vmem_limit_bytes=20 << 20),
         cost_estimate=pl.CostEstimate(flops=4 << 30, bytes_accessed=5 << 20, transcendentals=0),
         name="norm",
     )(
@@ -188,9 +186,9 @@
 
 
 def entry_kernel(
-    x_ref, prev_ref, next_ref, gain_ref, xw_ref, bcw_ref, xk_ref, bck_ref, wend_ref, dec_ref,
+    x_ref, prev_ref, next_ref, gain_ref, first_ref, bcw_ref, xk_ref, bck_ref, wend_ref, dec_ref, xw_hbm,
     xconv_ref, bc_ref, pay_ref,
-    ext_ref, xin_ref, bcin_ref, st_ref, bt_ref, rim_ref, weighted_ref,
+    ext_ref, xin_ref, bcin_ref, bt_ref, rim_ref, weighted_ref, acc_ref, reach_ref, xw_ref, sems,
 ):
     width = x_ref.shape[1]
     rows = x_ref.shape[0] // 2
@@ -226,60 +224,95 @@
         ext_ref[:EXTRA] = mm(ahead, rim_ref[0]).astype(bf16)
         ext_ref[EXTRA + 2 * rows :] = mm(behind, rim_ref[1]).astype(bf16)
         bcin_ref[...] = mm(ext_ref[...], bcw_ref[...]).astype(bf16).astype(f32)
+
+    def bc_piece(d, first):
+        at = slice(d * rows + first, d * rows + first + CHUNK)
+        bc_ref[at] = conv_rows(bcin_ref, bck_ref[...], d, rows, first, CHUNK)
+
+    def x_piece(d, first):
+        at = slice(d * rows + first, d * rows + first + CHUNK)
+        conv = conv_rows(xin_ref, xk_ref[...], d, rows, first, CHUNK)
+        xconv_ref[at] = conv
+        weighted_ref[at] = (conv.astype(f32) * reach_ref[at]).astype(bf16)
+
+    def states(d):
+        part = mm(bt_ref[d], weighted_ref[d * rows : (d + 1) * rows]).astype(bf16)
+        for g in range(TILE // LANES):
+            group = d * steps * (TILE // LANES) + (n - 1) * (TILE // LANES) + g
+            q, j = group // 5, group % 5
+            at = pl.ds(pl.multiple_of(16 * j, 16), 16)
+            for i in range(STATE // 16):
+                pay_ref[4 * i + q, at] = part[16 * i : 16 * i + 16, g * LANES : (g + 1) * LANES]
+
+    def product(k, weight):
+        depth = width // DEPTHS
+        at = slice(k * depth, (k + 1) * depth)
+        part = mm(ext_ref[:, at], weight(at))
+        if k == 0:
+            acc_ref[...] = part
+        elif k < DEPTHS - 1:
+            acc_ref[...] += part
+        else:
+            xin_ref[...] = (acc_ref[...] + part).astype(bf16).astype(f32)
+
+    def reach():
+        reach_ref[...] = mm(wend_ref[...], spread((n - 1) * (TILE // HEAD_DIM), TILE))
+
+    def fetch(tile):
+        at = pl.multiple_of(tile * TILE, TILE)
+        return pltpu.make_async_copy(
+            xw_hbm.at[:, pl.ds(at + TILE, TILE)], xw_ref.at[:, pl.ds(at, TILE)], sems.at[tile]
+        )
+
+    pieces = [(d, first) for d in range(2) for first in range(0, rows, CHUNK)]
+
+    @pl.when(n == 0)
+    def _():
+        for tile in range(xw_ref.shape[1] // TILE):
+            fetch(tile).start()
+        prelude()
+        weight = lambda at: first_ref[at]
+        for k in range(DEPTHS - 1):
+            product(k, weight)
+            for piece in pieces[2 * k : 2 * k + 2]:
+                bc_piece(*piece)
+        product(DEPTHS - 1, weight)
         for d in range(2):
-            for first in range(0, rows, CHUNK):
-                at = slice(d * rows + first, d * rows + first + CHUNK)
-                bc_ref[at] = conv_rows(bcin_ref, bck_ref[...], d, rows, first, CHUNK)
             at = slice(d * rows, (d + 1) * rows)
             bt_ref[d] = jnp.transpose(bc_ref[at, :STATE].astype(f32)).astype(bf16)
-
-    def product():
-        column = pl.multiple_of(jnp.minimum(n, steps - 1) * TILE, TILE)
-        return mm(ext_ref[...], xw_ref[:, pl.ds(column, TILE)]).astype(bf16).astype(f32)
-
-    def finish():
-        tile = n - 1
-        spread_n = spread(tile * (TILE // HEAD_DIM), TILE)
-        for d in range(2):
-            for first in range(0, rows, CHUNK):
-                at = slice(d * rows + first, d * rows + first + CHUNK)
-                conv = conv_rows(xin_ref, xk_ref[...], d, rows, first, CHUNK)
-                xconv_ref[at] = conv
-                weighted_ref[at] = (conv.astype(f32) * mm(wend_ref[at], spread_n)).astype(bf16)
-            column = pl.multiple_of(d * steps * TILE + tile * TILE, TILE)
-            st_ref[:, pl.ds(column, TILE)] = mm(
-                bt_ref[d], weighted_ref[d * rows : (d + 1) * rows]
-            ).astype(bf16)
-
-    @pl.when(n == 0)
-    def _():
-        prelude()
-        xin_ref[...] = product()
-
-    @pl.when((n > 0) & (n < steps))
-    def _():
-        finish()
-        xin_ref[...] = product()
-
-    @pl.when(n == steps)
-    def _():
-        finish()
-        slots = pay_ref.shape[0]
         row = iota((8, LANES), 0)
-        tails = []
         for d in range(2):
             dec = jnp.broadcast_to(dec_ref[d : d + 1], (8, LANES))
             hi = dec.astype(bf16).astype(f32)
-            tails.append(jnp.where(row == 0, hi, jnp.where(row == 1, dec - hi, 0.0)).astype(bf16))
-        for slot in range(slots):
-            i, q = slot // 4, slot % 4
-            for j in range(5):
-                column = (5 * q + j) * LANES
-                pay_ref[slot, 16 * j : 16 * j + 16] = st_ref[16 * i : 16 * i + 16, column : column + LANES]
-            pay_ref[slot, 80:88] = tails[q // 2]
-
-
-def entry(x, prev_rows, next_rows, gain, xw, bcw, xk, bck, wend, dec, slots):
+            tail = jnp.where(row == 0, hi, jnp.where(row == 1, dec - hi, 0.0)).astype(bf16)
+            for slot in range(pay_ref.shape[0]):
+                if slot % 4 // 2 == d:
+                    pay_ref[slot, 80:88] = tail
+
+    @pl.when((n > 0) & (n < steps))
+    def _():
+        fetch(n - 1).wait()
+        column = pl.multiple_of((n - 1) * TILE, TILE)
+        weight = lambda at: xw_ref[at, pl.ds(column, TILE)]
+        reach()
+        for k in range(DEPTHS - 1):
+            product(k, weight)
+            for piece in pieces[2 * k : 2 * k + 2]:
+                x_piece(*piece)
+            if k % 2 == 1:
+                states(k // 2)
+        product(DEPTHS - 1, weight)
+
+    @pl.when(n == steps)
+    def _():
+        reach()
+        for piece in pieces:
+            x_piece(*piece)
+        for d in range(2):
+            states(d)
+
+
+def entry(x, prev_rows, next_rows, gain, first, bcw, xk, bck, wend, dec, xw, slots):
     width = x.shape[1]
     rows = x.shape[0] // 2
     inner = xw.shape[1]
@@ -297,7 +330,7 @@
             vmem, vmem, vmem, once(width // LANES, LANES),
             vmem, vmem,
             pl.BlockSpec((4, TILE), lambda n: (0, behind(n))),
-            once(4, 2 * STATE), vmem, vmem,
+            once(4, 2 * STATE), vmem, vmem, pl.BlockSpec(memory_space=pltpu.HBM),
         ],
         out_specs=[
             pl.BlockSpec((2 * rows, TILE), lambda n: (0, behind(n))),
@@ -312,10 +345,13 @@
             pltpu.VMEM((2 * rows + 2 * EXTRA, width), bf16),
             pltpu.VMEM((2 * rows + 2 * EXTRA, TILE), f32),
             pltpu.VMEM((2 * rows + 2 * EXTRA, TILE), f32),
-            pltpu.VMEM((STATE, 2 * inner), bf16),
             pltpu.VMEM((2, STATE, rows), bf16),
             pltpu.VMEM((2, EXTRA + HALO, width), bf16),
             pltpu.VMEM((2 * rows, TILE), bf16),
+            pltpu.VMEM((2 * rows + 2 * EXTRA, TILE), f32),
+            pltpu.VMEM((2 * rows, TILE), f32),
+            pltpu.VMEM((width, inner - TILE), bf16),
+            pltpu.SemaphoreType.DMA((inner // TILE - 1,)),
         ],
         compiler_params=pltpu.CompilerParams(
             dimension_semantics=("arbitrary",), vmem_limit_bytes=26 << 20
@@ -324,7 +360,7 @@
             flops=2 * 544 * width * (inner + 256), bytes_accessed=12 << 20, transcendentals=0
         ),
         name="entry",
-    )(x, prev_rows, next_rows, off_chip(gain), xw, bcw, off_chip(xk), off_chip(bck), wend, dec)
+    )(x, prev_rows, next_rows, off_chip(gain), first, bcw, off_chip(xk), off_chip(bck), wend, dec, off_chip(xw))
 
 
 def open_gate_kernel(x_ref, zw_ref, z_ref):
@@ -599,7 +635,8 @@
         hidden, gain, dt_weight.T, dt_bias[None], log_rate[None], x_weight, bc_weight
     )
     xconv, bc, pay = entry(
-        normed, prev_rows, next_rows, gain, x_kept, bc_kept, x_kernel, bc_kernel, wend, dec, blocks
+        normed, prev_rows, next_rows, gain, x_kept, bc_kept, x_kernel, bc_kernel, wend, dec,
+        x_weight, blocks,
     )
     pay = lax.all_to_all(pay, "ctx", 0, 0, tiled=True)
     y = within(xconv, bc, cum, cumt, delta)

time: 92.5 us -> 91.2 us (0.986)
  Pallas kernels: 52 us -> 50.6 us
    pallas_call x1, Pallas kernels: 10.5 us -> 9.53 us  [entry(): pl.pallas_call(entry_kernel, grid=(steps + 1,), in_specs=[vmem, vmem, vme...]
where the time goes in v6:
time: 91.2 us; the launch traced here: 90.4 us
  Pallas kernels  50.6 us (55%)
  starting transfers between devices  25.4 us (28%)
  waiting for transfers between devices  11.3 us (12%)
  local copies, waits for them, and re-layouts  1.94 us (2%)
    all_to_all x1, starting transfers between devices, per_device(): pay = lax.all_to_all(pay, 'ctx', 0, 0, tiled=True)  9.86 us
    pallas_call x1, Pallas kernels, entry(): pl.pallas_call(entry_kernel, grid=(steps + 1,), in_specs=[vmem, vmem, vme...  9.53 us
    pallas_call x1, Pallas kernels, within(): pl.pallas_call(within_kernel, grid=(2, inner // TILE), in_specs=[pl.Block...  9.37 us
    pallas_call x3, Pallas kernels, project(): pl.pallas_call(functools.partial(project_kernel, len(adds)), in_specs=[pl...  8.84 us
    pallas_call x1, Pallas kernels, gate(): pl.pallas_call(gate_kernel, grid_spec=pltpu.PrefetchScalarGridSpec(num_sc...  7.68 us
    pallas_call x1, Pallas kernels, open_gate(): pl.pallas_call(open_gate_kernel, grid=(inner // TILE,), in_specs=[fixed(h...  7.45 us
    pallas_call x1, Pallas kernels, norm(): pl.pallas_call(norm_kernel, grid=(1,), in_specs=[fixed(rows, width), fixe...  5.63 us
    all_to_all x1, starting transfers between devices, per_device(): state = lax.all_to_all(state, 'ctx', 0, 0, tiled=True)  4.39 us
  transfers between devices with their start and end apart: 7, of which 3 were waited for; matrix products, arithmetic and copies ran while one was open for 1% of the time, Pallas kernels for 31%

profile of v6, /device:TPU:1, one launch (start us, length us, event | category | flops | bytes accessed | tf_op | source)
XLA Modules:
  0.0 90.4 jit_solution(10310749382931089969)
XLA Ops:
  0.0 0.9 %fusion = (bf16[16,2560]{1,0:T(8,128)(2,1)S(1)}, bf16[16,2560]{1,0:T(8,128)(2,1)S(1)}) fusion(bf16[256,2560]{1,0:T(8,128)(2,1)} %h_ref.1), kind=kLoop, calls=%fused_computation.3 | loop fusion | bytes 327680 | tf_op jit(solution)/shard_map/slice | solution.py:632
  0.9 3.9 %collective-permute-start = (bf16[16,2560]{1,0:T(8,128)(2,1)S(1)}, bf16[16,2560]{1,0:T(8,128)(2,1)S(1)}, u32[]{:S(2)}, u32[]{:S(2)}) collective-permute-start(bf16[16,2560]{1,0:T(8,128)(2,1)S(1)} %get-tuple-element.40), channel_id=1, source_target_pairs={{0,4},{4,8},{8,12},{12,16},{16,20},{20,24},{24,28},{28,32},{32,36}... | collective-permute-start | bytes 245768 | tf_op jit(solution)/shard_map/ppermute | solution.py:631
  4.9 1.3 %collective-permute-start.1 = (bf16[16,2560]{1,0:T(8,128)(2,1)S(1)}, bf16[16,2560]{1,0:T(8,128)(2,1)S(1)}, u32[]{:S(2)}, u32[]{:S(2)}) collective-permute-start(bf16[16,2560]{1,0:T(8,128)(2,1)S(1)} %get-tuple-element.39), channel_id=1, source_target_pairs={{4,0},{8,4},{12,8},{16,12},{20,16},{24,20},{28,24},{32,28},{36,32}... | collective-permute-start | bytes 245768 | tf_op jit(solution)/shard_map/ppermute | solution.py:632
  6.2 5.6 %norm.1 = (bf16[512,2560]{1,0:T(8,128)(2,1)S(1)}, f32[512,128]{1,0:T(8,128)S(1)}, f32[512,128]{1,0:T(8,128)S(1)}, f32[2,24,256]{2,1,0:T(8,128)S(1)}, bf16[512,25...) custom-call(bf16[256,2560]{1,0:T(8,128)(2,1)} %h_ref.1, ...), custom_call_target="tpu_custom_call" | custom-call | flops 4294967296 | bytes 5242880 | tf_op jit(solution)/shard_map/norm/pallas_call | solution.py:152
  11.8 0.0 collective-permute-done.prev_ref
  11.9 9.5 %entry.1 = (bf16[512,1280]{1,0:T(8,128)(2,1)}, bf16[512,256]{1,0:T(8,128)(2,1)}, bf16[32,88,128]{2,1,0:T(8,128)(2,1)}) custom-call(bf16[512,2560]{1,0:T(8,128)(2,1)S(1)} %get-tuple-element.22.x_ref, bf16[16,2560]{1,0:T(8,128)(2,1)S(1)} %collective-permute-done.prev_ref, bf16[16,2560]{1,0:T(8,128)(2,1)S(1)} %collective-permute-done.1.next_ref, ...), custom_call_target="tpu_custom_call" | custom-call | flops 4278190080 | bytes 12582912 | tf_op jit(solution)/shard_map/entry/pallas_call | solution.py:326
  21.4 9.9 %all-to-all-start = ((bf16[32,88,128]{2,1,0:T(8,128)(2,1)}), bf16[32,88,128]{2,1,0:T(8,128)(2,1)S(1)}, u32[]{:S(2)}, u32[]{:S(2)}) async-start(bf16[32,88,128]{2,1,0:T(8,128)(2,1)} %get-tuple-element.27), calls=%async_computation | async-start | bytes 1441792 | tf_op jit(solution)/shard_map/all_to_all | solution.py:641
  31.3 9.4 %within.1.y_ref = bf16[512,1280]{1,0:T(8,128)(2,1)} custom-call(bf16[512,1280]{1,0:T(8,128)(2,1)} %get-tuple-element.28.x_ref, bf16[512,256]{1,0:T(8,128)(2,1)} %get-tuple-element.29.bc_ref, f32[512,128]{1,0:T(8,128)S(1)} %get-tuple-element.30.cum_ref, f32[2,24,256]{2,1,0:T(8,128)S(1)} %get-tuple-element.31.cumt_ref, f32[512,128]{1,0:T(8,128)S(1)} %get-tuple-element.32.delta_ref), custom_call_target="tpu_custom_call" | custom-call | flops 3221225472 | bytes 5242880 | tf_op jit(solution)/shard_map/within/pallas_call | solution.py:418
  40.7 3.3 %all-to-all-done.pay_ref = bf16[32,88,128]{2,1,0:T(8,128)(2,1)S(1)} async-done(((bf16[32,88,128]{2,1,0:T(8,128)(2,1)}), bf16[32,88,128]{2,1,0:T(8,128)(2,1)S(1)}, u32[]{:S(2)}, u32[]{:S(2)}) %all-to-all-start) | async-done | bytes 720928 | tf_op jit(solution)/shard_map/all_to_all | solution.py:641
  44.0 2.1 %scan.1 = bf16[32,80,128]{2,1,0:T(8,128)(2,1)} custom-call(s32[1]{0:T(128)} %bitcast.7.q_ref, bf16[32,88,128]{2,1,0:T(8,128)(2,1)S(1)} %all-to-all-done.pay_ref), custom_call_target="tpu_custom_call" | custom-call | tf_op jit(solution)/shard_map/scan/pallas_call | solution.py:471
  46.1 4.4 %all-to-all-start.1 = ((bf16[32,80,128]{2,1,0:T(8,128)(2,1)}), bf16[32,80,128]{2,1,0:T(8,128)(2,1)S(1)}, u32[]{:S(2)}, u32[]{:S(2)}) async-start(bf16[32,80,128]{2,1,0:T(8,128)(2,1)} %scan.1), calls=%async_computation.1 | async-start | bytes 1310720 | tf_op jit(solution)/shard_map/all_to_all | solution.py:645
  50.5 7.5 %open_gate.1.z_ref = bf16[512,1280]{1,0:T(8,128)(2,1)S(1)} custom-call(bf16[512,2560]{1,0:T(8,128)(2,1)} %copy-done, bf16[2560,1280]{1,0:T(8,128)(2,1)} %zw_ref.1), custom_call_target="tpu_custom_call" | custom-call | flops 3355443200 | bytes 16777216 | tf_op jit(solution)/shard_map/open_gate/pallas_call | solution.py:374
  58.0 4.3 %all-to-all-done.1 = bf16[32,80,128]{2,1,0:T(8,128)(2,1)S(1)} async-done(((bf16[32,80,128]{2,1,0:T(8,128)(2,1)}), bf16[32,80,128]{2,1,0:T(8,128)(2,1)S(1)}, u32[]{:S(2)}, u32[]{:S(2)}) %all-to-all-start.1) | async-done | bytes 655392 | tf_op jit(solution)/shard_map/all_to_all | solution.py:645
  62.3 7.7 %gate.1 = (bf16[256,2560]{1,0:T(8,128)(2,1)S(1)}, bf16[256,640]{1,0:T(8,128)(2,1)}) custom-call(s32[1]{0:T(128)} %bitcast.2.target_ref, bf16[512,1280]{1,0:T(8,128)(2,1)} %within.1.y_ref, bf16[512,1280]{1,0:T(8,128)(2,1)S(1)} %open_gate.1.z_ref, bf16[512,256]{1,0:T(8,128)(2,1)} %get-tuple-element.29.bc_ref, f32[512,128]{1,0:T(8,128)S(1)} %get-tuple-element.30.cum_ref, ...), custom_call_target="tpu_custom_call" | custom-call | tf_op jit(solution)/shard_map/gate/pallas_call | solution.py:568
  70.0 3.0 %collective-permute-start.2 = (bf16[256,640]{1,0:T(8,128)(2,1)}, bf16[256,640]{1,0:T(8,128)(2,1)S(1)}, u32[]{:S(2)}, u32[]{:S(2)}) collective-permute-start(bf16[256,640]{1,0:T(8,128)(2,1)} %get-tuple-element.36), channel_id=1, source_target_pairs={{0,1},{1,0},{2,3},{3,2},{4,5},{5,4},{6,7},{7,6},{8,9},{9,8},{10,11... | collective-permute-start | bytes 983048 | tf_op jit(solution)/shard_map/ppermute | solution.py:654
  73.1 2.9 %project.3 = f32[256,640]{1,0:T(8,128)S(1)} custom-call(s32[1]{0:T(128)} %bitcast.1.q_ref, bf16[256,2560]{1,0:T(8,128)(2,1)S(1)} %get-tuple-element.37.g_ref, bf16[1280,2560]{1,0:T(8,128)(2,1)} %w_ref.7), custom_call_target="tpu_custom_call" | custom-call | flops 838860800 | bytes 5242880 | tf_op jit(solution)/shard_map/project/pallas_call | solution.py:609
  76.0 0.1 add_convert_fusion.1
  76.1 2.9 %project.4 = bf16[256,640]{1,0:T(8,128)(2,1)S(1)} custom-call(s32[1]{0:T(128)} %bitcast.10.q_ref, bf16[256,2560]{1,0:T(8,128)(2,1)S(1)} %get-tuple-element.37.g_ref, bf16[1280,2560]{1,0:T(8,128)(2,1)} %w_ref.7), custom_call_target="tpu_custom_call" | custom-call | flops 838860800 | bytes 5242880 | tf_op jit(solution)/shard_map/project/pallas_call | solution.py:609
  79.0 0.1 collective-permute-start.3
  79.1 2.8 %collective-permute-start.4 = (bf16[256,640]{1,0:T(8,128)(2,1)S(1)}, bf16[256,640]{1,0:T(8,128)(2,1)S(1)}, u32[]{:S(2)}, u32[]{:S(2)}) collective-permute-start(bf16[256,640]{1,0:T(8,128)(2,1)S(1)} %add_convert_fusion.1), channel_id=1, source_target_pairs={{0,2},{2,0},{1,3},{3,1},{4,6},{6,4},{5,7},{7,5},{8,10},{10,8},{9,1... | collective-permute-start | bytes 983048 | tf_op jit(solution)/shard_map/ppermute | solution.py:658
  81.9 1.0 %constant_dynamic-slice_fusion.rest_1_ = bf16[256,640]{1,0:T(8,128)(2,1)S(1)} fusion(bf16[256,2560]{1,0:T(8,128)(2,1)} %h_ref.1, s32[]{:T(128)S(6)} %select_n.21), kind=kLoop, calls=%fused_computation.2 | loop fusion | bytes 655364 | tf_op jit(solution)/shard_map/dynamic_slice | solution.py:662
  83.0 3.0 %project.5 = f32[256,640]{1,0:T(8,128)S(1)} custom-call(s32[1]{0:T(128)} %bitcast.q_ref, bf16[256,2560]{1,0:T(8,128)(2,1)S(1)} %get-tuple-element.37.g_ref, bf16[1280,2560]{1,0:T(8,128)(2,1)} %w_ref.7, bf16[256,640]{1,0:T(8,128)(2,1)S(1)} %collective-permute-done.3.rest_0_, bf16[256,640]{1,0:T(8,128)(2,1)S(1)} %constant_dynamic-slice_fusion.rest_1_), custom_call_target="tpu_custom_call" | custom-call | flops 838860800 | bytes 5242880 | tf_op jit(solution)/shard_map/project/pallas_call | solution.py:609
  85.9 3.7 %collective-permute-done.4 = bf16[256,640]{1,0:T(8,128)(2,1)S(1)} collective-permute-done((bf16[256,640]{1,0:T(8,128)(2,1)S(1)}, bf16[256,640]{1,0:T(8,128)(2,1)S(1)}, u32[]{:S(2)}, u32[]{:S(2)}) %collective-permute-start.4) | collective-permute-done | bytes 327712 | tf_op jit(solution)/shard_map/ppermute | solution.py:658
  89.6 0.8 add_convert_fusion
  (5 shorter events, 0.0 us)
Async XLA Ops:
  0.9 10.9 %collective-permute-start = (bf16[16,2560]{1,0:T(8,128)(2,1)S(1)}, bf16[16,2560]{1,0:T(8,128)(2,1)S(1)}, u32[]{:S(2)}, u32[]{:S(2)}) collective-permute-start(bf16[16,2560]{1,0:T(8,128)(2,1)S(1)} %get-tuple-element.40), channel_id=1, source_target_pairs={{0,4},{4,8},{8,12},{12,16},{16,20},{20,24},{24,28},{28,32},{32,36}... | collective-permute-start | bytes 245768 | tf_op jit(solution)/shard_map/ppermute | solution.py:631
  4.9 7.0 %collective-permute-start.1 = (bf16[16,2560]{1,0:T(8,128)(2,1)S(1)}, bf16[16,2560]{1,0:T(8,128)(2,1)S(1)}, u32[]{:S(2)}, u32[]{:S(2)}) collective-permute-start(bf16[16,2560]{1,0:T(8,128)(2,1)S(1)} %get-tuple-element.39), channel_id=1, source_target_pairs={{4,0},{8,4},{12,8},{16,12},{20,16},{24,20},{28,24},{32,28},{36,32}... | collective-permute-start | bytes 245768 | tf_op jit(solution)/shard_map/ppermute | solution.py:632
  11.8 9.6 %copy-start = (bf16[512,2560]{1,0:T(8,128)(2,1)}, bf16[512,2560]{1,0:T(8,128)(2,1)S(1)}, u32[]{:S(2)}) copy-start(bf16[512,2560]{1,0:T(8,128)(2,1)S(1)} %get-tuple-element.22.x_ref) | copy-start | bytes 7864324
  21.4 22.6 %all-to-all-start = ((bf16[32,88,128]{2,1,0:T(8,128)(2,1)}), bf16[32,88,128]{2,1,0:T(8,128)(2,1)S(1)}, u32[]{:S(2)}, u32[]{:S(2)}) async-start(bf16[32,88,128]{2,1,0:T(8,128)(2,1)} %get-tuple-element.27), calls=%async_computation | async-start | bytes 1441792 | tf_op jit(solution)/shard_map/all_to_all | solution.py:641
  46.1 16.2 %all-to-all-start.1 = ((bf16[32,80,128]{2,1,0:T(8,128)(2,1)}), bf16[32,80,128]{2,1,0:T(8,128)(2,1)S(1)}, u32[]{:S(2)}, u32[]{:S(2)}) async-start(bf16[32,80,128]{2,1,0:T(8,128)(2,1)} %scan.1), calls=%async_computation.1 | async-start | bytes 1310720 | tf_op jit(solution)/shard_map/all_to_all | solution.py:645
  70.0 6.0 %collective-permute-start.2 = (bf16[256,640]{1,0:T(8,128)(2,1)}, bf16[256,640]{1,0:T(8,128)(2,1)S(1)}, u32[]{:S(2)}, u32[]{:S(2)}) collective-permute-start(bf16[256,640]{1,0:T(8,128)(2,1)} %get-tuple-element.36), channel_id=1, source_target_pairs={{0,1},{1,0},{2,3},{3,2},{4,5},{5,4},{6,7},{7,6},{8,9},{9,8},{10,11... | collective-permute-start | bytes 983048 | tf_op jit(solution)/shard_map/ppermute | solution.py:654
  79.0 3.9 %collective-permute-start.3 = (bf16[256,640]{1,0:T(8,128)(2,1)S(1)}, bf16[256,640]{1,0:T(8,128)(2,1)S(1)}, u32[]{:S(2)}, u32[]{:S(2)}) collective-permute-start(bf16[256,640]{1,0:T(8,128)(2,1)S(1)} %project.4), channel_id=1, source_target_pairs={{0,1},{1,0},{2,3},{3,2},{4,5},{5,4},{6,7},{7,6},{8,9},{9,8},{10,11... | collective-permute-start | bytes 983048 | tf_op jit(solution)/shard_map/ppermute | solution.py:660
  79.1 10.4 %collective-permute-start.4 = (bf16[256,640]{1,0:T(8,128)(2,1)S(1)}, bf16[256,640]{1,0:T(8,128)(2,1)S(1)}, u32[]{:S(2)}, u32[]{:S(2)}) collective-permute-start(bf16[256,640]{1,0:T(8,128)(2,1)S(1)} %add_convert_fusion.1), channel_id=1, source_target_pairs={{0,2},{2,0},{1,3},{3,1},{4,6},{6,4},{5,7},{7,5},{8,10},{10,8},{9,1... | collective-permute-start | bytes 983048 | tf_op jit(solution)/shard_map/ppermute | solution.py:658

commit v7 on v6

--- a/solution.py
+++ b/solution.py
@@ -97,10 +97,20 @@
 ):
     rows, width = h_ref.shape
     heads = dtb_ref.shape[1]
-    copies = [pltpu.make_async_copy(bcw_ref, bcw_kept, sems.at[0])]
-    copies.append(pltpu.make_async_copy(xw_ref.at[:, :TILE], xw_kept, sems.at[1]))
-    for copy in copies:
-        copy.start()
+
+    def fetch(k):
+        part = pl.ds(pl.multiple_of(k * (width // DEPTHS), TILE), width // DEPTHS)
+        return (
+            pltpu.make_async_copy(bcw_ref.at[part], bcw_kept.at[part], sems.at[0, k]),
+            pltpu.make_async_copy(xw_ref.at[part, :TILE], xw_kept.at[part], sems.at[1, k]),
+        )
+
+    def start(k, _):
+        for copy in fetch(k):
+            copy.start()
+        return 0
+
+    lax.fori_loop(0, DEPTHS, start, 0)
 
     order = (iota((rows, rows), 1) == time_of(iota((rows, rows), 0), rows)).astype(bf16)
     flip = flip_matrix(TILE)
@@ -142,8 +152,9 @@
         wend_ref[at] = hi_lo(jnp.exp(jnp.minimum(last - cum, 0.0)) * delta[at])
         dec = jnp.where(iota((1, LANES), 1) < heads, jnp.exp(last), 0.0)
         dec_ref[d : d + 1] = dec
-    for copy in copies:
-        copy.wait()
+    for k in range(DEPTHS):
+        for copy in fetch(k):
+            copy.wait()
 
 
 def norm(hidden, gain, dtw, dtb, lr, xw, bcw):
@@ -175,7 +186,7 @@
         scratch_shapes=[
             pltpu.VMEM((rows, width), bf16),
             pltpu.VMEM((LANES, width), bf16),
-            pltpu.SemaphoreType.DMA((2,)),
+            pltpu.SemaphoreType.DMA((2, DEPTHS)),
         ],
         compiler_params=pltpu.CompilerParams(vmem_limit_bytes=20 << 20),
         cost_estimate=pl.CostEstimate(flops=4 << 30, bytes_accessed=5 << 20, transcendentals=0),
@@ -266,10 +277,13 @@
 
     pieces = [(d, first) for d in range(2) for first in range(0, rows, CHUNK)]
 
+    def start(tile, _):
+        fetch(tile).start()
+        return 0
+
     @pl.when(n == 0)
     def _():
-        for tile in range(xw_ref.shape[1] // TILE):
-            fetch(tile).start()
+        lax.fori_loop(0, xw_ref.shape[1] // TILE, start, 0)
         prelude()
         weight = lambda at: first_ref[at]
         for k in range(DEPTHS - 1):
@@ -439,7 +453,9 @@
 def scan_kernel(q_ref, pay_ref, out_ref, carry_ref, dec_ref):
     q = q_ref[0]
     half, turned = q % 2, q // 2
-    depth = pay_ref.shape[0]
+    depth = out_ref.shape[0]
+    step = pl.program_id(0)
+    base = depth * jnp.where(turned == 1, pl.num_programs(0) - 1 - step, step)
 
     @pl.when(pl.program_id(0) == 0)
     def _():
@@ -448,7 +464,7 @@
     first = half * (5 * LANES // HEAD_DIM)
     place = iota((LANES, 5 * LANES), 0) == first + iota((LANES, 5 * LANES), 1) // HEAD_DIM
     place = place.astype(bf16)
-    tails = pay_ref[:, 80:88].astype(f32).reshape(8 * depth, LANES).astype(bf16)
+    tails = pay_ref[pl.ds(base, depth), 80:88].astype(f32).reshape(8 * depth, LANES).astype(bf16)
     dec_ref[...] = mm(tails, place)
     carry = [carry_ref[16 * j : 16 * j + 16] for j in range(5)]
     for i in range(depth):
@@ -458,7 +474,7 @@
         for j in range(5):
             rows = slice(16 * j, 16 * j + 16)
             out_ref[at, rows] = carry[j].astype(bf16)
-            carry[j] = carry[j] * decay[:, j * LANES : (j + 1) * LANES] + pay_ref[at, rows].astype(f32)
+            carry[j] = carry[j] * decay[:, j * LANES : (j + 1) * LANES] + pay_ref[base + at, rows].astype(f32)
     for j in range(5):
         carry_ref[16 * j : 16 * j + 16] = carry[j]
 
@@ -473,7 +489,7 @@
         grid_spec=pltpu.PrefetchScalarGridSpec(
             num_scalar_prefetch=1,
             grid=(steps,),
-            in_specs=[pl.BlockSpec((depth, 88, LANES), chunk)],
+            in_specs=[pl.BlockSpec(memory_space=pltpu.VMEM)],
             out_specs=pl.BlockSpec((depth, 80, LANES), chunk),
             scratch_shapes=[pltpu.VMEM((80, LANES), f32), pltpu.VMEM((8 * depth, 5 * LANES), f32)],
         ),

time: 91.2 us -> 89.9 us (0.986)
  Pallas kernels: 50.6 us -> 48.8 us
    pallas_call x1, Pallas kernels: 5.63 us -> 4.15 us  [norm(): pl.pallas_call(norm_kernel, grid=(1,), in_specs=[fixed(rows, width), fixe...]
  transfers between devices with their start and end apart: 7 -> 7, of which waited for: 3 -> 3; matrix products, arithmetic and copies ran while one was open for 1% -> 1% of each run, Pallas kernels for 31% -> 30%
where the time goes in v7:
time: 89.9 us; the launch traced here: 89.1 us
  Pallas kernels  48.8 us (54%)
  starting transfers between devices  25.9 us (29%)
  waiting for transfers between devices  11.5 us (13%)
  local copies, waits for them, and re-layouts  1.94 us (2%)
    all_to_all x1, starting transfers between devices, per_device(): pay = lax.all_to_all(pay, 'ctx', 0, 0, tiled=True)  10.5 us
    pallas_call x1, Pallas kernels, within(): pl.pallas_call(within_kernel, grid=(2, inner // TILE), in_specs=[pl.Block...  9.37 us
    pallas_call x1, Pallas kernels, entry(): pl.pallas_call(entry_kernel, grid=(steps + 1,), in_specs=[vmem, vmem, vme...  9.16 us
    pallas_call x3, Pallas kernels, project(): pl.pallas_call(functools.partial(project_kernel, len(adds)), in_specs=[pl...  8.84 us
    pallas_call x1, Pallas kernels, gate(): pl.pallas_call(gate_kernel, grid_spec=pltpu.PrefetchScalarGridSpec(num_sc...  7.67 us
    pallas_call x1, Pallas kernels, open_gate(): pl.pallas_call(open_gate_kernel, grid=(inner // TILE,), in_specs=[fixed(h...  7.45 us
    all_to_all x1, starting transfers between devices, per_device(): state = lax.all_to_all(state, 'ctx', 0, 0, tiled=True)  4.42 us
    all_to_all x1, waiting for transfers between devices, per_device(): state = lax.all_to_all(state, 'ctx', 0, 0, tiled=True)  4.29 us
  transfers between devices with their start and end apart: 7, of which 3 were waited for; matrix products, arithmetic and copies ran while one was open for 1% of the time, Pallas kernels for 30%

profile of v7, /device:TPU:1, one launch (start us, length us, event | category | flops | bytes accessed | tf_op | source)
XLA Modules:
  0.0 89.1 jit_solution(14656026781263556074)
XLA Ops:
  0.0 0.9 %fusion = (bf16[16,2560]{1,0:T(8,128)(2,1)S(1)}, bf16[16,2560]{1,0:T(8,128)(2,1)S(1)}) fusion(bf16[256,2560]{1,0:T(8,128)(2,1)} %h_ref.1), kind=kLoop, calls=%fused_computation.3 | loop fusion | bytes 327680 | tf_op jit(solution)/shard_map/slice | solution.py:648
  0.9 3.9 %collective-permute-start = (bf16[16,2560]{1,0:T(8,128)(2,1)S(1)}, bf16[16,2560]{1,0:T(8,128)(2,1)S(1)}, u32[]{:S(2)}, u32[]{:S(2)}) collective-permute-start(bf16[16,2560]{1,0:T(8,128)(2,1)S(1)} %get-tuple-element.40), channel_id=1, source_target_pairs={{0,4},{4,8},{8,12},{12,16},{16,20},{20,24},{24,28},{28,32},{32,36}... | collective-permute-start | bytes 245768 | tf_op jit(solution)/shard_map/ppermute | solution.py:647
  4.9 1.3 %collective-permute-start.1 = (bf16[16,2560]{1,0:T(8,128)(2,1)S(1)}, bf16[16,2560]{1,0:T(8,128)(2,1)S(1)}, u32[]{:S(2)}, u32[]{:S(2)}) collective-permute-start(bf16[16,2560]{1,0:T(8,128)(2,1)S(1)} %get-tuple-element.39), channel_id=1, source_target_pairs={{4,0},{8,4},{12,8},{16,12},{20,16},{24,20},{28,24},{32,28},{36,32}... | collective-permute-start | bytes 245768 | tf_op jit(solution)/shard_map/ppermute | solution.py:648
  6.2 4.1 %norm.1 = (bf16[512,2560]{1,0:T(8,128)(2,1)S(1)}, f32[512,128]{1,0:T(8,128)S(1)}, f32[512,128]{1,0:T(8,128)S(1)}, f32[2,24,256]{2,1,0:T(8,128)S(1)}, bf16[512,25...) custom-call(bf16[256,2560]{1,0:T(8,128)(2,1)} %h_ref.1, ...), custom_call_target="tpu_custom_call" | custom-call | flops 4294967296 | bytes 5242880 | tf_op jit(solution)/shard_map/norm/pallas_call | solution.py:163
  10.4 0.0 collective-permute-done.1.next_ref
  10.4 9.2 %entry.1 = (bf16[512,1280]{1,0:T(8,128)(2,1)}, bf16[512,256]{1,0:T(8,128)(2,1)}, bf16[32,88,128]{2,1,0:T(8,128)(2,1)}) custom-call(bf16[512,2560]{1,0:T(8,128)(2,1)S(1)} %get-tuple-element.22.x_ref, bf16[16,2560]{1,0:T(8,128)(2,1)S(1)} %collective-permute-done.prev_ref, bf16[16,2560]{1,0:T(8,128)(2,1)S(1)} %collective-permute-done.1.next_ref, ...), custom_call_target="tpu_custom_call" | custom-call | flops 4278190080 | bytes 12582912 | tf_op jit(solution)/shard_map/entry/pallas_call | solution.py:340
  19.6 10.5 %all-to-all-start = ((bf16[32,88,128]{2,1,0:T(8,128)(2,1)}), bf16[32,88,128]{2,1,0:T(8,128)(2,1)S(1)}, u32[]{:S(2)}, u32[]{:S(2)}) async-start(bf16[32,88,128]{2,1,0:T(8,128)(2,1)} %get-tuple-element.27), calls=%async_computation | async-start | bytes 1441792 | tf_op jit(solution)/shard_map/all_to_all | solution.py:657
  30.1 9.4 %within.1.y_ref = bf16[512,1280]{1,0:T(8,128)(2,1)} custom-call(bf16[512,1280]{1,0:T(8,128)(2,1)} %get-tuple-element.28.x_ref, bf16[512,256]{1,0:T(8,128)(2,1)} %get-tuple-element.29.bc_ref, f32[512,128]{1,0:T(8,128)S(1)} %get-tuple-element.30.cum_ref, f32[2,24,256]{2,1,0:T(8,128)S(1)} %get-tuple-element.31.cumt_ref, f32[512,128]{1,0:T(8,128)S(1)} %get-tuple-element.32.delta_ref), custom_call_target="tpu_custom_call" | custom-call | flops 3221225472 | bytes 5242880 | tf_op jit(solution)/shard_map/within/pallas_call | solution.py:432
  39.4 3.3 %all-to-all-done.pay_ref = bf16[32,88,128]{2,1,0:T(8,128)(2,1)S(1)} async-done(((bf16[32,88,128]{2,1,0:T(8,128)(2,1)}), bf16[32,88,128]{2,1,0:T(8,128)(2,1)S(1)}, u32[]{:S(2)}, u32[]{:S(2)}) %all-to-all-start) | async-done | bytes 720928 | tf_op jit(solution)/shard_map/all_to_all | solution.py:657
  42.7 2.1 %scan.1 = bf16[32,80,128]{2,1,0:T(8,128)(2,1)} custom-call(s32[1]{0:T(128)} %bitcast.7.q_ref, bf16[32,88,128]{2,1,0:T(8,128)(2,1)S(1)} %all-to-all-done.pay_ref), custom_call_target="tpu_custom_call" | custom-call | tf_op jit(solution)/shard_map/scan/pallas_call | solution.py:487
  44.8 4.4 %all-to-all-start.1 = ((bf16[32,80,128]{2,1,0:T(8,128)(2,1)}), bf16[32,80,128]{2,1,0:T(8,128)(2,1)S(1)}, u32[]{:S(2)}, u32[]{:S(2)}) async-start(bf16[32,80,128]{2,1,0:T(8,128)(2,1)} %scan.1), calls=%async_computation.1 | async-start | bytes 1310720 | tf_op jit(solution)/shard_map/all_to_all | solution.py:661
  49.3 7.5 %open_gate.1.z_ref = bf16[512,1280]{1,0:T(8,128)(2,1)S(1)} custom-call(bf16[512,2560]{1,0:T(8,128)(2,1)} %copy-done, bf16[2560,1280]{1,0:T(8,128)(2,1)} %zw_ref.1), custom_call_target="tpu_custom_call" | custom-call | flops 3355443200 | bytes 16777216 | tf_op jit(solution)/shard_map/open_gate/pallas_call | solution.py:388
  56.8 4.3 %all-to-all-done.1 = bf16[32,80,128]{2,1,0:T(8,128)(2,1)S(1)} async-done(((bf16[32,80,128]{2,1,0:T(8,128)(2,1)}), bf16[32,80,128]{2,1,0:T(8,128)(2,1)S(1)}, u32[]{:S(2)}, u32[]{:S(2)}) %all-to-all-start.1) | async-done | bytes 655392 | tf_op jit(solution)/shard_map/all_to_all | solution.py:661
  61.1 7.7 %gate.1 = (bf16[256,2560]{1,0:T(8,128)(2,1)S(1)}, bf16[256,640]{1,0:T(8,128)(2,1)}) custom-call(s32[1]{0:T(128)} %bitcast.2.target_ref, bf16[512,1280]{1,0:T(8,128)(2,1)} %within.1.y_ref, bf16[512,1280]{1,0:T(8,128)(2,1)S(1)} %open_gate.1.z_ref, bf16[512,256]{1,0:T(8,128)(2,1)} %get-tuple-element.29.bc_ref, f32[512,128]{1,0:T(8,128)S(1)} %get-tuple-element.30.cum_ref, ...), custom_call_target="tpu_custom_call" | custom-call | tf_op jit(solution)/shard_map/gate/pallas_call | solution.py:584
  68.7 3.1 %collective-permute-start.2 = (bf16[256,640]{1,0:T(8,128)(2,1)}, bf16[256,640]{1,0:T(8,128)(2,1)S(1)}, u32[]{:S(2)}, u32[]{:S(2)}) collective-permute-start(bf16[256,640]{1,0:T(8,128)(2,1)} %get-tuple-element.36), channel_id=1, source_target_pairs={{0,1},{1,0},{2,3},{3,2},{4,5},{5,4},{6,7},{7,6},{8,9},{9,8},{10,11... | collective-permute-start | bytes 983048 | tf_op jit(solution)/shard_map/ppermute | solution.py:670
  71.8 2.9 %project.3 = f32[256,640]{1,0:T(8,128)S(1)} custom-call(s32[1]{0:T(128)} %bitcast.1.q_ref, bf16[256,2560]{1,0:T(8,128)(2,1)S(1)} %get-tuple-element.37.g_ref, bf16[1280,2560]{1,0:T(8,128)(2,1)} %w_ref.7), custom_call_target="tpu_custom_call" | custom-call | flops 838860800 | bytes 5242880 | tf_op jit(solution)/shard_map/project/pallas_call | solution.py:625
  74.8 0.1 add_convert_fusion.1
  74.8 2.9 %project.4 = bf16[256,640]{1,0:T(8,128)(2,1)S(1)} custom-call(s32[1]{0:T(128)} %bitcast.10.q_ref, bf16[256,2560]{1,0:T(8,128)(2,1)S(1)} %get-tuple-element.37.g_ref, bf16[1280,2560]{1,0:T(8,128)(2,1)} %w_ref.7), custom_call_target="tpu_custom_call" | custom-call | flops 838860800 | bytes 5242880 | tf_op jit(solution)/shard_map/project/pallas_call | solution.py:625
  77.8 0.1 collective-permute-start.3
  77.9 2.5 %collective-permute-start.4 = (bf16[256,640]{1,0:T(8,128)(2,1)S(1)}, bf16[256,640]{1,0:T(8,128)(2,1)S(1)}, u32[]{:S(2)}, u32[]{:S(2)}) collective-permute-start(bf16[256,640]{1,0:T(8,128)(2,1)S(1)} %add_convert_fusion.1), channel_id=1, source_target_pairs={{0,2},{2,0},{1,3},{3,1},{4,6},{6,4},{5,7},{7,5},{8,10},{10,8},{9,1... | collective-permute-start | bytes 983048 | tf_op jit(solution)/shard_map/ppermute | solution.py:674
  80.4 1.0 %constant_dynamic-slice_fusion.rest_1_ = bf16[256,640]{1,0:T(8,128)(2,1)S(1)} fusion(bf16[256,2560]{1,0:T(8,128)(2,1)} %h_ref.1, s32[]{:T(128)S(6)} %select_n.21), kind=kLoop, calls=%fused_computation.2 | loop fusion | bytes 655364 | tf_op jit(solution)/shard_map/dynamic_slice | solution.py:678
  81.4 3.0 %project.5 = f32[256,640]{1,0:T(8,128)S(1)} custom-call(s32[1]{0:T(128)} %bitcast.q_ref, bf16[256,2560]{1,0:T(8,128)(2,1)S(1)} %get-tuple-element.37.g_ref, bf16[1280,2560]{1,0:T(8,128)(2,1)} %w_ref.7, bf16[256,640]{1,0:T(8,128)(2,1)S(1)} %collective-permute-done.3.rest_0_, bf16[256,640]{1,0:T(8,128)(2,1)S(1)} %constant_dynamic-slice_fusion.rest_1_), custom_call_target="tpu_custom_call" | custom-call | flops 838860800 | bytes 5242880 | tf_op jit(solution)/shard_map/project/pallas_call | solution.py:625
  84.4 3.9 %collective-permute-done.4 = bf16[256,640]{1,0:T(8,128)(2,1)S(1)} collective-permute-done((bf16[256,640]{1,0:T(8,128)(2,1)S(1)}, bf16[256,640]{1,0:T(8,128)(2,1)S(1)}, u32[]{:S(2)}, u32[]{:S(2)}) %collective-permute-start.4) | collective-permute-done | bytes 327712 | tf_op jit(solution)/shard_map/ppermute | solution.py:674
  88.3 0.8 add_convert_fusion
  (5 shorter events, 0.0 us)
Async XLA Ops:
  0.9 9.4 %collective-permute-start = (bf16[16,2560]{1,0:T(8,128)(2,1)S(1)}, bf16[16,2560]{1,0:T(8,128)(2,1)S(1)}, u32[]{:S(2)}, u32[]{:S(2)}) collective-permute-start(bf16[16,2560]{1,0:T(8,128)(2,1)S(1)} %get-tuple-element.40), channel_id=1, source_target_pairs={{0,4},{4,8},{8,12},{12,16},{16,20},{20,24},{24,28},{28,32},{32,36}... | collective-permute-start | bytes 245768 | tf_op jit(solution)/shard_map/ppermute | solution.py:647
  4.9 5.5 %collective-permute-start.1 = (bf16[16,2560]{1,0:T(8,128)(2,1)S(1)}, bf16[16,2560]{1,0:T(8,128)(2,1)S(1)}, u32[]{:S(2)}, u32[]{:S(2)}) collective-permute-start(bf16[16,2560]{1,0:T(8,128)(2,1)S(1)} %get-tuple-element.39), channel_id=1, source_target_pairs={{4,0},{8,4},{12,8},{16,12},{20,16},{24,20},{28,24},{32,28},{36,32}... | collective-permute-start | bytes 245768 | tf_op jit(solution)/shard_map/ppermute | solution.py:648
  10.3 9.2 %copy-start = (bf16[512,2560]{1,0:T(8,128)(2,1)}, bf16[512,2560]{1,0:T(8,128)(2,1)S(1)}, u32[]{:S(2)}) copy-start(bf16[512,2560]{1,0:T(8,128)(2,1)S(1)} %get-tuple-element.22.x_ref) | copy-start | bytes 7864324
  19.6 23.2 %all-to-all-start = ((bf16[32,88,128]{2,1,0:T(8,128)(2,1)}), bf16[32,88,128]{2,1,0:T(8,128)(2,1)S(1)}, u32[]{:S(2)}, u32[]{:S(2)}) async-start(bf16[32,88,128]{2,1,0:T(8,128)(2,1)} %get-tuple-element.27), calls=%async_computation | async-start | bytes 1441792 | tf_op jit(solution)/shard_map/all_to_all | solution.py:657
  44.8 16.2 %all-to-all-start.1 = ((bf16[32,80,128]{2,1,0:T(8,128)(2,1)}), bf16[32,80,128]{2,1,0:T(8,128)(2,1)S(1)}, u32[]{:S(2)}, u32[]{:S(2)}) async-start(bf16[32,80,128]{2,1,0:T(8,128)(2,1)} %scan.1), calls=%async_computation.1 | async-start | bytes 1310720 | tf_op jit(solution)/shard_map/all_to_all | solution.py:661
  68.7 6.0 %collective-permute-start.2 = (bf16[256,640]{1,0:T(8,128)(2,1)}, bf16[256,640]{1,0:T(8,128)(2,1)S(1)}, u32[]{:S(2)}, u32[]{:S(2)}) collective-permute-start(bf16[256,640]{1,0:T(8,128)(2,1)} %get-tuple-element.36), channel_id=1, source_target_pairs={{0,1},{1,0},{2,3},{3,2},{4,5},{5,4},{6,7},{7,6},{8,9},{9,8},{10,11... | collective-permute-start | bytes 983048 | tf_op jit(solution)/shard_map/ppermute | solution.py:670
  77.8 3.6 %collective-permute-start.3 = (bf16[256,640]{1,0:T(8,128)(2,1)S(1)}, bf16[256,640]{1,0:T(8,128)(2,1)S(1)}, u32[]{:S(2)}, u32[]{:S(2)}) collective-permute-start(bf16[256,640]{1,0:T(8,128)(2,1)S(1)} %project.4), channel_id=1, source_target_pairs={{0,1},{1,0},{2,3},{3,2},{4,5},{5,4},{6,7},{7,6},{8,9},{9,8},{10,11... | collective-permute-start | bytes 983048 | tf_op jit(solution)/shard_map/ppermute | solution.py:676
  77.9 10.4 %collective-permute-start.4 = (bf16[256,640]{1,0:T(8,128)(2,1)S(1)}, bf16[256,640]{1,0:T(8,128)(2,1)S(1)}, u32[]{:S(2)}, u32[]{:S(2)}) collective-permute-start(bf16[256,640]{1,0:T(8,128)(2,1)S(1)} %add_convert_fusion.1), channel_id=1, source_target_pairs={{0,2},{2,0},{1,3},{3,1},{4,6},{6,4},{5,7},{7,5},{8,10},{10,8},{9,1... | collective-permute-start | bytes 983048 | tf_op jit(solution)/shard_map/ppermute | solution.py:674

commit v8 on v7

--- a/solution.py
+++ b/solution.py
@@ -13,6 +13,7 @@
 EXTRA = 32
 CHUNK = 64
 DEPTHS = 5
+FETCHES = 5
 TILE = 256
 LANES = 128
 epsilon = 1e-05
@@ -99,7 +100,7 @@
     heads = dtb_ref.shape[1]
 
     def fetch(k):
-        part = pl.ds(pl.multiple_of(k * (width // DEPTHS), TILE), width // DEPTHS)
+        part = pl.ds(pl.multiple_of(k * (width // FETCHES), TILE), width // FETCHES)
         return (
             pltpu.make_async_copy(bcw_ref.at[part], bcw_kept.at[part], sems.at[0, k]),
             pltpu.make_async_copy(xw_ref.at[part, :TILE], xw_kept.at[part], sems.at[1, k]),
@@ -110,7 +111,7 @@
             copy.start()
         return 0
 
-    lax.fori_loop(0, DEPTHS, start, 0)
+    lax.fori_loop(0, FETCHES, start, 0)
 
     order = (iota((rows, rows), 1) == time_of(iota((rows, rows), 0), rows)).astype(bf16)
     flip = flip_matrix(TILE)
@@ -152,7 +153,7 @@
         wend_ref[at] = hi_lo(jnp.exp(jnp.minimum(last - cum, 0.0)) * delta[at])
         dec = jnp.where(iota((1, LANES), 1) < heads, jnp.exp(last), 0.0)
         dec_ref[d : d + 1] = dec
-    for k in range(DEPTHS):
+    for k in range(FETCHES):
         for copy in fetch(k):
             copy.wait()
 
@@ -186,7 +187,7 @@
         scratch_shapes=[
             pltpu.VMEM((rows, width), bf16),
             pltpu.VMEM((LANES, width), bf16),
-            pltpu.SemaphoreType.DMA((2, DEPTHS)),
+            pltpu.SemaphoreType.DMA((2, FETCHES)),
         ],
         compiler_params=pltpu.CompilerParams(vmem_limit_bytes=20 << 20),
         cost_estimate=pl.CostEstimate(flops=4 << 30, bytes_accessed=5 << 20, transcendentals=0),
@@ -276,6 +277,7 @@
         )
 
     pieces = [(d, first) for d in range(2) for first in range(0, rows, CHUNK)]
+    share = [k * len(pieces) // (DEPTHS - 1) for k in range(DEPTHS)]
 
     def start(tile, _):
         fetch(tile).start()
@@ -288,7 +290,7 @@
         weight = lambda at: first_ref[at]
         for k in range(DEPTHS - 1):
             product(k, weight)
-            for piece in pieces[2 * k : 2 * k + 2]:
+            for piece in pieces[share[k] : share[k + 1]]:
                 bc_piece(*piece)
         product(DEPTHS - 1, weight)
         for d in range(2):
@@ -311,10 +313,10 @@
         reach()
         for k in range(DEPTHS - 1):
             product(k, weight)
-            for piece in pieces[2 * k : 2 * k + 2]:
-                x_piece(*piece)
-            if k % 2 == 1:
-                states(k // 2)
+            for i in range(share[k], share[k + 1]):
+                x_piece(*pieces[i])
+                if (i + 1) % (len(pieces) // 2) == 0:
+                    states(pieces[i][0])
         product(DEPTHS - 1, weight)
 
     @pl.when(n == steps)
@@ -543,36 +545,81 @@
 def gate_kernel(
     target_ref, y_ref, z_ref, bc_ref, cum_ref, st_ref, gain_ref, w_ref,
     g_ref, out_ref,
-    near_ref, far_ref, sems, held_ref,
+    kept_ref, acc_ref, held_ref, reach_ref, sems,
 ):
-    q = pl.program_id(0)
+    n = pl.program_id(0)
     rows, lanes = y_ref.shape
+    columns = out_ref.shape[1]
     groups = lanes // LANES
-    copies = weight_fetches(target_ref[0], w_ref, near_ref, far_ref, sems)
-
-    @pl.when(q == 0)
+    target = target_ref[0]
+
+    def fetch(p):
+        quarter = jnp.where(p < 2, target, 3 - target)
+        source = pl.ds(pl.multiple_of((p % 2) * lanes, LANES), lanes)
+        cols = pl.ds(pl.multiple_of(quarter * columns, LANES), columns)
+        to = pl.ds(pl.multiple_of(p * lanes, LANES), lanes)
+        return pltpu.make_async_copy(w_ref.at[source, cols], kept_ref.at[to], sems.at[p])
+
+    def start(p, _):
+        fetch(p).start()
+        return 0
+
+    @pl.when(n == 0)
     def _():
-        for copy in copies[1] + copies[0]:
-            copy.start()
-
-    state = jnp.concatenate([st_ref[:, 0, j].reshape(STATE, LANES) for j in range(groups)], axis=1)
-    carried = mm(bc_ref[:, STATE:], state)
-    reach = mm(hi_lo(jnp.exp(cum_ref[...])), spread((q % 2) * (lanes // HEAD_DIM), lanes))
-    same = iota((LANES, LANES), 0) // HEAD_DIM == iota((LANES, LANES), 1) // HEAD_DIM
-    same = same.astype(bf16)
-    for b in range(groups):
+        lax.fori_loop(0, 4, start, 0)
+
+    order = (iota((rows, rows), 0) == time_of(iota((rows, rows), 1), rows)).astype(bf16)
+    same = (iota((LANES, LANES), 0) // HEAD_DIM == iota((LANES, LANES), 1) // HEAD_DIM).astype(bf16)
+
+    def gate_group(q, b, carried, reach):
         at = slice(b * LANES, (b + 1) * LANES)
         y = y_ref[:, at].astype(f32) + carried[:, at] * reach[:, at]
         part = y * z_ref[:, at].astype(f32)
         mean_sq = mm((part * part).astype(bf16), same) * (1.0 / HEAD_DIM)
-        gain = gain_ref[pl.ds((q % 2) * groups + b, 1), :]
-        held_ref[:, at] = (part * lax.rsqrt(mean_sq + epsilon) * gain).astype(bf16)
-    order = (iota((rows, rows), 0) == time_of(iota((rows, rows), 1), rows)).astype(bf16)
-    g_ref[:, pl.ds(pl.multiple_of(q * lanes, LANES), lanes)] = mm(order, held_ref[...]).astype(bf16)
-
-    @pl.when(q == pl.num_programs(0) - 1)
-    def _():
-        project_into(out_ref, g_ref, copies, near_ref, far_ref, ())
+        row = (q % 2) * groups + b
+        scaled_part = part * lax.rsqrt(mean_sq + epsilon) * gain_ref[row : row + 1]
+        held_ref[:, at] = scaled_part.astype(bf16)
+
+    def settle(q):
+        g_ref[:, q * lanes : (q + 1) * lanes] = mm(order, held_ref[...]).astype(bf16)
+
+    def partial(p, first, last):
+        at = slice(p * lanes, (p + 1) * lanes)
+        part = mm(g_ref[:, at], kept_ref[at, first:last])
+        if p % 2:
+            acc_ref[p // 2, :, first:last] += part
+        else:
+            acc_ref[p // 2, :, first:last] = part
+
+    pieces = {0: (0, TILE), 2: (TILE, 2 * TILE), 3: (2 * TILE, columns)}
+
+    def step(k):
+        if k < 4 and k % 2 == 0:
+            reach_ref[...] = hi_lo(jnp.exp(cum_ref[...]))
+        if k > 0:
+            fetch(k - 1).wait()
+        if k < 4:
+            state = [st_ref[:, 0, j].reshape(STATE, LANES) for j in range(groups)]
+            carried = mm(bc_ref[:, STATE:], jnp.concatenate(state, axis=1))
+            reach = mm(reach_ref[...], spread((k % 2) * (lanes // HEAD_DIM), lanes))
+        for b in range(groups):
+            if k < 4:
+                gate_group(k, b, carried, reach)
+            if k > 0 and b in pieces:
+                partial(k - 1, *pieces[b])
+        if k < 4:
+            settle(k)
+            return
+        flip = flip_matrix(LANES)
+        blocks = columns // LANES
+        for b in range(blocks):
+            at = slice(b * LANES, (b + 1) * LANES)
+            source = slice((blocks - 1 - b) * LANES, (blocks - b) * LANES)
+            turned = mm(acc_ref[1, :, source].astype(bf16), flip)
+            out_ref[:, at] = (acc_ref[0, :, at] + turned).astype(bf16)
+
+    for k in range(5):
+        pl.when(n == k)(functools.partial(step, k))
 
 
 def gate(target, y, z, bc, cum, state, gain, weight):
@@ -581,22 +628,29 @@
     lanes = inner // 2
     groups = lanes // LANES
     columns = weight.shape[1] // 4
+    part = lambda n: jnp.minimum(n, 3)
     return pl.pallas_call(
         gate_kernel,
         grid_spec=pltpu.PrefetchScalarGridSpec(
             num_scalar_prefetch=1,
-            grid=(4,),
+            grid=(5,),
             in_specs=[
-                pl.BlockSpec((rows, lanes), lambda q, t: (q // 2, q % 2)),
-                pl.BlockSpec((rows, lanes), lambda q, t: (q // 2, q % 2)),
-                pl.BlockSpec((rows, 2 * STATE), lambda q, t: (q // 2, 0)),
-                pl.BlockSpec((rows, LANES), lambda q, t: (q // 2, 0)),
-                pl.BlockSpec((8, 1, groups, 16, LANES), lambda q, t: (0, q, 0, 0, 0)),
+                pl.BlockSpec((rows, lanes), lambda n, t: (part(n) // 2, part(n) % 2)),
+                pl.BlockSpec((rows, lanes), lambda n, t: (part(n) // 2, part(n) % 2)),
+                pl.BlockSpec((rows, 2 * STATE), lambda n, t: (part(n) // 2, 0)),
+                pl.BlockSpec((rows, LANES), lambda n, t: (part(n) // 2, 0)),
+                pl.BlockSpec((8, 1, groups, 16, LANES), lambda n, t: (0, part(n), 0, 0, 0)),
                 fixed(2 * groups, LANES),
                 pl.BlockSpec(memory_space=pltpu.HBM),
             ],
             out_specs=[fixed(rows, 2 * inner), fixed(rows, columns)],
-            scratch_shapes=weight_scratch(inner, columns) + [pltpu.VMEM((rows, lanes), bf16)],
+            scratch_shapes=[
+                pltpu.VMEM((2 * inner, columns), bf16),
+                pltpu.VMEM((2, rows, columns), f32),
+                pltpu.VMEM((rows, lanes), bf16),
+                pltpu.VMEM((rows, 2 * LANES), bf16),
+                pltpu.SemaphoreType.DMA((4,)),
+            ],
         ),
         out_shape=[
             jax.ShapeDtypeStruct((rows, 2 * inner), bf16),

time: 89.9 us -> 89.4 us (level)
  no operation moved by 1% of the time
where the time goes in v8:
time: 89.4 us; the launch traced here: 88.6 us
  Pallas kernels  48.2 us (54%)
  starting transfers between devices  25.9 us (29%)
  waiting for transfers between devices  11.5 us (13%)
  local copies, waits for them, and re-layouts  1.94 us (2%)
    all_to_all x1, starting transfers between devices, per_device(): pay = lax.all_to_all(pay, 'ctx', 0, 0, tiled=True)  10.5 us
    pallas_call x1, Pallas kernels, within(): pl.pallas_call(within_kernel, grid=(2, inner // TILE), in_specs=[pl.Block...  9.37 us
    pallas_call x1, Pallas kernels, entry(): pl.pallas_call(entry_kernel, grid=(steps + 1,), in_specs=[vmem, vmem, vme...  9.16 us
    pallas_call x3, Pallas kernels, project(): pl.pallas_call(functools.partial(project_kernel, len(adds)), in_specs=[pl...  8.84 us
    pallas_call x1, Pallas kernels, open_gate(): pl.pallas_call(open_gate_kernel, grid=(inner // TILE,), in_specs=[fixed(h...  7.45 us
    pallas_call x1, Pallas kernels, gate(): pl.pallas_call(gate_kernel, grid_spec=pltpu.PrefetchScalarGridSpec(num_sc...  7.12 us
    all_to_all x1, starting transfers between devices, per_device(): state = lax.all_to_all(state, 'ctx', 0, 0, tiled=True)  4.42 us
    all_to_all x1, waiting for transfers between devices, per_device(): state = lax.all_to_all(state, 'ctx', 0, 0, tiled=True)  4.29 us
  transfers between devices with their start and end apart: 7, of which 3 were waited for; matrix products, arithmetic and copies ran while one was open for 1% of the time, Pallas kernels for 30%

profile of v8, /device:TPU:1, one launch (start us, length us, event | category | flops | bytes accessed | tf_op | source)
XLA Modules:
  0.0 88.6 jit_solution(6233792133710420238)
XLA Ops:
  0.0 0.9 %fusion = (bf16[16,2560]{1,0:T(8,128)(2,1)S(1)}, bf16[16,2560]{1,0:T(8,128)(2,1)S(1)}) fusion(bf16[256,2560]{1,0:T(8,128)(2,1)} %h_ref.1), kind=kLoop, calls=%fused_computation.3 | loop fusion | bytes 327680 | tf_op jit(solution)/shard_map/slice | solution.py:702
  0.9 3.9 %collective-permute-start = (bf16[16,2560]{1,0:T(8,128)(2,1)S(1)}, bf16[16,2560]{1,0:T(8,128)(2,1)S(1)}, u32[]{:S(2)}, u32[]{:S(2)}) collective-permute-start(bf16[16,2560]{1,0:T(8,128)(2,1)S(1)} %get-tuple-element.40), channel_id=1, source_target_pairs={{0,4},{4,8},{8,12},{12,16},{16,20},{20,24},{24,28},{28,32},{32,36}... | collective-permute-start | bytes 245768 | tf_op jit(solution)/shard_map/ppermute | solution.py:701
  4.9 1.3 %collective-permute-start.1 = (bf16[16,2560]{1,0:T(8,128)(2,1)S(1)}, bf16[16,2560]{1,0:T(8,128)(2,1)S(1)}, u32[]{:S(2)}, u32[]{:S(2)}) collective-permute-start(bf16[16,2560]{1,0:T(8,128)(2,1)S(1)} %get-tuple-element.39), channel_id=1, source_target_pairs={{4,0},{8,4},{12,8},{16,12},{20,16},{24,20},{28,24},{32,28},{36,32}... | collective-permute-start | bytes 245768 | tf_op jit(solution)/shard_map/ppermute | solution.py:702
  6.2 4.1 %norm.1 = (bf16[512,2560]{1,0:T(8,128)(2,1)S(1)}, f32[512,128]{1,0:T(8,128)S(1)}, f32[512,128]{1,0:T(8,128)S(1)}, f32[2,24,256]{2,1,0:T(8,128)S(1)}, bf16[512,25...) custom-call(bf16[256,2560]{1,0:T(8,128)(2,1)} %h_ref.1, ...), custom_call_target="tpu_custom_call" | custom-call | flops 4294967296 | bytes 5242880 | tf_op jit(solution)/shard_map/norm/pallas_call | solution.py:164
  10.4 0.0 collective-permute-done.1.next_ref
  10.4 9.2 %entry.1 = (bf16[512,1280]{1,0:T(8,128)(2,1)}, bf16[512,256]{1,0:T(8,128)(2,1)}, bf16[32,88,128]{2,1,0:T(8,128)(2,1)}) custom-call(bf16[512,2560]{1,0:T(8,128)(2,1)S(1)} %get-tuple-element.22.x_ref, bf16[16,2560]{1,0:T(8,128)(2,1)S(1)} %collective-permute-done.prev_ref, bf16[16,2560]{1,0:T(8,128)(2,1)S(1)} %collective-permute-done.1.next_ref, ...), custom_call_target="tpu_custom_call" | custom-call | flops 4278190080 | bytes 12582912 | tf_op jit(solution)/shard_map/entry/pallas_call | solution.py:342
  19.6 10.5 %all-to-all-start = ((bf16[32,88,128]{2,1,0:T(8,128)(2,1)}), bf16[32,88,128]{2,1,0:T(8,128)(2,1)S(1)}, u32[]{:S(2)}, u32[]{:S(2)}) async-start(bf16[32,88,128]{2,1,0:T(8,128)(2,1)} %get-tuple-element.27), calls=%async_computation | async-start | bytes 1441792 | tf_op jit(solution)/shard_map/all_to_all | solution.py:711
  30.1 9.4 %within.1.y_ref = bf16[512,1280]{1,0:T(8,128)(2,1)} custom-call(bf16[512,1280]{1,0:T(8,128)(2,1)} %get-tuple-element.28.x_ref, bf16[512,256]{1,0:T(8,128)(2,1)} %get-tuple-element.29.bc_ref, f32[512,128]{1,0:T(8,128)S(1)} %get-tuple-element.30.cum_ref, f32[2,24,256]{2,1,0:T(8,128)S(1)} %get-tuple-element.31.cumt_ref, f32[512,128]{1,0:T(8,128)S(1)} %get-tuple-element.32.delta_ref), custom_call_target="tpu_custom_call" | custom-call | flops 3221225472 | bytes 5242880 | tf_op jit(solution)/shard_map/within/pallas_call | solution.py:434
  39.4 3.3 %all-to-all-done.pay_ref = bf16[32,88,128]{2,1,0:T(8,128)(2,1)S(1)} async-done(((bf16[32,88,128]{2,1,0:T(8,128)(2,1)}), bf16[32,88,128]{2,1,0:T(8,128)(2,1)S(1)}, u32[]{:S(2)}, u32[]{:S(2)}) %all-to-all-start) | async-done | bytes 720928 | tf_op jit(solution)/shard_map/all_to_all | solution.py:711
  42.7 2.1 %scan.1 = bf16[32,80,128]{2,1,0:T(8,128)(2,1)} custom-call(s32[1]{0:T(128)} %bitcast.7.q_ref, bf16[32,88,128]{2,1,0:T(8,128)(2,1)S(1)} %all-to-all-done.pay_ref), custom_call_target="tpu_custom_call" | custom-call | tf_op jit(solution)/shard_map/scan/pallas_call | solution.py:489
  44.8 4.4 %all-to-all-start.1 = ((bf16[32,80,128]{2,1,0:T(8,128)(2,1)}), bf16[32,80,128]{2,1,0:T(8,128)(2,1)S(1)}, u32[]{:S(2)}, u32[]{:S(2)}) async-start(bf16[32,80,128]{2,1,0:T(8,128)(2,1)} %scan.1), calls=%async_computation.1 | async-start | bytes 1310720 | tf_op jit(solution)/shard_map/all_to_all | solution.py:715
  49.3 7.5 %open_gate.1.z_ref = bf16[512,1280]{1,0:T(8,128)(2,1)S(1)} custom-call(bf16[512,2560]{1,0:T(8,128)(2,1)} %copy-done, bf16[2560,1280]{1,0:T(8,128)(2,1)} %zw_ref.1), custom_call_target="tpu_custom_call" | custom-call | flops 3355443200 | bytes 16777216 | tf_op jit(solution)/shard_map/open_gate/pallas_call | solution.py:390
  56.8 4.3 %all-to-all-done.1 = bf16[32,80,128]{2,1,0:T(8,128)(2,1)S(1)} async-done(((bf16[32,80,128]{2,1,0:T(8,128)(2,1)}), bf16[32,80,128]{2,1,0:T(8,128)(2,1)S(1)}, u32[]{:S(2)}, u32[]{:S(2)}) %all-to-all-start.1) | async-done | bytes 655392 | tf_op jit(solution)/shard_map/all_to_all | solution.py:715
  61.1 7.1 %gate.1 = (bf16[256,2560]{1,0:T(8,128)(2,1)S(1)}, bf16[256,640]{1,0:T(8,128)(2,1)}) custom-call(s32[1]{0:T(128)} %bitcast.2.target_ref, bf16[512,1280]{1,0:T(8,128)(2,1)} %within.1.y_ref, bf16[512,1280]{1,0:T(8,128)(2,1)S(1)} %open_gate.1.z_ref, bf16[512,256]{1,0:T(8,128)(2,1)} %get-tuple-element.29.bc_ref, f32[512,128]{1,0:T(8,128)S(1)} %get-tuple-element.30.cum_ref, ...), custom_call_target="tpu_custom_call" | custom-call | tf_op jit(solution)/shard_map/gate/pallas_call | solution.py:632
  68.2 3.1 %collective-permute-start.2 = (bf16[256,640]{1,0:T(8,128)(2,1)}, bf16[256,640]{1,0:T(8,128)(2,1)S(1)}, u32[]{:S(2)}, u32[]{:S(2)}) collective-permute-start(bf16[256,640]{1,0:T(8,128)(2,1)} %get-tuple-element.36), channel_id=1, source_target_pairs={{0,1},{1,0},{2,3},{3,2},{4,5},{5,4},{6,7},{7,6},{8,9},{9,8},{10,11... | collective-permute-start | bytes 983048 | tf_op jit(solution)/shard_map/ppermute | solution.py:724
  71.3 2.9 %project.3 = f32[256,640]{1,0:T(8,128)S(1)} custom-call(s32[1]{0:T(128)} %bitcast.1.q_ref, bf16[256,2560]{1,0:T(8,128)(2,1)S(1)} %get-tuple-element.37.g_ref, bf16[1280,2560]{1,0:T(8,128)(2,1)} %w_ref.7), custom_call_target="tpu_custom_call" | custom-call | flops 838860800 | bytes 5242880 | tf_op jit(solution)/shard_map/project/pallas_call | solution.py:679
  74.2 0.1 add_convert_fusion.1
  74.3 3.0 %project.4 = bf16[256,640]{1,0:T(8,128)(2,1)S(1)} custom-call(s32[1]{0:T(128)} %bitcast.10.q_ref, bf16[256,2560]{1,0:T(8,128)(2,1)S(1)} %get-tuple-element.37.g_ref, bf16[1280,2560]{1,0:T(8,128)(2,1)} %w_ref.7), custom_call_target="tpu_custom_call" | custom-call | flops 838860800 | bytes 5242880 | tf_op jit(solution)/shard_map/project/pallas_call | solution.py:679
  77.3 0.1 collective-permute-start.3
  77.4 2.5 %collective-permute-start.4 = (bf16[256,640]{1,0:T(8,128)(2,1)S(1)}, bf16[256,640]{1,0:T(8,128)(2,1)S(1)}, u32[]{:S(2)}, u32[]{:S(2)}) collective-permute-start(bf16[256,640]{1,0:T(8,128)(2,1)S(1)} %add_convert_fusion.1), channel_id=1, source_target_pairs={{0,2},{2,0},{1,3},{3,1},{4,6},{6,4},{5,7},{7,5},{8,10},{10,8},{9,1... | collective-permute-start | bytes 983048 | tf_op jit(solution)/shard_map/ppermute | solution.py:728
  79.9 1.0 %constant_dynamic-slice_fusion.rest_1_ = bf16[256,640]{1,0:T(8,128)(2,1)S(1)} fusion(bf16[256,2560]{1,0:T(8,128)(2,1)} %h_ref.1, s32[]{:T(128)S(6)} %select_n.21), kind=kLoop, calls=%fused_computation.2 | loop fusion | bytes 655364 | tf_op jit(solution)/shard_map/dynamic_slice | solution.py:732
  80.9 3.0 %project.5 = f32[256,640]{1,0:T(8,128)S(1)} custom-call(s32[1]{0:T(128)} %bitcast.q_ref, bf16[256,2560]{1,0:T(8,128)(2,1)S(1)} %get-tuple-element.37.g_ref, bf16[1280,2560]{1,0:T(8,128)(2,1)} %w_ref.7, bf16[256,640]{1,0:T(8,128)(2,1)S(1)} %collective-permute-done.3.rest_0_, bf16[256,640]{1,0:T(8,128)(2,1)S(1)} %constant_dynamic-slice_fusion.rest_1_), custom_call_target="tpu_custom_call" | custom-call | flops 838860800 | bytes 5242880 | tf_op jit(solution)/shard_map/project/pallas_call | solution.py:679
  83.9 3.9 %collective-permute-done.4 = bf16[256,640]{1,0:T(8,128)(2,1)S(1)} collective-permute-done((bf16[256,640]{1,0:T(8,128)(2,1)S(1)}, bf16[256,640]{1,0:T(8,128)(2,1)S(1)}, u32[]{:S(2)}, u32[]{:S(2)}) %collective-permute-start.4) | collective-permute-done | bytes 327712 | tf_op jit(solution)/shard_map/ppermute | solution.py:728
  87.8 0.8 add_convert_fusion
  (5 shorter events, 0.0 us)
Async XLA Ops:
  0.9 9.4 %collective-permute-start = (bf16[16,2560]{1,0:T(8,128)(2,1)S(1)}, bf16[16,2560]{1,0:T(8,128)(2,1)S(1)}, u32[]{:S(2)}, u32[]{:S(2)}) collective-permute-start(bf16[16,2560]{1,0:T(8,128)(2,1)S(1)} %get-tuple-element.40), channel_id=1, source_target_pairs={{0,4},{4,8},{8,12},{12,16},{16,20},{20,24},{24,28},{28,32},{32,36}... | collective-permute-start | bytes 245768 | tf_op jit(solution)/shard_map/ppermute | solution.py:701
  4.9 5.5 %collective-permute-start.1 = (bf16[16,2560]{1,0:T(8,128)(2,1)S(1)}, bf16[16,2560]{1,0:T(8,128)(2,1)S(1)}, u32[]{:S(2)}, u32[]{:S(2)}) collective-permute-start(bf16[16,2560]{1,0:T(8,128)(2,1)S(1)} %get-tuple-element.39), channel_id=1, source_target_pairs={{4,0},{8,4},{12,8},{16,12},{20,16},{24,20},{28,24},{32,28},{36,32}... | collective-permute-start | bytes 245768 | tf_op jit(solution)/shard_map/ppermute | solution.py:702
  10.3 9.2 %copy-start = (bf16[512,2560]{1,0:T(8,128)(2,1)}, bf16[512,2560]{1,0:T(8,128)(2,1)S(1)}, u32[]{:S(2)}) copy-start(bf16[512,2560]{1,0:T(8,128)(2,1)S(1)} %get-tuple-element.22.x_ref) | copy-start | bytes 7864324
  19.6 23.2 %all-to-all-start = ((bf16[32,88,128]{2,1,0:T(8,128)(2,1)}), bf16[32,88,128]{2,1,0:T(8,128)(2,1)S(1)}, u32[]{:S(2)}, u32[]{:S(2)}) async-start(bf16[32,88,128]{2,1,0:T(8,128)(2,1)} %get-tuple-element.27), calls=%async_computation | async-start | bytes 1441792 | tf_op jit(solution)/shard_map/all_to_all | solution.py:711
  44.8 16.2 %all-to-all-start.1 = ((bf16[32,80,128]{2,1,0:T(8,128)(2,1)}), bf16[32,80,128]{2,1,0:T(8,128)(2,1)S(1)}, u32[]{:S(2)}, u32[]{:S(2)}) async-start(bf16[32,80,128]{2,1,0:T(8,128)(2,1)} %scan.1), calls=%async_computation.1 | async-start | bytes 1310720 | tf_op jit(solution)/shard_map/all_to_all | solution.py:715
  68.2 6.0 %collective-permute-start.2 = (bf16[256,640]{1,0:T(8,128)(2,1)}, bf16[256,640]{1,0:T(8,128)(2,1)S(1)}, u32[]{:S(2)}, u32[]{:S(2)}) collective-permute-start(bf16[256,640]{1,0:T(8,128)(2,1)} %get-tuple-element.36), channel_id=1, source_target_pairs={{0,1},{1,0},{2,3},{3,2},{4,5},{5,4},{6,7},{7,6},{8,9},{9,8},{10,11... | collective-permute-start | bytes 983048 | tf_op jit(solution)/shard_map/ppermute | solution.py:724
  77.3 3.6 %collective-permute-start.3 = (bf16[256,640]{1,0:T(8,128)(2,1)S(1)}, bf16[256,640]{1,0:T(8,128)(2,1)S(1)}, u32[]{:S(2)}, u32[]{:S(2)}) collective-permute-start(bf16[256,640]{1,0:T(8,128)(2,1)S(1)} %project.4), channel_id=1, source_target_pairs={{0,1},{1,0},{2,3},{3,2},{4,5},{5,4},{6,7},{7,6},{8,9},{9,8},{10,11... | collective-permute-start | bytes 983048 | tf_op jit(solution)/shard_map/ppermute | solution.py:730
  77.4 10.4 %collective-permute-start.4 = (bf16[256,640]{1,0:T(8,128)(2,1)S(1)}, bf16[256,640]{1,0:T(8,128)(2,1)S(1)}, u32[]{:S(2)}, u32[]{:S(2)}) collective-permute-start(bf16[256,640]{1,0:T(8,128)(2,1)S(1)} %add_convert_fusion.1), channel_id=1, source_target_pairs={{0,2},{2,0},{1,3},{3,1},{4,6},{6,4},{5,7},{7,5},{8,10},{10,8},{9,1... | collective-permute-start | bytes 983048 | tf_op jit(solution)/shard_map/ppermute | solution.py:728

commit v9 on v8

--- a/solution.py
+++ b/solution.py
@@ -403,7 +403,7 @@
     )(off_chip(x), off_chip(zw))
 
 
-def within_kernel(x_ref, bc_ref, cum_ref, cumt_ref, delta_ref, y_ref, gram_ref):
+def within_kernel(x_ref, bc_ref, cum_ref, cumt_ref, delta_ref, y_ref, reach_ref, gram_ref, decay_ref, size_ref):
     d, n = pl.program_id(0), pl.program_id(1)
     rows = x_ref.shape[0]
     heads = TILE // HEAD_DIM
@@ -416,8 +416,12 @@
         t, s = time_of(iota((rows, rows), 0), rows), time_of(iota((rows, rows), 1), rows)
         seen = jnp.where(d == 0, t - s, s - t) >= 0
         gram_ref[...] = jnp.where(seen, gram, 0.0)
-
-    weighted = x_ref[...].astype(f32) * mm(hi_lo(delta_ref[...]), spread(n * heads, TILE))
+        decay_ref[...] = hi_lo(jnp.exp(cum_ref[...]))
+        size_ref[...] = hi_lo(delta_ref[...])
+
+    place = spread(n * heads, TILE)
+    reach_ref[...] = mm(decay_ref[...], place).astype(bf16)
+    weighted = x_ref[...].astype(f32) * mm(size_ref[...], place)
     cum = pltpu.roll(cum_ref[...], (LANES - n * heads) % LANES, 1)
     owner = iota((rows, TILE), 1) // HEAD_DIM
     total = jnp.zeros((rows, TILE), f32)
@@ -441,9 +445,13 @@
             pl.BlockSpec((1, 24, rows), lambda d, n: (d, 0, 0)),
             pl.BlockSpec((rows, LANES), lambda d, n: (d, 0)),
         ],
-        out_specs=pl.BlockSpec((rows, TILE), lambda d, n: (d, n)),
-        out_shape=pltpu.HBM((2 * rows, inner), bf16),
-        scratch_shapes=[pltpu.VMEM((rows, rows), f32)],
+        out_specs=[pl.BlockSpec((rows, TILE), lambda d, n: (d, n))] * 2,
+        out_shape=[pltpu.HBM((2 * rows, inner), bf16)] * 2,
+        scratch_shapes=[
+            pltpu.VMEM((rows, rows), f32),
+            pltpu.VMEM((rows, 2 * LANES), bf16),
+            pltpu.VMEM((rows, 2 * LANES), bf16),
+        ],
         compiler_params=pltpu.CompilerParams(
             dimension_semantics=("arbitrary", "arbitrary"), vmem_limit_bytes=12 << 20
         ),
@@ -543,9 +551,9 @@
 
 
 def gate_kernel(
-    target_ref, y_ref, z_ref, bc_ref, cum_ref, st_ref, gain_ref, w_ref,
+    target_ref, y_ref, z_ref, bc_ref, reach_ref, st_ref, gain_ref, w_ref,
     g_ref, out_ref,
-    kept_ref, acc_ref, held_ref, reach_ref, sems,
+    kept_ref, acc_ref, held_ref, sems,
 ):
     n = pl.program_id(0)
     rows, lanes = y_ref.shape
@@ -571,9 +579,9 @@
     order = (iota((rows, rows), 0) == time_of(iota((rows, rows), 1), rows)).astype(bf16)
     same = (iota((LANES, LANES), 0) // HEAD_DIM == iota((LANES, LANES), 1) // HEAD_DIM).astype(bf16)
 
-    def gate_group(q, b, carried, reach):
+    def gate_group(q, b, carried):
         at = slice(b * LANES, (b + 1) * LANES)
-        y = y_ref[:, at].astype(f32) + carried[:, at] * reach[:, at]
+        y = y_ref[:, at].astype(f32) + carried[:, at] * reach_ref[:, at].astype(f32)
         part = y * z_ref[:, at].astype(f32)
         mean_sq = mm((part * part).astype(bf16), same) * (1.0 / HEAD_DIM)
         row = (q % 2) * groups + b
@@ -594,17 +602,14 @@
     pieces = {0: (0, TILE), 2: (TILE, 2 * TILE), 3: (2 * TILE, columns)}
 
     def step(k):
-        if k < 4 and k % 2 == 0:
-            reach_ref[...] = hi_lo(jnp.exp(cum_ref[...]))
         if k > 0:
             fetch(k - 1).wait()
         if k < 4:
             state = [st_ref[:, 0, j].reshape(STATE, LANES) for j in range(groups)]
             carried = mm(bc_ref[:, STATE:], jnp.concatenate(state, axis=1))
-            reach = mm(reach_ref[...], spread((k % 2) * (lanes // HEAD_DIM), lanes))
         for b in range(groups):
             if k < 4:
-                gate_group(k, b, carried, reach)
+                gate_group(k, b, carried)
             if k > 0 and b in pieces:
                 partial(k - 1, *pieces[b])
         if k < 4:
@@ -622,7 +627,7 @@
         pl.when(n == k)(functools.partial(step, k))
 
 
-def gate(target, y, z, bc, cum, state, gain, weight):
+def gate(target, y, z, bc, reach, state, gain, weight):
     rows = y.shape[0] // 2
     inner = y.shape[1]
     lanes = inner // 2
@@ -638,7 +643,7 @@
                 pl.BlockSpec((rows, lanes), lambda n, t: (part(n) // 2, part(n) % 2)),
                 pl.BlockSpec((rows, lanes), lambda n, t: (part(n) // 2, part(n) % 2)),
                 pl.BlockSpec((rows, 2 * STATE), lambda n, t: (part(n) // 2, 0)),
-                pl.BlockSpec((rows, LANES), lambda n, t: (part(n) // 2, 0)),
+                pl.BlockSpec((rows, lanes), lambda n, t: (part(n) // 2, part(n) % 2)),
                 pl.BlockSpec((8, 1, groups, 16, LANES), lambda n, t: (0, part(n), 0, 0, 0)),
                 fixed(2 * groups, LANES),
                 pl.BlockSpec(memory_space=pltpu.HBM),
@@ -648,7 +653,6 @@
                 pltpu.VMEM((2 * inner, columns), bf16),
                 pltpu.VMEM((2, rows, columns), f32),
                 pltpu.VMEM((rows, lanes), bf16),
-                pltpu.VMEM((rows, 2 * LANES), bf16),
                 pltpu.SemaphoreType.DMA((4,)),
             ],
         ),
@@ -660,7 +664,7 @@
             dimension_semantics=("arbitrary",), vmem_limit_bytes=20 << 20
         ),
         name="gate",
-    )(target, off_chip(y), z, off_chip(bc), cum, state.reshape(8, 4, groups, 16, LANES), off_chip(gain), off_chip(weight))
+    )(target, off_chip(y), z, off_chip(bc), off_chip(reach), state.reshape(8, 4, groups, 16, LANES), off_chip(gain), off_chip(weight))
 
 
 def project_kernel(has_add, q_ref, g_ref, w_ref, *rest):
@@ -709,7 +713,7 @@
         x_weight, blocks,
     )
     pay = lax.all_to_all(pay, "ctx", 0, 0, tiled=True)
-    y = within(xconv, bc, cum, cumt, delta)
+    y, reach = within(xconv, bc, cum, cumt, delta)
     pay, y = lax.optimization_barrier((pay, y))
     state = scan((place % 4)[None], pay)
     state = lax.all_to_all(state, "ctx", 0, 0, tiled=True)
@@ -719,7 +723,7 @@
     core_swap = [(0, 1), (1, 0), (2, 3), (3, 2)]
     far_swap = [(0, 2), (2, 0), (1, 3), (3, 1)]
     gated, first = gate(
-        quarter(1 - far, 1 - core), y, open_z, bc, cum, state, out_gain.reshape(-1, LANES), out_weight
+        quarter(1 - far, 1 - core), y, open_z, bc, reach, state, out_gain.reshape(-1, LANES), out_weight
     )
     first = lax.ppermute(first, "head", core_swap)
     second = project(quarter(1 - far, core), gated, out_weight, f32)

time: 89.4 us -> 90 us (level)
  transfers between devices with their start and end apart: 7 -> 7, of which waited for: 3 -> 3; matrix products, arithmetic and copies ran while one was open for 1% -> 1% of each run, Pallas kernels for 30% -> 31%
where the time goes in v9:
time: 90 us; the launch traced here: 89.1 us
  Pallas kernels  48.7 us (54%)
  starting transfers between devices  26.6 us (30%)
  waiting for transfers between devices  10.9 us (12%)
  local copies, waits for them, and re-layouts  1.94 us (2%)
    all_to_all x1, starting transfers between devices, per_device(): pay = lax.all_to_all(pay, 'ctx', 0, 0, tiled=True)  10.5 us
    pallas_call x1, Pallas kernels, within(): pl.pallas_call(within_kernel, grid=(2, inner // TILE), in_specs=[pl.Block...  10 us
    pallas_call x1, Pallas kernels, entry(): pl.pallas_call(entry_kernel, grid=(steps + 1,), in_specs=[vmem, vmem, vme...  9.16 us
    pallas_call x3, Pallas kernels, project(): pl.pallas_call(functools.partial(project_kernel, len(adds)), in_specs=[pl...  8.84 us
    pallas_call x1, Pallas kernels, open_gate(): pl.pallas_call(open_gate_kernel, grid=(inner // TILE,), in_specs=[fixed(h...  7.45 us
    pallas_call x1, Pallas kernels, gate(): pl.pallas_call(gate_kernel, grid_spec=pltpu.PrefetchScalarGridSpec(num_sc...  6.94 us
    all_to_all x1, starting transfers between devices, per_device(): state = lax.all_to_all(state, 'ctx', 0, 0, tiled=True)  5.14 us
    all_to_all x1, waiting for transfers between devices, per_device(): state = lax.all_to_all(state, 'ctx', 0, 0, tiled=True)  4.29 us
  transfers between devices with their start and end apart: 7, of which 3 were waited for; matrix products, arithmetic and copies ran while one was open for 1% of the time, Pallas kernels for 31%

profile of v9, /device:TPU:1, one launch (start us, length us, event | category | flops | bytes accessed | tf_op | source)
XLA Modules:
  0.0 89.1 jit_solution(3599689862044782322)
XLA Ops:
  0.0 0.9 %fusion = (bf16[16,2560]{1,0:T(8,128)(2,1)S(1)}, bf16[16,2560]{1,0:T(8,128)(2,1)S(1)}) fusion(bf16[256,2560]{1,0:T(8,128)(2,1)} %h_ref.1), kind=kLoop, calls=%fused_computation.3 | loop fusion | bytes 327680 | tf_op jit(solution)/shard_map/slice | solution.py:706
  0.9 3.9 %collective-permute-start = (bf16[16,2560]{1,0:T(8,128)(2,1)S(1)}, bf16[16,2560]{1,0:T(8,128)(2,1)S(1)}, u32[]{:S(2)}, u32[]{:S(2)}) collective-permute-start(bf16[16,2560]{1,0:T(8,128)(2,1)S(1)} %get-tuple-element.44), channel_id=1, source_target_pairs={{0,4},{4,8},{8,12},{12,16},{16,20},{20,24},{24,28},{28,32},{32,36}... | collective-permute-start | bytes 245768 | tf_op jit(solution)/shard_map/ppermute | solution.py:705
  4.9 1.3 %collective-permute-start.1 = (bf16[16,2560]{1,0:T(8,128)(2,1)S(1)}, bf16[16,2560]{1,0:T(8,128)(2,1)S(1)}, u32[]{:S(2)}, u32[]{:S(2)}) collective-permute-start(bf16[16,2560]{1,0:T(8,128)(2,1)S(1)} %get-tuple-element.43), channel_id=1, source_target_pairs={{4,0},{8,4},{12,8},{16,12},{20,16},{24,20},{28,24},{32,28},{36,32}... | collective-permute-start | bytes 245768 | tf_op jit(solution)/shard_map/ppermute | solution.py:706
  6.2 4.1 %norm.1 = (bf16[512,2560]{1,0:T(8,128)(2,1)S(1)}, f32[512,128]{1,0:T(8,128)S(1)}, f32[512,128]{1,0:T(8,128)S(1)}, f32[2,24,256]{2,1,0:T(8,128)S(1)}, bf16[512,25...) custom-call(bf16[256,2560]{1,0:T(8,128)(2,1)} %h_ref.1, ...), custom_call_target="tpu_custom_call" | custom-call | flops 4294967296 | bytes 5242880 | tf_op jit(solution)/shard_map/norm/pallas_call | solution.py:164
  10.4 0.0 collective-permute-done.1.next_ref
  10.4 9.2 %entry.1 = (bf16[512,1280]{1,0:T(8,128)(2,1)}, bf16[512,256]{1,0:T(8,128)(2,1)}, bf16[32,88,128]{2,1,0:T(8,128)(2,1)}) custom-call(bf16[512,2560]{1,0:T(8,128)(2,1)S(1)} %get-tuple-element.24.x_ref, bf16[16,2560]{1,0:T(8,128)(2,1)S(1)} %collective-permute-done.prev_ref, bf16[16,2560]{1,0:T(8,128)(2,1)S(1)} %collective-permute-done.1.next_ref, ...), custom_call_target="tpu_custom_call" | custom-call | flops 4278190080 | bytes 12582912 | tf_op jit(solution)/shard_map/entry/pallas_call | solution.py:342
  19.6 10.5 %all-to-all-start = ((bf16[32,88,128]{2,1,0:T(8,128)(2,1)}), bf16[32,88,128]{2,1,0:T(8,128)(2,1)S(1)}, u32[]{:S(2)}, u32[]{:S(2)}) async-start(bf16[32,88,128]{2,1,0:T(8,128)(2,1)} %get-tuple-element.29), calls=%async_computation | async-start | bytes 1441792 | tf_op jit(solution)/shard_map/all_to_all | solution.py:715
  30.1 10.0 %within.1 = (bf16[512,1280]{1,0:T(8,128)(2,1)}, bf16[512,1280]{1,0:T(8,128)(2,1)}) custom-call(bf16[512,1280]{1,0:T(8,128)(2,1)} %get-tuple-element.30.x_ref, bf16[512,256]{1,0:T(8,128)(2,1)} %get-tuple-element.31.bc_ref, f32[512,128]{1,0:T(8,128)S(1)} %get-tuple-element.32.cum_ref, f32[2,24,256]{2,1,0:T(8,128)S(1)} %get-tuple-element.33.cumt_ref, ...), custom_call_target="tpu_custom_call" | custom-call | flops 3221225472 | bytes 5242880 | tf_op jit(solution)/shard_map/within/pallas_call | solution.py:438
  40.1 2.6 %all-to-all-done.pay_ref = bf16[32,88,128]{2,1,0:T(8,128)(2,1)S(1)} async-done(((bf16[32,88,128]{2,1,0:T(8,128)(2,1)}), bf16[32,88,128]{2,1,0:T(8,128)(2,1)S(1)}, u32[]{:S(2)}, u32[]{:S(2)}) %all-to-all-start) | async-done | bytes 720928 | tf_op jit(solution)/shard_map/all_to_all | solution.py:715
  42.7 2.2 %scan.1 = bf16[32,80,128]{2,1,0:T(8,128)(2,1)} custom-call(s32[1]{0:T(128)} %bitcast.7.q_ref, bf16[32,88,128]{2,1,0:T(8,128)(2,1)S(1)} %all-to-all-done.pay_ref), custom_call_target="tpu_custom_call" | custom-call | tf_op jit(solution)/shard_map/scan/pallas_call | solution.py:497
  44.9 5.1 %all-to-all-start.1 = ((bf16[32,80,128]{2,1,0:T(8,128)(2,1)}), bf16[32,80,128]{2,1,0:T(8,128)(2,1)S(1)}, u32[]{:S(2)}, u32[]{:S(2)}) async-start(bf16[32,80,128]{2,1,0:T(8,128)(2,1)} %scan.1), calls=%async_computation.1 | async-start | bytes 1310720 | tf_op jit(solution)/shard_map/all_to_all | solution.py:719
  50.1 7.5 %open_gate.1.z_ref = bf16[512,1280]{1,0:T(8,128)(2,1)S(1)} custom-call(bf16[512,2560]{1,0:T(8,128)(2,1)} %copy-done, bf16[2560,1280]{1,0:T(8,128)(2,1)} %zw_ref.1), custom_call_target="tpu_custom_call" | custom-call | flops 3355443200 | bytes 16777216 | tf_op jit(solution)/shard_map/open_gate/pallas_call | solution.py:390
  57.5 4.3 %all-to-all-done.1 = bf16[32,80,128]{2,1,0:T(8,128)(2,1)S(1)} async-done(((bf16[32,80,128]{2,1,0:T(8,128)(2,1)}), bf16[32,80,128]{2,1,0:T(8,128)(2,1)S(1)}, u32[]{:S(2)}, u32[]{:S(2)}) %all-to-all-start.1) | async-done | bytes 655392 | tf_op jit(solution)/shard_map/all_to_all | solution.py:719
  61.8 6.9 %gate.1 = (bf16[256,2560]{1,0:T(8,128)(2,1)S(1)}, bf16[256,640]{1,0:T(8,128)(2,1)}) custom-call(s32[1]{0:T(128)} %bitcast.2.target_ref, bf16[512,1280]{1,0:T(8,128)(2,1)} %get-tuple-element.36.y_ref, bf16[512,1280]{1,0:T(8,128)(2,1)S(1)} %open_gate.1.z_ref, bf16[512,256]{1,0:T(8,128)(2,1)} %get-tuple-element.31.bc_ref, ...), custom_call_target="tpu_custom_call" | custom-call | tf_op jit(solution)/shard_map/gate/pallas_call | solution.py:637
  68.8 3.1 %collective-permute-start.2 = (bf16[256,640]{1,0:T(8,128)(2,1)}, bf16[256,640]{1,0:T(8,128)(2,1)S(1)}, u32[]{:S(2)}, u32[]{:S(2)}) collective-permute-start(bf16[256,640]{1,0:T(8,128)(2,1)} %get-tuple-element.40), channel_id=1, source_target_pairs={{0,1},{1,0},{2,3},{3,2},{4,5},{5,4},{6,7},{7,6},{8,9},{9,8},{10,11... | collective-permute-start | bytes 983048 | tf_op jit(solution)/shard_map/ppermute | solution.py:728
  71.8 2.9 %project.3 = f32[256,640]{1,0:T(8,128)S(1)} custom-call(s32[1]{0:T(128)} %bitcast.1.q_ref, bf16[256,2560]{1,0:T(8,128)(2,1)S(1)} %get-tuple-element.41.g_ref, bf16[1280,2560]{1,0:T(8,128)(2,1)} %w_ref.7), custom_call_target="tpu_custom_call" | custom-call | flops 838860800 | bytes 5242880 | tf_op jit(solution)/shard_map/project/pallas_call | solution.py:683
  74.8 0.1 add_convert_fusion.1
  74.9 3.0 %project.4 = bf16[256,640]{1,0:T(8,128)(2,1)S(1)} custom-call(s32[1]{0:T(128)} %bitcast.10.q_ref, bf16[256,2560]{1,0:T(8,128)(2,1)S(1)} %get-tuple-element.41.g_ref, bf16[1280,2560]{1,0:T(8,128)(2,1)} %w_ref.7), custom_call_target="tpu_custom_call" | custom-call | flops 838860800 | bytes 5242880 | tf_op jit(solution)/shard_map/project/pallas_call | solution.py:683
  77.8 0.1 collective-permute-start.3
  77.9 2.5 %collective-permute-start.4 = (bf16[256,640]{1,0:T(8,128)(2,1)S(1)}, bf16[256,640]{1,0:T(8,128)(2,1)S(1)}, u32[]{:S(2)}, u32[]{:S(2)}) collective-permute-start(bf16[256,640]{1,0:T(8,128)(2,1)S(1)} %add_convert_fusion.1), channel_id=1, source_target_pairs={{0,2},{2,0},{1,3},{3,1},{4,6},{6,4},{5,7},{7,5},{8,10},{10,8},{9,1... | collective-permute-start | bytes 983048 | tf_op jit(solution)/shard_map/ppermute | solution.py:732
  80.5 1.0 %constant_dynamic-slice_fusion.rest_1_ = bf16[256,640]{1,0:T(8,128)(2,1)S(1)} fusion(bf16[256,2560]{1,0:T(8,128)(2,1)} %h_ref.1, s32[]{:T(128)S(6)} %select_n.21), kind=kLoop, calls=%fused_computation.2 | loop fusion | bytes 655364 | tf_op jit(solution)/shard_map/dynamic_slice | solution.py:736
  81.5 3.0 %project.5 = f32[256,640]{1,0:T(8,128)S(1)} custom-call(s32[1]{0:T(128)} %bitcast.q_ref, bf16[256,2560]{1,0:T(8,128)(2,1)S(1)} %get-tuple-element.41.g_ref, bf16[1280,2560]{1,0:T(8,128)(2,1)} %w_ref.7, bf16[256,640]{1,0:T(8,128)(2,1)S(1)} %collective-permute-done.3.rest_0_, bf16[256,640]{1,0:T(8,128)(2,1)S(1)} %constant_dynamic-slice_fusion.rest_1_), custom_call_target="tpu_custom_call" | custom-call | flops 838860800 | bytes 5242880 | tf_op jit(solution)/shard_map/project/pallas_call | solution.py:683
  84.4 3.9 %collective-permute-done.4 = bf16[256,640]{1,0:T(8,128)(2,1)S(1)} collective-permute-done((bf16[256,640]{1,0:T(8,128)(2,1)S(1)}, bf16[256,640]{1,0:T(8,128)(2,1)S(1)}, u32[]{:S(2)}, u32[]{:S(2)}) %collective-permute-start.4) | collective-permute-done | bytes 327712 | tf_op jit(solution)/shard_map/ppermute | solution.py:732
  88.4 0.8 add_convert_fusion
  (5 shorter events, 0.0 us)
Async XLA Ops:
  0.9 9.4 %collective-permute-start = (bf16[16,2560]{1,0:T(8,128)(2,1)S(1)}, bf16[16,2560]{1,0:T(8,128)(2,1)S(1)}, u32[]{:S(2)}, u32[]{:S(2)}) collective-permute-start(bf16[16,2560]{1,0:T(8,128)(2,1)S(1)} %get-tuple-element.44), channel_id=1, source_target_pairs={{0,4},{4,8},{8,12},{12,16},{16,20},{20,24},{24,28},{28,32},{32,36}... | collective-permute-start | bytes 245768 | tf_op jit(solution)/shard_map/ppermute | solution.py:705
  4.9 5.5 %collective-permute-start.1 = (bf16[16,2560]{1,0:T(8,128)(2,1)S(1)}, bf16[16,2560]{1,0:T(8,128)(2,1)S(1)}, u32[]{:S(2)}, u32[]{:S(2)}) collective-permute-start(bf16[16,2560]{1,0:T(8,128)(2,1)S(1)} %get-tuple-element.43), channel_id=1, source_target_pairs={{4,0},{8,4},{12,8},{16,12},{20,16},{24,20},{28,24},{32,28},{36,32}... | collective-permute-start | bytes 245768 | tf_op jit(solution)/shard_map/ppermute | solution.py:706
  10.3 9.2 %copy-start = (bf16[512,2560]{1,0:T(8,128)(2,1)}, bf16[512,2560]{1,0:T(8,128)(2,1)S(1)}, u32[]{:S(2)}) copy-start(bf16[512,2560]{1,0:T(8,128)(2,1)S(1)} %get-tuple-element.24.x_ref) | copy-start | bytes 7864324
  19.6 23.2 %all-to-all-start = ((bf16[32,88,128]{2,1,0:T(8,128)(2,1)}), bf16[32,88,128]{2,1,0:T(8,128)(2,1)S(1)}, u32[]{:S(2)}, u32[]{:S(2)}) async-start(bf16[32,88,128]{2,1,0:T(8,128)(2,1)} %get-tuple-element.29), calls=%async_computation | async-start | bytes 1441792 | tf_op jit(solution)/shard_map/all_to_all | solution.py:715
  44.9 16.9 %all-to-all-start.1 = ((bf16[32,80,128]{2,1,0:T(8,128)(2,1)}), bf16[32,80,128]{2,1,0:T(8,128)(2,1)S(1)}, u32[]{:S(2)}, u32[]{:S(2)}) async-start(bf16[32,80,128]{2,1,0:T(8,128)(2,1)} %scan.1), calls=%async_computation.1 | async-start | bytes 1310720 | tf_op jit(solution)/shard_map/all_to_all | solution.py:719
  68.8 6.0 %collective-permute-start.2 = (bf16[256,640]{1,0:T(8,128)(2,1)}, bf16[256,640]{1,0:T(8,128)(2,1)S(1)}, u32[]{:S(2)}, u32[]{:S(2)}) collective-permute-start(bf16[256,640]{1,0:T(8,128)(2,1)} %get-tuple-element.40), channel_id=1, source_target_pairs={{0,1},{1,0},{2,3},{3,2},{4,5},{5,4},{6,7},{7,6},{8,9},{9,8},{10,11... | collective-permute-start | bytes 983048 | tf_op jit(solution)/shard_map/ppermute | solution.py:728
  77.8 3.6 %collective-permute-start.3 = (bf16[256,640]{1,0:T(8,128)(2,1)S(1)}, bf16[256,640]{1,0:T(8,128)(2,1)S(1)}, u32[]{:S(2)}, u32[]{:S(2)}) collective-permute-start(bf16[256,640]{1,0:T(8,128)(2,1)S(1)} %project.4), channel_id=1, source_target_pairs={{0,1},{1,0},{2,3},{3,2},{4,5},{5,4},{6,7},{7,6},{8,9},{9,8},{10,11... | collective-permute-start | bytes 983048 | tf_op jit(solution)/shard_map/ppermute | solution.py:734
  77.9 10.4 %collective-permute-start.4 = (bf16[256,640]{1,0:T(8,128)(2,1)S(1)}, bf16[256,640]{1,0:T(8,128)(2,1)S(1)}, u32[]{:S(2)}, u32[]{:S(2)}) collective-permute-start(bf16[256,640]{1,0:T(8,128)(2,1)S(1)} %add_convert_fusion.1), channel_id=1, source_target_pairs={{0,2},{2,0},{1,3},{3,1},{4,6},{6,4},{5,7},{7,5},{8,10},{10,8},{9,1... | collective-permute-start | bytes 983048 | tf_op jit(solution)/shard_map/ppermute | solution.py:732

commit v10 on v8

--- a/solution.py
+++ b/solution.py
@@ -403,7 +403,7 @@
     )(off_chip(x), off_chip(zw))
 
 
-def within_kernel(x_ref, bc_ref, cum_ref, cumt_ref, delta_ref, y_ref, gram_ref):
+def within_kernel(x_ref, bc_ref, cum_ref, cumt_ref, delta_ref, y_ref, gram_ref, size_ref):
     d, n = pl.program_id(0), pl.program_id(1)
     rows = x_ref.shape[0]
     heads = TILE // HEAD_DIM
@@ -416,8 +416,9 @@
         t, s = time_of(iota((rows, rows), 0), rows), time_of(iota((rows, rows), 1), rows)
         seen = jnp.where(d == 0, t - s, s - t) >= 0
         gram_ref[...] = jnp.where(seen, gram, 0.0)
-
-    weighted = x_ref[...].astype(f32) * mm(hi_lo(delta_ref[...]), spread(n * heads, TILE))
+        size_ref[...] = hi_lo(delta_ref[...])
+
+    weighted = x_ref[...].astype(f32) * mm(size_ref[...], spread(n * heads, TILE))
     cum = pltpu.roll(cum_ref[...], (LANES - n * heads) % LANES, 1)
     owner = iota((rows, TILE), 1) // HEAD_DIM
     total = jnp.zeros((rows, TILE), f32)
@@ -443,7 +444,7 @@
         ],
         out_specs=pl.BlockSpec((rows, TILE), lambda d, n: (d, n)),
         out_shape=pltpu.HBM((2 * rows, inner), bf16),
-        scratch_shapes=[pltpu.VMEM((rows, rows), f32)],
+        scratch_shapes=[pltpu.VMEM((rows, rows), f32), pltpu.VMEM((rows, 2 * LANES), bf16)],
         compiler_params=pltpu.CompilerParams(
             dimension_semantics=("arbitrary", "arbitrary"), vmem_limit_bytes=12 << 20
         ),
@@ -709,11 +710,12 @@
         x_weight, blocks,
     )
     pay = lax.all_to_all(pay, "ctx", 0, 0, tiled=True)
+    open_z = open_gate(normed, z_weight)
+    pay, open_z = lax.optimization_barrier((pay, open_z))
+    state = scan((place % 4)[None], pay)
+    state, xconv = lax.optimization_barrier((state, xconv))
+    state = lax.all_to_all(state, "ctx", 0, 0, tiled=True)
     y = within(xconv, bc, cum, cumt, delta)
-    pay, y = lax.optimization_barrier((pay, y))
-    state = scan((place % 4)[None], pay)
-    state = lax.all_to_all(state, "ctx", 0, 0, tiled=True)
-    open_z = open_gate(normed, z_weight)
     core, far = head % 2, head // 2
     quarter = lambda f, c: (2 * f + c)[None]
     core_swap = [(0, 1), (1, 0), (2, 3), (3, 2)]

time: 89.4 us -> 88.8 us (level)
    all_to_all x1, waiting for transfers between devices: 4.29 us -> 2.25 us  [per_device(): state = lax.all_to_all(state, 'ctx', 0, 0, tiled=True)]
    all_to_all x1, waiting for transfers between devices: 3.3 us -> 5.21 us  [per_device(): pay = lax.all_to_all(pay, 'ctx', 0, 0, tiled=True)]
where the time goes in v10:
time: 88.8 us; the launch traced here: 88 us
  Pallas kernels  48.1 us (54%)
  starting transfers between devices  25.5 us (29%)
  waiting for transfers between devices  11.4 us (13%)
  local copies, waits for them, and re-layouts  1.94 us (2%)
    all_to_all x1, starting transfers between devices, per_device(): pay = lax.all_to_all(pay, 'ctx', 0, 0, tiled=True)  10.5 us
    pallas_call x1, Pallas kernels, within(): pl.pallas_call(within_kernel, grid=(2, inner // TILE), in_specs=[pl.Block...  9.33 us
    pallas_call x1, Pallas kernels, entry(): pl.pallas_call(entry_kernel, grid=(steps + 1,), in_specs=[vmem, vmem, vme...  9.13 us
    pallas_call x3, Pallas kernels, project(): pl.pallas_call(functools.partial(project_kernel, len(adds)), in_specs=[pl...  8.84 us
    pallas_call x1, Pallas kernels, open_gate(): pl.pallas_call(open_gate_kernel, grid=(inner // TILE,), in_specs=[fixed(h...  7.45 us
    pallas_call x1, Pallas kernels, gate(): pl.pallas_call(gate_kernel, grid_spec=pltpu.PrefetchScalarGridSpec(num_sc...  7.13 us
    all_to_all x1, waiting for transfers between devices, per_device(): pay = lax.all_to_all(pay, 'ctx', 0, 0, tiled=True)  5.21 us
    pallas_call x1, Pallas kernels, norm(): pl.pallas_call(norm_kernel, grid=(1,), in_specs=[fixed(rows, width), fixe...  4.15 us
  transfers between devices with their start and end apart: 7, of which 3 were waited for; matrix products, arithmetic and copies ran while one was open for 1% of the time, Pallas kernels for 30%

profile of v10, /device:TPU:1, one launch (start us, length us, event | category | flops | bytes accessed | tf_op | source)
XLA Modules:
  0.0 88.0 jit_solution(5690592913993932916)
XLA Ops:
  0.0 0.9 %fusion = (bf16[16,2560]{1,0:T(8,128)(2,1)S(1)}, bf16[16,2560]{1,0:T(8,128)(2,1)S(1)}) fusion(bf16[256,2560]{1,0:T(8,128)(2,1)} %h_ref.1), kind=kLoop, calls=%fused_computation.3 | loop fusion | bytes 327680 | tf_op jit(solution)/shard_map/slice | solution.py:703
  0.9 3.9 %collective-permute-start = (bf16[16,2560]{1,0:T(8,128)(2,1)S(1)}, bf16[16,2560]{1,0:T(8,128)(2,1)S(1)}, u32[]{:S(2)}, u32[]{:S(2)}) collective-permute-start(bf16[16,2560]{1,0:T(8,128)(2,1)S(1)} %get-tuple-element.44), channel_id=1, source_target_pairs={{0,4},{4,8},{8,12},{12,16},{16,20},{20,24},{24,28},{28,32},{32,36}... | collective-permute-start | bytes 245768 | tf_op jit(solution)/shard_map/ppermute | solution.py:702
  4.9 1.3 %collective-permute-start.1 = (bf16[16,2560]{1,0:T(8,128)(2,1)S(1)}, bf16[16,2560]{1,0:T(8,128)(2,1)S(1)}, u32[]{:S(2)}, u32[]{:S(2)}) collective-permute-start(bf16[16,2560]{1,0:T(8,128)(2,1)S(1)} %get-tuple-element.43), channel_id=1, source_target_pairs={{4,0},{8,4},{12,8},{16,12},{20,16},{24,20},{28,24},{32,28},{36,32}... | collective-permute-start | bytes 245768 | tf_op jit(solution)/shard_map/ppermute | solution.py:703
  6.2 4.1 %norm.1 = (bf16[512,2560]{1,0:T(8,128)(2,1)S(1)}, f32[512,128]{1,0:T(8,128)S(1)}, f32[512,128]{1,0:T(8,128)S(1)}, f32[2,24,256]{2,1,0:T(8,128)S(1)}, bf16[512,25...) custom-call(bf16[256,2560]{1,0:T(8,128)(2,1)} %h_ref.1, ...), custom_call_target="tpu_custom_call" | custom-call | flops 4294967296 | bytes 5242880 | tf_op jit(solution)/shard_map/norm/pallas_call | solution.py:164
  10.4 0.0 collective-permute-done.1.next_ref
  10.4 9.1 %entry.1 = (bf16[512,1280]{1,0:T(8,128)(2,1)}, bf16[512,256]{1,0:T(8,128)(2,1)}, bf16[32,88,128]{2,1,0:T(8,128)(2,1)}) custom-call(bf16[512,2560]{1,0:T(8,128)(2,1)S(1)} %get-tuple-element.24.x_ref, bf16[16,2560]{1,0:T(8,128)(2,1)S(1)} %collective-permute-done.prev_ref, bf16[16,2560]{1,0:T(8,128)(2,1)S(1)} %collective-permute-done.1.next_ref, ...), custom_call_target="tpu_custom_call" | custom-call | flops 4278190080 | bytes 12582912 | tf_op jit(solution)/shard_map/entry/pallas_call | solution.py:342
  19.5 10.5 %all-to-all-start = ((bf16[32,88,128]{2,1,0:T(8,128)(2,1)}), bf16[32,88,128]{2,1,0:T(8,128)(2,1)S(1)}, u32[]{:S(2)}, u32[]{:S(2)}) async-start(bf16[32,88,128]{2,1,0:T(8,128)(2,1)} %get-tuple-element.29), calls=%async_computation | async-start | bytes 1441792 | tf_op jit(solution)/shard_map/all_to_all | solution.py:712
  30.0 7.5 %open_gate.1.z_ref = bf16[512,1280]{1,0:T(8,128)(2,1)S(1)} custom-call(bf16[512,2560]{1,0:T(8,128)(2,1)} %copy-done, bf16[2560,1280]{1,0:T(8,128)(2,1)} %zw_ref.1), custom_call_target="tpu_custom_call" | custom-call | flops 3355443200 | bytes 16777216 | tf_op jit(solution)/shard_map/open_gate/pallas_call | solution.py:390
  37.5 5.2 %all-to-all-done.pay_ref = bf16[32,88,128]{2,1,0:T(8,128)(2,1)S(1)} async-done(((bf16[32,88,128]{2,1,0:T(8,128)(2,1)}), bf16[32,88,128]{2,1,0:T(8,128)(2,1)S(1)}, u32[]{:S(2)}, u32[]{:S(2)}) %all-to-all-start) | async-done | bytes 720928 | tf_op jit(solution)/shard_map/all_to_all | solution.py:712
  42.7 2.1 %scan.1 = bf16[32,80,128]{2,1,0:T(8,128)(2,1)} custom-call(s32[1]{0:T(128)} %bitcast.3.q_ref, bf16[32,88,128]{2,1,0:T(8,128)(2,1)S(1)} %all-to-all-done.pay_ref), custom_call_target="tpu_custom_call" | custom-call | tf_op jit(solution)/shard_map/scan/pallas_call | solution.py:490
  44.8 3.9 %all-to-all-start.1 = ((bf16[32,80,128]{2,1,0:T(8,128)(2,1)}), bf16[32,80,128]{2,1,0:T(8,128)(2,1)S(1)}, u32[]{:S(2)}, u32[]{:S(2)}) async-start(bf16[32,80,128]{2,1,0:T(8,128)(2,1)} %scan.1), calls=%async_computation.1 | async-start | bytes 1310720 | tf_op jit(solution)/shard_map/all_to_all | solution.py:717
  48.8 9.3 %within.1.y_ref = bf16[512,1280]{1,0:T(8,128)(2,1)} custom-call(bf16[512,1280]{1,0:T(8,128)(2,1)} %get-tuple-element.32.x_ref, bf16[512,256]{1,0:T(8,128)(2,1)} %get-tuple-element.33.bc_ref, f32[512,128]{1,0:T(8,128)S(1)} %get-tuple-element.34.cum_ref, f32[2,24,256]{2,1,0:T(8,128)S(1)} %get-tuple-element.35.cumt_ref, f32[512,128]{1,0:T(8,128)S(1)} %get-tuple-element.36.delta_ref), custom_call_target="tpu_custom_call" | custom-call | flops 3221225472 | bytes 5242880 | tf_op jit(solution)/shard_map/within/pallas_call | solution.py:435
  58.1 2.2 %all-to-all-done.1 = bf16[32,80,128]{2,1,0:T(8,128)(2,1)S(1)} async-done(((bf16[32,80,128]{2,1,0:T(8,128)(2,1)}), bf16[32,80,128]{2,1,0:T(8,128)(2,1)S(1)}, u32[]{:S(2)}, u32[]{:S(2)}) %all-to-all-start.1) | async-done | bytes 655392 | tf_op jit(solution)/shard_map/all_to_all | solution.py:717
  60.3 7.1 %gate.1 = (bf16[256,2560]{1,0:T(8,128)(2,1)S(1)}, bf16[256,640]{1,0:T(8,128)(2,1)}) custom-call(s32[1]{0:T(128)} %bitcast.2.target_ref, bf16[512,1280]{1,0:T(8,128)(2,1)} %within.1.y_ref, bf16[512,1280]{1,0:T(8,128)(2,1)S(1)} %open_gate.1.z_ref, bf16[512,256]{1,0:T(8,128)(2,1)} %get-tuple-element.33.bc_ref, f32[512,128]{1,0:T(8,128)S(1)} %get-tuple-element.34.cum_ref, ...), custom_call_target="tpu_custom_call" | custom-call | tf_op jit(solution)/shard_map/gate/pallas_call | solution.py:633
  67.5 3.3 %collective-permute-start.2 = (bf16[256,640]{1,0:T(8,128)(2,1)}, bf16[256,640]{1,0:T(8,128)(2,1)S(1)}, u32[]{:S(2)}, u32[]{:S(2)}) collective-permute-start(bf16[256,640]{1,0:T(8,128)(2,1)} %get-tuple-element.40), channel_id=1, source_target_pairs={{0,1},{1,0},{2,3},{3,2},{4,5},{5,4},{6,7},{7,6},{8,9},{9,8},{10,11... | collective-permute-start | bytes 983048 | tf_op jit(solution)/shard_map/ppermute | solution.py:726
  70.7 2.9 %project.3 = f32[256,640]{1,0:T(8,128)S(1)} custom-call(s32[1]{0:T(128)} %bitcast.1.q_ref, bf16[256,2560]{1,0:T(8,128)(2,1)S(1)} %get-tuple-element.41.g_ref, bf16[1280,2560]{1,0:T(8,128)(2,1)} %w_ref.7), custom_call_target="tpu_custom_call" | custom-call | flops 838860800 | bytes 5242880 | tf_op jit(solution)/shard_map/project/pallas_call | solution.py:680
  73.7 0.1 add_convert_fusion.1
  73.8 2.9 %project.4 = bf16[256,640]{1,0:T(8,128)(2,1)S(1)} custom-call(s32[1]{0:T(128)} %bitcast.10.q_ref, bf16[256,2560]{1,0:T(8,128)(2,1)S(1)} %get-tuple-element.41.g_ref, bf16[1280,2560]{1,0:T(8,128)(2,1)} %w_ref.7), custom_call_target="tpu_custom_call" | custom-call | flops 838860800 | bytes 5242880 | tf_op jit(solution)/shard_map/project/pallas_call | solution.py:680
  76.7 0.1 collective-permute-start.3
  76.8 2.5 %collective-permute-start.4 = (bf16[256,640]{1,0:T(8,128)(2,1)S(1)}, bf16[256,640]{1,0:T(8,128)(2,1)S(1)}, u32[]{:S(2)}, u32[]{:S(2)}) collective-permute-start(bf16[256,640]{1,0:T(8,128)(2,1)S(1)} %add_convert_fusion.1), channel_id=1, source_target_pairs={{0,2},{2,0},{1,3},{3,1},{4,6},{6,4},{5,7},{7,5},{8,10},{10,8},{9,1... | collective-permute-start | bytes 983048 | tf_op jit(solution)/shard_map/ppermute | solution.py:730
  79.3 1.0 %constant_dynamic-slice_fusion.rest_1_ = bf16[256,640]{1,0:T(8,128)(2,1)S(1)} fusion(bf16[256,2560]{1,0:T(8,128)(2,1)} %h_ref.1, s32[]{:T(128)S(6)} %select_n.21), kind=kLoop, calls=%fused_computation.2 | loop fusion | bytes 655364 | tf_op jit(solution)/shard_map/dynamic_slice | solution.py:734
  80.3 3.0 %project.5 = f32[256,640]{1,0:T(8,128)S(1)} custom-call(s32[1]{0:T(128)} %bitcast.q_ref, bf16[256,2560]{1,0:T(8,128)(2,1)S(1)} %get-tuple-element.41.g_ref, bf16[1280,2560]{1,0:T(8,128)(2,1)} %w_ref.7, bf16[256,640]{1,0:T(8,128)(2,1)S(1)} %collective-permute-done.3.rest_0_, bf16[256,640]{1,0:T(8,128)(2,1)S(1)} %constant_dynamic-slice_fusion.rest_1_), custom_call_target="tpu_custom_call" | custom-call | flops 838860800 | bytes 5242880 | tf_op jit(solution)/shard_map/project/pallas_call | solution.py:680
  83.3 4.0 %collective-permute-done.4 = bf16[256,640]{1,0:T(8,128)(2,1)S(1)} collective-permute-done((bf16[256,640]{1,0:T(8,128)(2,1)S(1)}, bf16[256,640]{1,0:T(8,128)(2,1)S(1)}, u32[]{:S(2)}, u32[]{:S(2)}) %collective-permute-start.4) | collective-permute-done | bytes 327712 | tf_op jit(solution)/shard_map/ppermute | solution.py:730
  87.2 0.8 add_convert_fusion
  (5 shorter events, 0.0 us)
Async XLA Ops:
  0.9 9.4 %collective-permute-start = (bf16[16,2560]{1,0:T(8,128)(2,1)S(1)}, bf16[16,2560]{1,0:T(8,128)(2,1)S(1)}, u32[]{:S(2)}, u32[]{:S(2)}) collective-permute-start(bf16[16,2560]{1,0:T(8,128)(2,1)S(1)} %get-tuple-element.44), channel_id=1, source_target_pairs={{0,4},{4,8},{8,12},{12,16},{16,20},{20,24},{24,28},{28,32},{32,36}... | collective-permute-start | bytes 245768 | tf_op jit(solution)/shard_map/ppermute | solution.py:702
  4.9 5.5 %collective-permute-start.1 = (bf16[16,2560]{1,0:T(8,128)(2,1)S(1)}, bf16[16,2560]{1,0:T(8,128)(2,1)S(1)}, u32[]{:S(2)}, u32[]{:S(2)}) collective-permute-start(bf16[16,2560]{1,0:T(8,128)(2,1)S(1)} %get-tuple-element.43), channel_id=1, source_target_pairs={{4,0},{8,4},{12,8},{16,12},{20,16},{24,20},{28,24},{32,28},{36,32}... | collective-permute-start | bytes 245768 | tf_op jit(solution)/shard_map/ppermute | solution.py:703
  10.3 9.2 %copy-start = (bf16[512,2560]{1,0:T(8,128)(2,1)}, bf16[512,2560]{1,0:T(8,128)(2,1)S(1)}, u32[]{:S(2)}) copy-start(bf16[512,2560]{1,0:T(8,128)(2,1)S(1)} %get-tuple-element.24.x_ref) | copy-start | bytes 7864324
  19.5 23.2 %all-to-all-start = ((bf16[32,88,128]{2,1,0:T(8,128)(2,1)}), bf16[32,88,128]{2,1,0:T(8,128)(2,1)S(1)}, u32[]{:S(2)}, u32[]{:S(2)}) async-start(bf16[32,88,128]{2,1,0:T(8,128)(2,1)} %get-tuple-element.29), calls=%async_computation | async-start | bytes 1441792 | tf_op jit(solution)/shard_map/all_to_all | solution.py:712
  44.8 15.5 %all-to-all-start.1 = ((bf16[32,80,128]{2,1,0:T(8,128)(2,1)}), bf16[32,80,128]{2,1,0:T(8,128)(2,1)S(1)}, u32[]{:S(2)}, u32[]{:S(2)}) async-start(bf16[32,80,128]{2,1,0:T(8,128)(2,1)} %scan.1), calls=%async_computation.1 | async-start | bytes 1310720 | tf_op jit(solution)/shard_map/all_to_all | solution.py:717
  67.5 6.2 %collective-permute-start.2 = (bf16[256,640]{1,0:T(8,128)(2,1)}, bf16[256,640]{1,0:T(8,128)(2,1)S(1)}, u32[]{:S(2)}, u32[]{:S(2)}) collective-permute-start(bf16[256,640]{1,0:T(8,128)(2,1)} %get-tuple-element.40), channel_id=1, source_target_pairs={{0,1},{1,0},{2,3},{3,2},{4,5},{5,4},{6,7},{7,6},{8,9},{9,8},{10,11... | collective-permute-start | bytes 983048 | tf_op jit(solution)/shard_map/ppermute | solution.py:726
  76.7 3.6 %collective-permute-start.3 = (bf16[256,640]{1,0:T(8,128)(2,1)S(1)}, bf16[256,640]{1,0:T(8,128)(2,1)S(1)}, u32[]{:S(2)}, u32[]{:S(2)}) collective-permute-start(bf16[256,640]{1,0:T(8,128)(2,1)S(1)} %project.4), channel_id=1, source_target_pairs={{0,1},{1,0},{2,3},{3,2},{4,5},{5,4},{6,7},{7,6},{8,9},{9,8},{10,11... | collective-permute-start | bytes 983048 | tf_op jit(solution)/shard_map/ppermute | solution.py:732
  76.8 10.4 %collective-permute-start.4 = (bf16[256,640]{1,0:T(8,128)(2,1)S(1)}, bf16[256,640]{1,0:T(8,128)(2,1)S(1)}, u32[]{:S(2)}, u32[]{:S(2)}) collective-permute-start(bf16[256,640]{1,0:T(8,128)(2,1)S(1)} %add_convert_fusion.1), channel_id=1, source_target_pairs={{0,2},{2,0},{1,3},{3,1},{4,6},{6,4},{5,7},{7,5},{8,10},{10,8},{9,1... | collective-permute-start | bytes 983048 | tf_op jit(solution)/shard_map/ppermute | solution.py:730
